TPU v7x, 128 devices: a whole 4x4x4 slice. The times are simulated.
128 devices in a mesh: req: 16 (over y, z), head: 8 (over x, core).
Axes of the slice: x: 4, y: 4, z: 4, core: 2. Of those that a mesh axis runs over, the one named last changes fastest.
Arguments:
- hidden: bfloat16 [2048, 6144], P('req'), may hold values from -15 to 15
- attn_norm_gain: float32 [6144], replicated, may hold values from 0.3 to 3
- attn_norm_bias: float32 [6144], replicated, may hold values from -4 to 4
- mlp_norm_gain: float32 [6144], replicated, may hold values from 0.3 to 3
- mlp_norm_bias: float32 [6144], replicated, may hold values from -4 to 4
- qkv_weight: bfloat16 [6144, 9216], P('req', 'head'), may hold values from -0.078125 to 0.078125
- qkv_bias: float32 [9216], P('head'), may hold values from -3 to 3
- out_weight: bfloat16 [3072, 6144], P('head', 'req'), may hold values from -0.625 to 0.625
- out_bias: float32 [6144], replicated, may hold values from -3 to 3
- up_weight: bfloat16 [6144, 12288], P('req', 'head'), may hold values from -0.078125 to 0.078125
- up_bias: float32 [12288], P('head'), may hold values from -3 to 3
- down_weight: bfloat16 [12288, 6144], P('head', 'req'), may hold values from -0.0546875 to 0.0546875
- down_bias: float32 [6144], replicated, may hold values from -3 to 3
- cache_keys: bfloat16 [16, 4096, 3072], P('req', None, 'head'), may hold values from -1300 to 1300
- cache_values: bfloat16 [16, 4096, 3072], P('req', None, 'head'), may hold values from -6 to 6
- cached_len: int32 [16], P('req'), may hold values from 128 to 4096, as said below
Outputs:
- hidden_out: bfloat16 [2048, 6144], P('req')
- new_keys: bfloat16 [16, 128, 3072], P('req', None, 'head')
- new_values: bfloat16 [16, 128, 3072], P('req', None, 'head')
Inputs may be any that keep to these rules, and one draw needn't show every extreme that they name: `cached_len`: each entry is 128 or 4096, and both values occur.
All inputs are finite; a program needn't handle non-finite values.
Results may differ from a plain program's by a relative error of at most 0.0085.
The roundings to bfloat16 on the way count: a program that leaves them out, or rounds other values in their place, can miss the bound.
Values may be sent and summed in bfloat16 or wider, within the bound.
A program may use at most 128 MiB of HBM per device.

v0:
```python
import math

import jax
import jax.numpy as jnp
from jax import lax
from jax.sharding import PartitionSpec as P

DH = 96
ROT = 24
NEW = 128
CACHE = 4096
KBLOCK = 512


def normalize(values, norm_gain, norm_shift):
    widened = values.astype(jnp.float32)
    center = jnp.mean(widened, axis=-1, keepdims=True)
    spread = jnp.mean(jnp.square(widened - center), axis=-1, keepdims=True)
    return ((widened - center) * lax.rsqrt(spread + 1e-05) * norm_gain + norm_shift).astype(
        jnp.bfloat16
    )


def rotate(values, position):
    halfway = ROT // 2
    exponent = jnp.arange(halfway, dtype=jnp.float32) * (2.0 / ROT)
    frequency = jnp.power(10000.0, -exponent)
    angle = position[:, None] * frequency[None, :]
    cosine = jnp.cos(angle)[:, None, :]
    sine_part = jnp.sin(angle)[:, None, :]
    lower_half = values[..., :halfway]
    upper_half = values[..., halfway:ROT]
    return jnp.concatenate(
        [
            lower_half * cosine - upper_half * sine_part,
            upper_half * cosine + lower_half * sine_part,
            values[..., ROT:],
        ],
        axis=-1,
    )


def attend_request(qkv_rows, keys_old, values_old, length, local_heads):
    scale_factor = 1.0 / math.sqrt(DH)
    split_rows = qkv_rows.reshape(NEW, local_heads, 3, DH)
    position = length.astype(jnp.float32) + jnp.arange(NEW, dtype=jnp.float32)
    queries = rotate(split_rows[:, :, 0], position).astype(jnp.bfloat16)
    key_new = rotate(split_rows[:, :, 1], position).astype(jnp.bfloat16)
    value_new = split_rows[:, :, 2].astype(jnp.bfloat16)
    query_index = jnp.arange(NEW, dtype=jnp.int32)
    fresh_scores = (
        jnp.einsum("qhd,khd->hqk", queries, key_new, preferred_element_type=jnp.float32)
        * scale_factor
    )
    fresh_scores = jnp.where(
        (query_index[None, :] <= query_index[:, None])[None], fresh_scores, -1e30
    )
    block_total = (length + KBLOCK - 1) // KBLOCK
    key_offsets = jnp.arange(KBLOCK, dtype=jnp.int32)

    def score_block(block_index, carry):
        score_store, highest = carry
        first_key = block_index * KBLOCK
        key_block = lax.dynamic_slice_in_dim(keys_old, first_key, KBLOCK, 0)
        block_scores = (
            jnp.einsum("qhd,khd->hqk", queries, key_block, preferred_element_type=jnp.float32)
            * scale_factor
        )
        block_scores = jnp.where(
            (first_key + key_offsets < length)[None, None, :], block_scores, -1e30
        )
        score_store = lax.dynamic_update_slice_in_dim(score_store, block_scores, first_key, 2)
        return (score_store, jnp.maximum(highest, jnp.max(block_scores, axis=-1)))

    empty_store = jnp.zeros((local_heads, NEW, CACHE), jnp.float32)
    score_store, highest = lax.fori_loop(
        0, block_total, score_block, (empty_store, jnp.max(fresh_scores, axis=-1))
    )
    fresh_weights = jnp.exp(fresh_scores - highest[..., None])

    def weigh_block(block_index, carry):
        mixed, denominator = carry
        first_key = block_index * KBLOCK
        block_scores = lax.dynamic_slice_in_dim(score_store, first_key, KBLOCK, 2)
        block_weights = jnp.exp(block_scores - highest[..., None])
        value_block = lax.dynamic_slice_in_dim(values_old, first_key, KBLOCK, 0)
        mixed = mixed + jnp.einsum(
            "hqk,khd->qhd",
            block_weights.astype(jnp.bfloat16),
            value_block,
            preferred_element_type=jnp.float32,
        )
        return (mixed, denominator + jnp.sum(block_weights, axis=-1))

    initial = (
        jnp.einsum(
            "hqk,khd->qhd",
            fresh_weights.astype(jnp.bfloat16),
            value_new,
            preferred_element_type=jnp.float32,
        ),
        jnp.sum(fresh_weights, axis=-1),
    )
    mixed, denominator = lax.fori_loop(0, block_total, weigh_block, initial)
    attended = (mixed / jnp.transpose(denominator)[:, :, None]).astype(jnp.bfloat16)
    width = local_heads * DH
    return (
        attended.reshape(NEW, width),
        key_new.reshape(NEW, width),
        value_new.reshape(NEW, width),
    )


def body(
    hidden,
    attn_norm_gain,
    attn_norm_bias,
    mlp_norm_gain,
    mlp_norm_bias,
    qkv_weight,
    qkv_bias,
    out_weight,
    out_bias,
    up_weight,
    up_bias,
    down_weight,
    down_bias,
    cache_keys,
    cache_values,
    cached_len,
):
    qkv_cols = qkv_weight.shape[1]
    local_heads = qkv_cols // (3 * DH)
    attn_normed = normalize(hidden, attn_norm_gain, attn_norm_bias)
    mlp_normed = normalize(hidden, mlp_norm_gain, mlp_norm_bias)
    attn_blocks, mlp_blocks = (
        lax.all_to_all(attn_normed, "req", split_axis=1, concat_axis=0, tiled=True),
        lax.all_to_all(mlp_normed, "req", split_axis=1, concat_axis=0, tiled=True),
    )
    qkv_term = jnp.dot(attn_blocks, qkv_weight, preferred_element_type=jnp.float32)
    up_term = jnp.dot(mlp_blocks, up_weight, preferred_element_type=jnp.float32)
    summed = lax.psum_scatter(
        jnp.concatenate([qkv_term, up_term], axis=1), "req", scatter_dimension=0, tiled=True
    )
    qkv_sum = summed[:, :qkv_cols]
    up_sum = summed[:, qkv_cols:]
    qkv = qkv_sum + qkv_bias
    units = jax.nn.gelu(up_sum + up_bias, approximate=True).astype(jnp.bfloat16)
    keys_old = cache_keys[0].reshape(CACHE, local_heads, DH)
    values_old = cache_values[0].reshape(CACHE, local_heads, DH)
    attended_rows, key_rows, value_rows = attend_request(
        qkv, keys_old, values_old, cached_len[0], local_heads
    )
    key_list = [key_rows]
    value_list = [value_rows]
    new_keys = jnp.stack(key_list, axis=0)
    new_values = jnp.stack(value_list, axis=0)
    joined = jnp.concatenate([attended_rows, units], axis=1)
    head_width = attended_rows.shape[1]
    shard_rows = lax.all_gather(joined, "req", axis=0, tiled=True)
    attention_part = jnp.dot(
        shard_rows[:, :head_width], out_weight, preferred_element_type=jnp.float32
    )
    partial_out = attention_part + jnp.dot(
        shard_rows[:, head_width:], down_weight, preferred_element_type=jnp.float32
    )
    bias_total = out_bias + down_bias
    spread_out = lax.all_to_all(partial_out, "req", split_axis=0, concat_axis=1, tiled=True)
    summed_out = lax.psum(spread_out, "head")
    result = (hidden.astype(jnp.float32) + summed_out + bias_total).astype(jnp.bfloat16)
    return (result, new_keys, new_values)


def solution(mesh):
    return jax.shard_map(
        body,
        mesh=mesh,
        in_specs=(
            P("req", None),
            P(),
            P(),
            P(),
            P(),
            P("req", "head"),
            P("head"),
            P("head", "req"),
            P(),
            P("req", "head"),
            P("head"),
            P("head", "req"),
            P(),
            P("req", None, "head"),
            P("req", None, "head"),
            P("req"),
        ),
        out_specs=(P("req", None), P("req", None, "head"), P("req", None, "head")),
        check_vma=False,
    )
```

profile of v0, /device:TPU:1, one launch (start us, length us, event | category | flops | bytes accessed | tf_op | source)
XLA Modules:
  0.0 497.1 jit_solution(11655447223252928488)
XLA Ops:
  10.9 5.4 %fusion.21 = (bf16[128,6144]{0,1:T(8,128)(2,1)}, bf16[128,6144]{0,1:T(8,128)(2,1)S(1)}) fusion(bf16[128,6144]{0,1:T(8,128)(2,1)S(1)} %copy.39, f32[6144]{0:T(1024)S(1)} %copy-done.7, f32[6144]{0:T(1024)S(1)} %copy-done.8, f32[128]{0:T(128)S(1)} %add_rsqrt_fusion, f32[128]{0:T(128)S(1)} %broadcast_multiply_fusion, f32[6144]{0:T(1024)S(1)} %copy-done.9, ...), kind=kLoop, calls=%fused_computation.29 | loop fusion | flops 7077888 | bytes 4817920 | tf_op jit(solution)/shard_map/convert_element_type | solution.py:19
  16.4 30.0 %all_to_all.57 = bf16[128,16,384]{0,2,1:T(8,128)(2,1)} all-to-all(bf16[128,16,384]{0,2,1:T(8,128)(2,1)S(1)} %bitcast.67), channel_id=1, replica_groups=mesh['req'=16,'head'=8] {'req'}, dimensions={1} | all-to-all | bytes 3145728 | tf_op jit(solution)/shard_map/all_to_all | solution.py:138
  46.4 3.7 all-to-all-start
  50.2 2.6 copy.41
  52.8 17.9 %all-to-all-done = bf16[128,16,384]{0,2,1:T(8,128)(2,1)S(1)} async-done(((bf16[128,16,384]{0,2,1:T(8,128)(2,1)}), bf16[128,16,384]{0,2,1:T(8,128)(2,1)S(1)}, u32[]{:S(2)}, u32[]{:S(2)}) %all-to-all-start) | async-done | bytes 1572896 | tf_op jit(solution)/shard_map/all_to_all | solution.py:137
  73.7 5.1 %fusion.47 = f32[2048,1536]{0,1:T(8,128)S(1)} fusion(bf16[2048,384]{1,0:T(8,128)(2,1)} %bitcast.63, bf16[384,1536]{1,0:T(8,128)(2,1)S(1)} %copy-done), kind=kOutput, calls=%fused_computation.79 | convolution fusion | flops 2415919104 | bytes 15335424 | tf_op jit(solution)/shard_map/dot_general | solution.py:141
  78.8 2.8 fusion.46
  81.6 11.1 %pad_maximum_fusion = f32[2048,2688]{0,1:T(8,128)} fusion(f32[2048,1536]{0,1:T(8,128)S(1)} %fusion.47, f32[2048,1152]{0,1:T(8,128)S(1)} %fusion.46), kind=kLoop, calls=%fused_computation.18 | loop fusion | flops 5505024 | bytes 44040192 | tf_op jit(solution)/shard_map/concatenate | solution.py:143
  93.6 4.8 copy.45
  98.4 4.9 copy.47
  103.4 127.5 %reduce-scatter.2.cloned.1.call-done = f32[128,2688]{0,1:T(8,128)} async-done(((f32[2048,2688]{0,1:T(8,128)}), f32[128,2688]{0,1:T(8,128)}) %reduce-scatter.2.cloned.1.call-update) | async-done | bytes 1376272 | tf_op jit(solution)/shard_map/reduce_scatter | solution.py:142
  232.6 3.8 broadcast_in_dim.20
  236.3 24.3 %while.26 = (s32[]{:T(128)}, f32[4,128,4096]{1,2,0:T(8,128)}, f32[4,128]{1,0:T(4,128)S(1)}, s32[]{:T(128)}, s32[]{:T(128)}, /*index=5*/bf16[4096,4,96]{0,2,1:T(8...) while((s32[]{:T(128)}, f32[4,128,4096]{1,2,0:T(8,128)}, ...), condition=%wide.region_6.7_spmd.clone, body=%wide.region_4.6_spmd.clone.sunk | while | flops 51119108 | bytes 1550499 | solution.py:76
  255.2 2.4 fusion.70
  258.3 2.4 fusion.70
  260.9 27.4 %while.25 = (s32[]{:T(128)}, f32[128,4,96]{0,2,1:T(8,128)S(1)}, f32[4,128]{1,0:T(4,128)S(1)}, s32[]{:T(128)}, bf16[4096,4,96]{0,2,1:T(8,128)(2,1)}, /*index=5*/f...) while((s32[]{:T(128)}, f32[128,4,96]{0,2,1:T(8,128)S(1)}, ...), condition=%wide.region_10.11_spmd, body=%wide.region_8.10_spmd.sunk | while | flops 51429380 | bytes 7090339 | solution.py:104
  290.7 71.9 %all-gather.2.cloned.1.call-done = bf16[2048,1920]{0,1:T(8,128)(2,1)} async-done(((bf16[128,1920]{0,1:T(8,128)(2,1)}), bf16[2048,1920]{0,1:T(8,128)(2,1)}) %all-gather.2.cloned.1.call-update) | async-done | bytes 7864336 | tf_op jit(solution)/shard_map/all_gather | solution.py:160
  362.6 5.9 %fusion.14 = f32[2048,384]{1,0:T(8,128)S(1)} fusion(bf16[1536,384]{1,0:T(8,128)(2,1)} %param.31, bf16[2048,1920]{0,1:T(8,128)(2,1)} %all-gather.2.cloned.1.call-done), kind=kOutput, calls=%fused_computation.19 | convolution fusion | flops 2415919104 | bytes 10616832 | tf_op jit(solution)/shard_map/dot_general | solution.py:164
  368.5 2.6 convolution_add_fusion
  371.2 41.2 %all_to_all.58 = f32[16,128,384]{2,1,0:T(8,128)} all-to-all(f32[16,128,384]{2,1,0:T(8,128)S(1)} %bitcast.60), channel_id=1, replica_groups=mesh['req'=16,'head'=8] {'req'}, dimensions={0} | all-to-all | bytes 6291456 | tf_op jit(solution)/shard_map/all_to_all | solution.py:168
  412.4 3.6 copy.49
  418.2 66.5 %all-reduce.2.cloned.1.call-done = f32[128,6144]{0,1:T(8,128)} async-done(((f32[128,6144]{0,1:T(8,128)}), f32[128,6144]{0,1:T(8,128)}) %all-reduce.2.cloned.1.call-update) | async-done | bytes 3145744 | tf_op jit(solution)/shard_map/psum | solution.py:169
  484.7 3.3 fusion.26
  488.0 2.6 copy.50
  (125 shorter events, 60.2 us)
Async XLA Ops:
  7.2 66.5 %copy-start = (bf16[384,1536]{1,0:T(8,128)(2,1)S(1)}, bf16[384,1536]{1,0:T(8,128)(2,1)}, u32[]{:S(2)}) copy-start(bf16[384,1536]{1,0:T(8,128)(2,1)} %param.29) | copy-start | bytes 3538948
  7.2 3.7 copy-start.8
  7.2 3.7 copy-start.7
  7.2 3.7 copy-start.10
  7.2 3.7 copy-start.9
  9.2 7.2 %copy-start.2 = (bf16[128,6144]{0,1:T(8,128)(2,1)}, bf16[128,6144]{0,1:T(8,128)(2,1)S(1)}, u32[]{:S(2)}) copy-start(bf16[128,6144]{0,1:T(8,128)(2,1)S(1)} %copy.39) | copy-start | bytes 4718596
  46.4 24.3 %all-to-all-start = ((bf16[128,16,384]{0,2,1:T(8,128)(2,1)}), bf16[128,16,384]{0,2,1:T(8,128)(2,1)S(1)}, u32[]{:S(2)}, u32[]{:S(2)}) async-start(bf16[128,16,384]{0,2,1:T(8,128)(2,1)} %bitcast.66), calls=%async_computation | async-start | bytes 3145728 | tf_op jit(solution)/shard_map/all_to_all | solution.py:137
  50.1 180.7 %reduce-scatter.2.cloned.1.call-start = ((), (), s32[]{:S(2)}) async-start(), calls=%async_computation.4 | async-start | bytes 23396352 | tf_op jit(solution)/shard_map/reduce_scatter | solution.py:142
  70.7 1.1 copy-start.4
  73.7 5.1 %copy-start.5 = (bf16[384,1152]{1,0:T(8,128)(2,1)S(1)}, bf16[384,1152]{1,0:T(8,128)(2,1)}, u32[]{:S(2)}) copy-start(bf16[384,1152]{1,0:T(8,128)(2,1)} %param.25) | copy-start | bytes 2654212
  92.7 269.9 %all-gather.2.cloned.1.call-start = ((), (), s32[]{:S(2)}) async-start(), calls=%async_computation.5 | async-start | bytes 8355840 | tf_op jit(solution)/shard_map/all_gather | solution.py:160
  98.4 132.5 %copy-start.13 = (f32[1152]{0:T(1024)S(1)}, f32[1152]{0:T(1024)}, u32[]{:S(2)}) copy-start(f32[1152]{0:T(1024)} %param.26) | copy-start | bytes 13828
  260.9 27.4 %copy-start.14 = (f32[1536]{0:T(1024)S(1)}, f32[1536]{0:T(1024)}, u32[]{:S(2)}) copy-start(f32[1536]{0:T(1024)} %param.30) | copy-start | bytes 18436
  290.7 77.8 %copy-start.6 = (bf16[384,384]{1,0:T(8,128)(2,1)S(1)}, bf16[384,384]{1,0:T(8,128)(2,1)}, u32[]{:S(2)}) copy-start(bf16[384,384]{1,0:T(8,128)(2,1)} %param.27) | copy-start | bytes 884740
  290.7 194.0 %all-reduce.2.cloned.1.call-start = ((), (), s32[]{:S(2)}) async-start(), calls=%async_computation.6 | async-start | bytes 6291456 | tf_op jit(solution)/shard_map/psum | solution.py:169
  415.9 0.7 copy-start.11
  415.9 0.8 copy-start.12
  415.9 68.7 %copy-start.3 = (bf16[128,6144]{0,1:T(8,128)(2,1)S(1)}, bf16[128,6144]{0,1:T(8,128)(2,1)}, u32[]{:S(2)}) copy-start(bf16[128,6144]{0,1:T(8,128)(2,1)} %copy-done.2) | copy-start | bytes 4718596
  484.7 5.9 %copy-start.1 = (bf16[384,1536]{1,0:T(8,128)(2,1)S(1)}, bf16[384,1536]{1,0:T(8,128)(2,1)}, u32[]{:S(2)}) copy-start(bf16[384,1536]{1,0:T(8,128)(2,1)} %param.29) | copy-start | bytes 3538948
Sparse Core Ops, SparseCore 0:
  92.8 138.0 reduce-scatter.1
  290.8 71.7 all-gather.1
  416.1 68.5 all-reduce.1
where the time goes:
time: 500 us; the launch traced here: 497 us
  waiting for transfers between devices  284 us (57%)
  blocking collectives  71.2 us (14%)
  matrix products  46.9 us (9%)
  local copies, waits for them, and re-layouts  42.6 us (9%)
  other arithmetic  33.5 us (7%)
  between operations  14.7 us (3%)
    reduce_scatter x1, waiting for transfers between devices, body(): lax.psum_scatter(jnp.concatenate([qkv_term, up_term], axis=1), 'req', sca...  127 us
    all_gather x1, waiting for transfers between devices, body(): shard_rows = lax.all_gather(joined, 'req', axis=0, tiled=True)  71.9 us
    psum x1, waiting for transfers between devices, body(): summed_out = lax.psum(spread_out, 'head')  66.5 us
    all_to_all x1, blocking collectives, body(): lax.all_to_all(partial_out, 'req', split_axis=0, concat_axis=1, tiled=True)  41.2 us
    all_to_all x1, blocking collectives, body(): lax.all_to_all(mlp_normed, 'req', split_axis=1, concat_axis=0, tiled=True)  30 us
    dot_general x8, matrix products, score_block(): jnp.einsum('qhd,khd->hqk', queries, key_block, preferred_element_type=jnp...  19 us
    all_to_all x1, waiting for transfers between devices, body(): lax.all_to_all(attn_normed, 'req', split_axis=1, concat_axis=0, tiled=True)  17.9 us
    unnamed x36, local copies, waits for them, and re-layouts  17.6 us
  transfers between devices with their start and end apart: 4, of which 4 were waited for; matrix products, arithmetic and copies ran while one was open for 3% of the time, Pallas kernels for 0%

commit v1 on v0

v1 whole, which is shorter than its diff:
```python
import functools
import math

import jax
import jax.numpy as jnp
from jax import lax
from jax.experimental import pallas as pl
from jax.experimental.pallas import tpu as pltpu
from jax.sharding import PartitionSpec as P

DH = 96
ROT = 24
NEW = 128
CACHE = 4096
KB = 512
NT = (((1,), (1,)), ((), ()))


def normalize(values, norm_gain, norm_shift):
    widened = values.astype(jnp.float32)
    center = jnp.mean(widened, axis=-1, keepdims=True)
    spread = jnp.mean(jnp.square(widened - center), axis=-1, keepdims=True)
    return ((widened - center) * lax.rsqrt(spread + 1e-05) * norm_gain + norm_shift).astype(
        jnp.bfloat16
    )


def rotation_tables(length):
    position = length.astype(jnp.float32) + jnp.arange(NEW, dtype=jnp.float32)
    halfway = ROT // 2
    exponent = jnp.arange(halfway, dtype=jnp.float32) * (2.0 / ROT)
    frequency = jnp.power(10000.0, -exponent)
    angle = position[None, :] * frequency[:, None]
    cosine, sine = jnp.cos(angle), jnp.sin(angle)
    return jnp.concatenate([cosine, cosine], 0), jnp.concatenate([-sine, sine], 0)


def attention_kernel(
    heads, len_ref, qkv_ref, bias_ref, cos_ref, sin_ref, k_hbm, v_hbm,
    att_ref, nk_ref, nv_ref, kbuf, vbuf, sbuf, qexp, ksem, vsem,
):
    scale = 1.0 / math.sqrt(DH)
    length = len_ref[0]
    width = heads * DH
    blocks = CACHE // KB
    used = (length + KB - 1) // KB

    def fetch(i, hbm, buf, sem):
        rows = pl.ds(pl.multiple_of(i * KB, KB), KB)
        return pltpu.make_async_copy(hbm.at[rows], buf.at[rows], sem.at[i])

    for hbm, buf, sem in ((k_hbm, kbuf, ksem), (v_hbm, vbuf, vsem)):
        @pl.loop(0, used)
        def _(i):
            fetch(i, hbm, buf, sem).start()

    cosine, sine = cos_ref[...], sin_ref[...]

    def turned(rows):
        low = rows[:ROT]
        swapped = jnp.concatenate([low[ROT // 2:], low[: ROT // 2]], axis=0)
        return jnp.concatenate([low * cosine + swapped * sine, rows[ROT:]], axis=0)

    def block(j, part):
        at = pl.ds((3 * j + part) * DH, DH)
        return qkv_ref[at, :] + bias_ref[at, :]

    queries = jnp.concatenate([turned(block(j, 0)) for j in range(heads)], 0).T.astype(jnp.bfloat16)
    keys = jnp.concatenate([turned(block(j, 1)) for j in range(heads)], 0).T.astype(jnp.bfloat16)
    values = jnp.concatenate([block(j, 2) for j in range(heads)], 0).T.astype(jnp.bfloat16)
    nk_ref[...] = keys
    nv_ref[...] = values
    lane_head = lax.broadcasted_iota(jnp.int32, (NEW, width), 1) // DH
    for j in range(heads):
        qexp[pl.ds(j * NEW, NEW), :] = jnp.where(lane_head == j, queries, jnp.zeros_like(queries))
    rows = heads * NEW
    fresh = lax.dot_general(qexp[...], keys, NT, preferred_element_type=jnp.float32) * scale
    row_at = lax.broadcasted_iota(jnp.int32, (rows, NEW), 0) % NEW
    col_at = lax.broadcasted_iota(jnp.int32, (rows, NEW), 1)
    fresh = jnp.where(col_at <= row_at, fresh, -1e30)

    def score(i, top):
        fetch(i, k_hbm, kbuf, ksem).wait()
        at = pl.ds(pl.multiple_of(i * KB, KB), KB)
        part = lax.dot_general(qexp[...], kbuf[at, :], NT, preferred_element_type=jnp.float32) * scale
        col = lax.broadcasted_iota(jnp.int32, (rows, KB), 1) + i * KB
        part = jnp.where(col < length, part, -1e30)
        sbuf[:, at] = part
        for t in range(KB // NEW):
            top = jnp.maximum(top, part[:, t * NEW:(t + 1) * NEW])
        return top

    top = lax.fori_loop(0, used, score, fresh)
    highest = jnp.max(top, axis=1, keepdims=True)
    fresh_weights = jnp.exp(fresh - highest)
    mixed = jnp.dot(fresh_weights.astype(jnp.bfloat16), values, preferred_element_type=jnp.float32)

    def weigh(i, carry):
        mixed, total = carry
        fetch(i, v_hbm, vbuf, vsem).wait()
        at = pl.ds(pl.multiple_of(i * KB, KB), KB)
        weights = jnp.exp(sbuf[:, at] - highest)
        for t in range(KB // NEW):
            total = total + weights[:, t * NEW:(t + 1) * NEW]
        mixed = mixed + jnp.dot(weights.astype(jnp.bfloat16), vbuf[at, :], preferred_element_type=jnp.float32)
        return mixed, total

    mixed, total = lax.fori_loop(0, used, weigh, (mixed, fresh_weights))
    total = jnp.sum(total, axis=1, keepdims=True)
    out = jnp.zeros((NEW, width), jnp.float32)
    for j in range(heads):
        at = slice(j * NEW, (j + 1) * NEW)
        out = jnp.where(lane_head == j, mixed[at] / total[at], out)
    att_ref[...] = out.astype(jnp.bfloat16)


def attention(qkv_t, bias, length, keys_old, values_old):
    heads = qkv_t.shape[0] // (3 * DH)
    width = heads * DH
    cosine, sine = rotation_tables(length[0])
    vmem = pl.BlockSpec(memory_space=pltpu.VMEM)
    hbm = pl.BlockSpec(memory_space=pl.ANY)
    out = jax.ShapeDtypeStruct((NEW, width), jnp.bfloat16)
    return pl.pallas_call(
        functools.partial(attention_kernel, heads),
        out_shape=(out, out, out),
        in_specs=[pl.BlockSpec(memory_space=pltpu.SMEM), vmem, vmem, vmem, vmem, hbm, hbm],
        out_specs=(vmem, vmem, vmem),
        scratch_shapes=[
            pltpu.VMEM((CACHE, width), jnp.bfloat16),
            pltpu.VMEM((CACHE, width), jnp.bfloat16),
            pltpu.VMEM((heads * NEW, CACHE), jnp.float32),
            pltpu.VMEM((heads * NEW, width), jnp.bfloat16),
            pltpu.SemaphoreType.DMA((CACHE // KB,)),
            pltpu.SemaphoreType.DMA((CACHE // KB,)),
        ],
        compiler_params=pltpu.CompilerParams(vmem_limit_bytes=60 * 2**20),
        name="attention",
    )(length, qkv_t, bias[:, None], cosine, sine, keys_old, values_old)


def body(
    hidden,
    attn_norm_gain,
    attn_norm_bias,
    mlp_norm_gain,
    mlp_norm_bias,
    qkv_weight,
    qkv_bias,
    out_weight,
    out_bias,
    up_weight,
    up_bias,
    down_weight,
    down_bias,
    cache_keys,
    cache_values,
    cached_len,
):
    qkv_cols = qkv_weight.shape[1]
    attn_normed = normalize(hidden, attn_norm_gain, attn_norm_bias)
    mlp_normed = normalize(hidden, mlp_norm_gain, mlp_norm_bias)
    attn_blocks, mlp_blocks = (
        lax.all_to_all(attn_normed, "req", split_axis=1, concat_axis=0, tiled=True),
        lax.all_to_all(mlp_normed, "req", split_axis=1, concat_axis=0, tiled=True),
    )
    qkv_term = jnp.dot(attn_blocks, qkv_weight, preferred_element_type=jnp.float32)
    up_term = jnp.dot(mlp_blocks, up_weight, preferred_element_type=jnp.float32)
    summed = lax.psum_scatter(
        jnp.concatenate([qkv_term, up_term], axis=1), "req", scatter_dimension=0, tiled=True
    )
    qkv_sum = summed[:, :qkv_cols]
    up_sum = summed[:, qkv_cols:]
    units = jax.nn.gelu(up_sum + up_bias, approximate=True).astype(jnp.bfloat16)
    attended_rows, key_rows, value_rows = attention(
        qkv_sum.T, qkv_bias, cached_len, cache_keys[0], cache_values[0]
    )
    new_keys, new_values = key_rows[None], value_rows[None]
    joined = jnp.concatenate([attended_rows, units], axis=1)
    head_width = attended_rows.shape[1]
    shard_rows = lax.all_gather(joined, "req", axis=0, tiled=True)
    attention_part = jnp.dot(
        shard_rows[:, :head_width], out_weight, preferred_element_type=jnp.float32
    )
    partial_out = attention_part + jnp.dot(
        shard_rows[:, head_width:], down_weight, preferred_element_type=jnp.float32
    )
    bias_total = out_bias + down_bias
    spread_out = lax.all_to_all(partial_out, "req", split_axis=0, concat_axis=1, tiled=True)
    summed_out = lax.psum(spread_out, "head")
    result = (hidden.astype(jnp.float32) + summed_out + bias_total).astype(jnp.bfloat16)
    return (result, new_keys, new_values)


def solution(mesh):
    return jax.shard_map(
        body,
        mesh=mesh,
        in_specs=(
            P("req", None),
            P(),
            P(),
            P(),
            P(),
            P("req", "head"),
            P("head"),
            P("head", "req"),
            P(),
            P("req", "head"),
            P("head"),
            P("head", "req"),
            P(),
            P("req", None, "head"),
            P("req", None, "head"),
            P("req"),
        ),
        out_specs=(P("req", None), P("req", None, "head"), P("req", None, "head")),
        check_vma=False,
    )
```

time: 500 us -> 459 us (0.918)
  matrix products: 46.9 us -> 16.4 us
  local copies, waits for them, and re-layouts: 42.6 us -> 18.1 us
  waiting for transfers between devices: 284 us -> 303 us
  other arithmetic: 33.5 us -> 24.6 us
    dot_general x18 -> x0, matrix products: 30.5 us -> none  [the longest x8 19 us: score_block(): jnp.einsum('qhd,khd->hqk', queries, key_block, preferred_element_type=jnp...]
    dynamic_slice x16 -> x0, local copies, waits for them, and re-layouts: 13.1 us -> none  [weigh_block(): block_scores = lax.dynamic_slice_in_dim(score_store, first_key, KBLOCK, 2)]
    unnamed x36 -> x28, local copies, waits for them, and re-layouts: 17.6 us -> 5.36 us
    all_gather x1, waiting for transfers between devices: 71.9 us -> 80.9 us  [body(): shard_rows = lax.all_gather(joined, 'req', axis=0, tiled=True)]
    reduce_scatter x1, waiting for transfers between devices: 127 us -> 136 us  [body(): lax.psum_scatter(jnp.concatenate([qkv_term, up_term], axis=1), 'req', sca...]
    lt x8 -> x0, other arithmetic: 5.2 us -> none  [score_block(): first_key + key_offsets < length]
  transfers between devices with their start and end apart: 4 -> 4, of which waited for: 4 -> 4; matrix products, arithmetic and copies ran while one was open for 3% -> 1% of each run, Pallas kernels for 0% -> 0%
where the time goes in v1:
time: 459 us; the launch traced here: 457 us
  waiting for transfers between devices  303 us (66%)
  blocking collectives  71.2 us (16%)
  other arithmetic  24.6 us (5%)
  local copies, waits for them, and re-layouts  18.1 us (4%)
  matrix products  16.4 us (4%)
  between operations  14.6 us (3%)
  Pallas kernels  4.99 us (1%)
    reduce_scatter x1, waiting for transfers between devices, body(): lax.psum_scatter(jnp.concatenate([qkv_term, up_term], axis=1), 'req', sca...  136 us
    all_gather x1, waiting for transfers between devices, body(): shard_rows = lax.all_gather(joined, 'req', axis=0, tiled=True)  80.9 us
    psum x1, waiting for transfers between devices, body(): summed_out = lax.psum(spread_out, 'head')  68 us
    all_to_all x1, blocking collectives, body(): lax.all_to_all(partial_out, 'req', split_axis=0, concat_axis=1, tiled=True)  41.2 us
    all_to_all x1, blocking collectives, body(): lax.all_to_all(mlp_normed, 'req', split_axis=1, concat_axis=0, tiled=True)  30 us
    all_to_all x1, waiting for transfers between devices, body(): lax.all_to_all(attn_normed, 'req', split_axis=1, concat_axis=0, tiled=True)  18.1 us
    concatenate x1, other arithmetic, body(): jnp.concatenate([qkv_term, up_term], axis=1)  11.1 us
  transfers between devices with their start and end apart: 4, of which 4 were waited for; matrix products, arithmetic and copies ran while one was open for 1% of the time, Pallas kernels for 0%

profile of v1, /device:TPU:1, one launch (start us, length us, event | category | flops | bytes accessed | tf_op | source)
XLA Modules:
  0.0 457.1 jit_solution(7266400672752379773)
XLA Ops:
  7.2 2.0 copy.24
  10.9 5.4 %fusion.7 = (bf16[128,6144]{0,1:T(8,128)(2,1)}, bf16[128,6144]{0,1:T(8,128)(2,1)S(1)}) fusion(bf16[128,6144]{0,1:T(8,128)(2,1)S(1)} %copy.24, f32[6144]{0:T(1024)S(1)} %copy-done.5, f32[6144]{0:T(1024)S(1)} %copy-done.6, f32[128]{0:T(128)S(1)} %add_rsqrt_fusion, f32[128]{0:T(128)S(1)} %broadcast_multiply_fusion, f32[6144]{0:T(1024)S(1)} %copy-done.7, ...), kind=kLoop, calls=%fused_computation.11 | loop fusion | flops 7077888 | bytes 4817920 | tf_op jit(solution)/shard_map/convert_element_type | solution.py:23
  16.4 30.0 %all_to_all.57 = bf16[128,16,384]{0,2,1:T(8,128)(2,1)} all-to-all(bf16[128,16,384]{0,2,1:T(8,128)(2,1)S(1)} %bitcast.29), channel_id=1, replica_groups=mesh['req'=16,'head'=8] {'req'}, dimensions={1} | all-to-all | bytes 3145728 | tf_op jit(solution)/shard_map/all_to_all | solution.py:165
  46.4 4.4 all-to-all-start
  50.9 2.6 copy.26
  53.5 18.1 %all-to-all-done = bf16[128,16,384]{0,2,1:T(8,128)(2,1)} async-done(((bf16[128,16,384]{0,2,1:T(8,128)(2,1)}), bf16[128,16,384]{0,2,1:T(8,128)(2,1)}, u32[]{:S(2)}, u32[]{:S(2)}) %all-to-all-start) | async-done | bytes 1572896 | tf_op jit(solution)/shard_map/all_to_all | solution.py:164
  71.5 2.6 copy.25
  74.1 5.2 %fusion.24 = f32[2048,1536]{0,1:T(8,128)S(1)} fusion(bf16[2048,384]{1,0:T(8,128)(2,1)} %bitcast.26, bf16[384,1536]{1,0:T(8,128)(2,1)S(1)} %copy-done), kind=kOutput, calls=%fused_computation.41 | convolution fusion | flops 2415919104 | bytes 15335424 | tf_op jit(solution)/shard_map/dot_general | solution.py:168
  79.3 2.8 fusion.23
  82.1 11.1 %pad_maximum_fusion = f32[2048,2688]{0,1:T(8,128)} fusion(f32[2048,1536]{0,1:T(8,128)S(1)} %fusion.24, f32[2048,1152]{0,1:T(8,128)S(1)} %fusion.23), kind=kLoop, calls=%fused_computation | loop fusion | flops 5505024 | bytes 44040192 | tf_op jit(solution)/shard_map/concatenate | solution.py:170
  93.9 1.0 broadcast_in_dim.9.bias_ref
  95.7 135.5 %reduce-scatter.2.cloned.1.call-done = f32[128,2688]{0,1:T(8,128)} async-done(((f32[2048,2688]{0,1:T(8,128)}), f32[128,2688]{0,1:T(8,128)}) %reduce-scatter.2.cloned.1.call-update) | async-done | bytes 1376272 | tf_op jit(solution)/shard_map/reduce_scatter | solution.py:169
  231.3 1.9 slice_bitcast_fusion.qkv_ref
  233.2 5.0 %attention.1 = (bf16[128,384]{1,0:T(8,128)(2,1)}, bf16[128,384]{1,0:T(8,128)(2,1)}, bf16[128,384]{1,0:T(8,128)(2,1)}) custom-call(s32[1]{0:T(128)S(6)} %copy.32.len_ref, f32[1152,128]{1,0:T(8,128)} %slice_bitcast_fusion.qkv_ref, f32[1152,1]{1,0:T(8,128)} %broadcast_in_dim.9.bias_ref, f32[24,128]{1,0:T(8,128)} %get-tuple-element.17.cos_ref, ...), custom_call_target="tpu_custom_call" | custom-call | tf_op jit(solution)/shard_map/attention/pallas_call | solution.py:124
  238.2 1.0 copy.28
  239.2 1.5 fusion.21
  241.6 80.9 %all-gather.2.cloned.1.call-done = bf16[2048,1920]{0,1:T(8,128)(2,1)} async-done(((bf16[128,1920]{0,1:T(8,128)(2,1)}), bf16[2048,1920]{0,1:T(8,128)(2,1)}) %all-gather.2.cloned.1.call-update) | async-done | bytes 7864336 | tf_op jit(solution)/shard_map/all_gather | solution.py:181
  322.5 5.9 %fusion = f32[2048,384]{1,0:T(8,128)S(1)} fusion(bf16[1536,384]{1,0:T(8,128)(2,1)} %param.27, bf16[2048,1920]{0,1:T(8,128)(2,1)} %all-gather.2.cloned.1.call-done), kind=kOutput, calls=%fused_computation.1 | convolution fusion | flops 2415919104 | bytes 10616832 | tf_op jit(solution)/shard_map/dot_general | solution.py:185
  328.4 2.6 convolution_add_fusion
  331.0 41.2 %all_to_all.58 = f32[16,128,384]{2,1,0:T(8,128)} all-to-all(f32[16,128,384]{2,1,0:T(8,128)S(1)} %bitcast.24), channel_id=1, replica_groups=mesh['req'=16,'head'=8] {'req'}, dimensions={0} | all-to-all | bytes 6291456 | tf_op jit(solution)/shard_map/all_to_all | solution.py:189
  372.2 3.6 copy.29
  376.6 68.0 %all-reduce.2.cloned.1.call-done = f32[128,6144]{0,1:T(8,128)} async-done(((f32[128,6144]{0,1:T(8,128)}), f32[128,6144]{0,1:T(8,128)}) %all-reduce.2.cloned.1.call-update) | async-done | bytes 3145744 | tf_op jit(solution)/shard_map/psum | solution.py:190
  444.6 3.4 fusion.12
  448.0 2.6 copy.30
  (42 shorter events, 4.2 us)
Async XLA Ops:
  7.2 67.0 %copy-start = (bf16[384,1536]{1,0:T(8,128)(2,1)S(1)}, bf16[384,1536]{1,0:T(8,128)(2,1)}, u32[]{:S(2)}) copy-start(bf16[384,1536]{1,0:T(8,128)(2,1)} %param.25) | copy-start | bytes 3538948
  7.2 3.7 copy-start.6
  7.2 3.7 copy-start.5
  7.2 3.7 copy-start.8
  7.2 3.7 copy-start.7
  46.4 25.1 %all-to-all-start = ((bf16[128,16,384]{0,2,1:T(8,128)(2,1)}), bf16[128,16,384]{0,2,1:T(8,128)(2,1)}, u32[]{:S(2)}, u32[]{:S(2)}) async-start(bf16[128,16,384]{0,2,1:T(8,128)(2,1)} %bitcast.28), calls=%async_computation | async-start | bytes 3145728 | tf_op jit(solution)/shard_map/all_to_all | solution.py:164
  50.8 180.4 %reduce-scatter.2.cloned.1.call-start = ((), (), s32[]{:S(2)}) async-start(), calls=%async_computation.4 | async-start | bytes 23396352 | tf_op jit(solution)/shard_map/reduce_scatter | solution.py:169
  74.1 5.2 %copy-start.2 = (bf16[16,128,384]{2,1,0:T(8,128)(2,1)S(1)}, bf16[16,128,384]{2,1,0:T(8,128)(2,1)}, u32[]{:S(2)}) copy-start(bf16[16,128,384]{2,1,0:T(8,128)(2,1)} %copy.25) | copy-start | bytes 4718596
  74.1 5.2 %copy-start.3 = (bf16[384,1152]{1,0:T(8,128)(2,1)S(1)}, bf16[384,1152]{1,0:T(8,128)(2,1)}, u32[]{:S(2)}) copy-start(bf16[384,1152]{1,0:T(8,128)(2,1)} %param.21) | copy-start | bytes 2654212
  93.2 0.7 copy-start.11
  93.2 229.3 %all-gather.2.cloned.1.call-start = ((), (), s32[]{:S(2)}) async-start(), calls=%async_computation.5 | async-start | bytes 8355840 | tf_op jit(solution)/shard_map/all_gather | solution.py:181
  233.2 6.0 %copy-start.12 = (f32[1536]{0:T(1024)S(1)}, f32[1536]{0:T(1024)}, u32[]{:S(2)}) copy-start(f32[1536]{0:T(1024)} %param.26) | copy-start | bytes 18436
  241.5 86.9 %copy-start.4 = (bf16[384,384]{1,0:T(8,128)(2,1)S(1)}, bf16[384,384]{1,0:T(8,128)(2,1)}, u32[]{:S(2)}) copy-start(bf16[384,384]{1,0:T(8,128)(2,1)} %param.23) | copy-start | bytes 884740
  241.6 203.0 %all-reduce.2.cloned.1.call-start = ((), (), s32[]{:S(2)}) async-start(), calls=%async_computation.6 | async-start | bytes 6291456 | tf_op jit(solution)/shard_map/psum | solution.py:190
  375.8 0.7 copy-start.9
  375.8 0.8 copy-start.10
  444.6 5.9 %copy-start.1 = (bf16[384,1536]{1,0:T(8,128)(2,1)S(1)}, bf16[384,1536]{1,0:T(8,128)(2,1)}, u32[]{:S(2)}) copy-start(bf16[384,1536]{1,0:T(8,128)(2,1)} %param.25) | copy-start | bytes 3538948
Sparse Core Ops, SparseCore 0:
  93.3 137.8 reduce-scatter.1
  241.7 80.7 all-gather.1
  375.9 68.6 all-reduce.1

commit v2 on v1

--- a/solution.py
+++ b/solution.py
@@ -14,15 +14,6 @@
 CACHE = 4096
 KB = 512
 NT = (((1,), (1,)), ((), ()))
-
-
-def normalize(values, norm_gain, norm_shift):
-    widened = values.astype(jnp.float32)
-    center = jnp.mean(widened, axis=-1, keepdims=True)
-    spread = jnp.mean(jnp.square(widened - center), axis=-1, keepdims=True)
-    return ((widened - center) * lax.rsqrt(spread + 1e-05) * norm_gain + norm_shift).astype(
-        jnp.bfloat16
-    )
 
 
 def rotation_tables(length):
@@ -139,6 +130,571 @@
     )(length, qkv_t, bias[:, None], cosine, sine, keys_old, values_old)
 
 
+MESH = pl.DeviceIdType.MESH
+SIDE = 4
+HALF = 3072
+PART = 1536
+EXT = PART + 128
+VMEM_LIMIT = 62 * 2**20
+
+
+def place():
+    req, head = lax.axis_index("req"), lax.axis_index("head")
+    return req // SIDE, req % SIDE, head // 2, head % 2
+
+
+def meet(barrier, others):
+    for count, target, alone in others:
+        @pl.loop(0, count)
+        def _(i):
+            @pl.when(alone(i))
+            def _():
+                pl.semaphore_signal(barrier, inc=1, device_id=target(i), device_id_type=MESH)
+
+
+def ring_units(y, z, x, core, own, slot, part, send_sem, recv_sem):
+    def send(colour, dp, ds, half, along, step):
+        to = [dp, ds]
+        to[along] = (to[along] + step) % SIDE if isinstance(to[along], int) else lax.rem(
+            to[along] + step + SIDE, SIDE)
+        on_z = (colour == 0) == (along == 0)
+        dev_y = y if on_z else lax.rem(y + step + SIDE, SIDE)
+        dev_z = lax.rem(z + step + SIDE, SIDE) if on_z else z
+        is_own = isinstance(dp, int) and isinstance(ds, int) and dp == 0 and ds == 0
+        src = own(colour, half) if is_own else part(slot(colour, dp, ds, 0), colour, half)
+        source = (colour, dp, ds)
+        dst = part(slot(*source, 0), colour, half) if slot.absolute else part(
+            slot(colour, to[0], to[1], 0), colour, half)
+        return pltpu.make_async_remote_copy(
+            src_ref=src, dst_ref=dst, send_sem=send_sem.at[colour],
+            recv_sem=recv_sem.at[colour, half, to[0] * SIDE + to[1]],
+            device_id=(dev_y * SIDE + dev_z, 2 * x + core), device_id_type=MESH,
+        )
+
+    def arrived(colour, dp, ds, half):
+        ref = part(slot(colour, dp, ds, 0), colour, half)
+        pltpu.make_async_copy(ref, ref, recv_sem.at[colour, half, dp * SIDE + ds]).wait()
+
+    return send, arrived
+
+
+FIRST = ((1, 0), (3, 1), (1, 1), (3, 0), (2, 0), (2, 1))
+
+
+def ring_start(send):
+    for along in (0, 1):
+        for half in (0, 1):
+            for colour in (0, 1):
+                for step in (1, -1):
+                    send(colour, 0, 0, half, along, step).start()
+
+
+def ring_first(send, arrived):
+    for dp, half in FIRST:
+        for colour in (0, 1):
+            arrived(colour, dp, 0, half)
+            if (dp, half) in ((1, 0), (3, 1)):
+                send(colour, dp, 0, half, 0, 1 if dp == 1 else -1).start()
+            for step in (1, -1):
+                send(colour, dp, 0, half, 1, step).start()
+
+
+def ring_second(send, arrived, dp):
+    for ds, half in FIRST:
+        for colour in (0, 1):
+            arrived(colour, dp, ds, half)
+            if (ds, half) in ((1, 0), (3, 1)):
+                send(colour, dp, ds, half, 1, 1 if ds == 1 else -1).start()
+
+
+def gray(i):
+    return i + (i // 2) * (1 - 2 * (i % 2))
+
+
+class Relative:
+    absolute = False
+
+    def __call__(self, colour, dp, ds, _):
+        return dp * SIDE + ds
+
+
+class Absolute:
+    absolute = True
+
+    def __init__(self, y, z):
+        self.y, self.z = y, z
+
+    def __call__(self, colour, dp, ds, _):
+        dy, dz = (ds, dp) if colour == 0 else (dp, ds)
+        return lax.rem(self.y - dy + SIDE, SIDE) * SIDE + lax.rem(self.z - dz + SIDE, SIDE)
+
+
+def front_kernel(
+    xe_ref, wt_ref, gain_ref, ub_ref, qkv_ref, units_ref,
+    xbuf, wbuf, nbuf, pbuf, rbuf, bbuf, qsend, qrecv,
+    xsend_sem, xrecv_sem, own_sem, wsend_sem, wrecv_sem, wself_sem,
+    bias_sem, pair_sem, qsend_sem, qrecv_sem,
+):
+    y, z, x, core = place()
+    me = y * SIDE + z
+    mate = 1 - core
+    barrier = pltpu.get_barrier_semaphore()
+
+    def plane(i):
+        return (i // 2, 2 * x + i % 2)
+
+    meet(barrier, [(32, plane, lambda i: i != 2 * me + core)])
+    pl.semaphore_wait(barrier, 31)
+
+    goal = y // 2
+    kat = pl.ds(pl.multiple_of(((y % 2) * SIDE + z) * 384, 384), 384)
+
+    def wcopy(r):
+        return pltpu.make_async_remote_copy(
+            src_ref=wt_ref.at[r], dst_ref=wbuf.at[:, core, :, kat],
+            send_sem=wsend_sem, recv_sem=wrecv_sem,
+            device_id=(r, 2 * x + goal), device_id_type=MESH,
+        )
+
+    @pl.loop(1, 16)
+    def _(i):
+        wcopy(lax.rem(y + i // SIDE, SIDE) * SIDE + lax.rem(z + i % SIDE, SIDE)).start()
+
+    def mate_w():
+        return pltpu.make_async_remote_copy(
+            src_ref=wt_ref.at[me], dst_ref=wbuf.at[:, core, :, kat],
+            send_sem=wself_sem, recv_sem=wrecv_sem,
+            device_id=(me, 2 * x + mate), device_id_type=MESH,
+        )
+
+    @pl.when(goal != core)
+    def _():
+        mate_w().start()
+
+    @pl.when(goal == core)
+    def _():
+        pltpu.make_async_copy(wt_ref.at[me], wbuf.at[:, core, :, kat], wrecv_sem).start()
+
+    def part(s, colour, half):
+        return xbuf.at[colour, s, pl.ds(64 * half, 64)]
+
+    def own(colour, half):
+        return xe_ref.at[colour, pl.ds(64 * half, 64)]
+
+    send, arrived = ring_units(y, z, x, core, own, Relative(), part, xsend_sem, xrecv_sem)
+    ring_start(send)
+    own_copies = [
+        pltpu.make_async_copy(xe_ref.at[colour], xbuf.at[colour, 0], own_sem.at[colour])
+        for colour in (0, 1)
+    ]
+    for copy in own_copies:
+        copy.start()
+    bias_own = pltpu.make_async_copy(ub_ref, bbuf.at[core], bias_sem.at[0])
+    bias_mate = pltpu.make_async_remote_copy(
+        src_ref=ub_ref, dst_ref=bbuf.at[core], send_sem=bias_sem.at[1], recv_sem=bias_sem.at[2],
+        device_id=(me, 2 * x + mate), device_id_type=MESH,
+    )
+    bias_own.start()
+    bias_mate.start()
+    pbuf[...] = jnp.zeros_like(pbuf)
+    for copy in own_copies:
+        copy.wait()
+    ring_first(send, arrived)
+
+    def compute(colour, dp):
+        @pl.loop(0, SIDE)
+        def _(ds):
+            s = dp * SIDE + ds
+            stat = xbuf[colour, s, :, PART:EXT].astype(jnp.float32)
+            center = stat[:, 0:1] + stat[:, 1:2] + stat[:, 2:3]
+            spread = stat[:, 3:4] + stat[:, 4:5] + stat[:, 5:6]
+            rows = pl.ds(pl.multiple_of(ds * NEW, NEW), NEW)
+            for k in range(PART // 512):
+                at = slice(k * 512, (k + 1) * 512)
+                value = (xbuf[colour, s, :, at].astype(jnp.float32) - center) * spread
+                for kind in (0, 1):
+                    nbuf[kind, rows, at] = (
+                        value * gain_ref[colour, 2 * kind:2 * kind + 1, at]
+                        + gain_ref[colour, 2 * kind + 1:2 * kind + 2, at]
+                    ).astype(jnp.bfloat16)
+
+        for kind in (0, 1):
+            left = wbuf[kind, :, :, pl.ds(pl.multiple_of(colour * PART, PART), PART)]
+            product = lax.dot_general(
+                left.reshape(192, PART), nbuf[kind], NT, preferred_element_type=jnp.float32
+            )
+            for ds in range(SIDE):
+                dy = colour * dp + (1 - colour) * ds
+                dz = colour * ds + (1 - colour) * dp
+                row = lax.rem(y - dy + SIDE, SIDE) * SIDE + lax.rem(z - dz + SIDE, SIDE)
+                pbuf[row, 192 * kind:192 * (kind + 1), :] += product[:, ds * NEW:(ds + 1) * NEW]
+
+    @pl.loop(0, SIDE)
+    def _(i):
+        dp = gray(i)
+        ring_second(send, arrived, dp)
+
+        @pl.when(i == 0)
+        def _():
+            pltpu.make_async_copy(wbuf, wbuf, wrecv_sem).wait()
+
+        @pl.loop(0, 2)
+        def _(colour):
+            compute(colour, dp)
+
+    pair = pltpu.make_async_remote_copy(
+        src_ref=pbuf.at[pl.ds(8 * mate, 8)], dst_ref=rbuf,
+        send_sem=pair_sem.at[0], recv_sem=pair_sem.at[1],
+        device_id=(me, 2 * x + mate), device_id_type=MESH,
+    )
+    pair.start()
+    bias_own.wait()
+    bias_mate.wait()
+    pair.wait_recv()
+    mine = pl.ds(pl.multiple_of(me * 72, 8), 72)
+
+    @pl.loop(0, 8)
+    def _(q):
+        row = 8 * core + q
+        total = pbuf[row] + rbuf[q]
+        for h in (0, 1):
+            qsend[2 * q + h] = total[96 * h:96 * h + 72]
+            remote = pltpu.make_async_remote_copy(
+                src_ref=qsend.at[2 * q + h], dst_ref=qrecv.at[mine],
+                send_sem=qsend_sem, recv_sem=qrecv_sem,
+                device_id=(row, 2 * x + h), device_id_type=MESH,
+            )
+            away = jnp.logical_or(row != me, core != h)
+
+            @pl.when(away)
+            def _():
+                remote.start()
+
+            @pl.when(jnp.logical_not(away))
+            def _():
+                pltpu.make_async_copy(qsend.at[2 * q + h], qrecv.at[mine], qrecv_sem).start()
+        at = pl.ds(pl.multiple_of(q * NEW, NEW), NEW)
+        for h in (0, 1):
+            u = total[192 + 96 * h:288 + 96 * h] + bbuf[h]
+            inner = 0.7978845608028654 * (u + 0.044715 * (u * u * u))
+            units_ref[h, :, at] = (0.5 * u * (1.0 + jnp.tanh(inner))).astype(jnp.bfloat16)
+
+    pltpu.make_async_copy(qrecv, qrecv, qrecv_sem).wait()
+    qkv_ref[...] = qrecv[...]
+    pair.wait_send()
+
+    @pl.when(goal == core)
+    def _():
+        some = qsend.at[pl.ds(0, 15)]
+        pltpu.make_async_copy(some, some, qsend_sem).wait()
+
+    @pl.when(goal != core)
+    def _():
+        pltpu.make_async_copy(qsend, qsend, qsend_sem).wait()
+        mate_w().wait_send()
+
+    some = wt_ref.at[pl.ds(0, 15)]
+    pltpu.make_async_copy(some, some, wsend_sem).wait()
+    for colour in (0, 1):
+        some = xbuf.at[colour, pl.ds(1, 15)]
+        pltpu.make_async_copy(some, some, xsend_sem.at[colour]).wait()
+
+
+def pieces(value):
+    high = lax.reduce_precision(value, 8, 7)
+    rest = value - high
+    middle = lax.reduce_precision(rest, 8, 7)
+    return [high, middle, rest - middle]
+
+
+def front(hidden, gains, qkv_weight, up_weight, up_bias):
+    req, core = lax.axis_index("req"), lax.axis_index("head") % 2
+    widened = hidden.astype(jnp.float32)
+    center = jnp.mean(widened, axis=-1, keepdims=True)
+    spread = lax.rsqrt(jnp.mean(jnp.square(widened - center), axis=-1, keepdims=True) + 1e-05)
+    stat = jnp.concatenate(pieces(center) + pieces(spread), axis=1).astype(jnp.bfloat16)
+    stat = jnp.pad(stat, ((0, 0), (0, 122)))
+    mine = lax.dynamic_slice_in_dim(hidden, core * HALF, HALF, 1)
+    xe = jnp.stack([
+        jnp.concatenate([mine[:, :PART], stat], axis=1),
+        jnp.concatenate([mine[:, PART:], stat], axis=1),
+    ])
+    depth = qkv_weight.shape[0]
+    wq = jnp.pad(qkv_weight.T.reshape(16, 72, depth), ((0, 0), (0, 24), (0, 0)))
+    wt = jnp.stack([wq, up_weight.T.reshape(16, 96, depth)], axis=1)
+    gain = lax.dynamic_slice_in_dim(jnp.stack(gains), core * HALF, HALF, 1)
+    gain = gain.reshape(4, 2, PART).transpose(1, 0, 2)
+    bias = lax.dynamic_slice_in_dim(up_bias, req * 96, 96, 0)
+    bias = jnp.broadcast_to(bias[:, None], (96, 128))
+    vmem = pl.BlockSpec(memory_space=pltpu.VMEM)
+    hbm = pl.BlockSpec(memory_space=pl.ANY)
+    dma = pltpu.SemaphoreType.DMA
+    return pl.pallas_call(
+        front_kernel,
+        out_shape=(
+            jax.ShapeDtypeStruct((1152, NEW), jnp.float32),
+            jax.ShapeDtypeStruct((2, 96, 1024), jnp.bfloat16),
+        ),
+        in_specs=[hbm, hbm, vmem, hbm],
+        out_specs=(vmem, vmem),
+        scratch_shapes=[
+            pltpu.VMEM((2, 16, NEW, EXT), jnp.bfloat16),
+            pltpu.VMEM((2, 2, 96, HALF), jnp.bfloat16),
+            pltpu.VMEM((2, 512, PART), jnp.bfloat16),
+            pltpu.VMEM((16, 384, NEW), jnp.float32),
+            pltpu.VMEM((8, 384, NEW), jnp.float32),
+            pltpu.VMEM((2, 96, NEW), jnp.float32),
+            pltpu.VMEM((16, 72, NEW), jnp.float32),
+            pltpu.VMEM((1152, NEW), jnp.float32),
+            dma((2,)), dma((2, 2, 16)), dma((2,)), dma, dma, dma,
+            dma((3,)), dma((2,)), dma, dma,
+        ],
+        compiler_params=pltpu.CompilerParams(
+            collective_id=0, has_side_effects=True, vmem_limit_bytes=VMEM_LIMIT
+        ),
+        name="front",
+    )(xe, wt, gain, bias)
+
+
+def back_kernel(
+    units_ref, att_ref, wd_ref, wo_ref, base_ref, out_ref,
+    ubuf, abuf, dbuf, obuf_w, dturn, total, rsum, share, fbuf, fout,
+    usend_sem, urecv_sem, own_sem, asend_sem, aself_sem, arecv_sem, w_sem,
+    rsend_sem, rrecv_sem, fsend_sem, frecv_sem, gsend_sem, grecv_sem,
+):
+    y, z, x, core = place()
+    me = y * SIDE + z
+    mate = 1 - core
+    goal = y // 2
+    barrier = pltpu.get_barrier_semaphore()
+
+    def plane(i):
+        return (i // 2, 2 * x + i % 2)
+
+    def line(i):
+        return (me, i)
+
+    meet(barrier, [
+        (32, plane, lambda i: i != 2 * me + core),
+        (8, line, lambda i: i // 2 != x),
+    ])
+    pl.semaphore_wait(barrier, 37)
+
+    spot = (y % 2) * SIDE + z
+    alane = pl.ds(pl.multiple_of(core * 384, 384), 384)
+
+    def acopy(r, sem):
+        return pltpu.make_async_remote_copy(
+            src_ref=att_ref, dst_ref=abuf.at[spot, :, alane],
+            send_sem=sem, recv_sem=arecv_sem,
+            device_id=(r, 2 * x + goal), device_id_type=MESH,
+        )
+
+    @pl.loop(1, 16)
+    def _(i):
+        acopy(lax.rem(y + i // SIDE, SIDE) * SIDE + lax.rem(z + i % SIDE, SIDE), asend_sem).start()
+
+    def mate_a():
+        return pltpu.make_async_remote_copy(
+            src_ref=att_ref, dst_ref=abuf.at[spot, :, alane],
+            send_sem=aself_sem, recv_sem=arecv_sem,
+            device_id=(me, 2 * x + mate), device_id_type=MESH,
+        )
+
+    @pl.when(goal != core)
+    def _():
+        mate_a().start()
+
+    @pl.when(goal == core)
+    def _():
+        pltpu.make_async_copy(att_ref, abuf.at[spot, :, alane], arecv_sem).start()
+
+    def lanes(colour, half):
+        return pl.ds((2 * colour + half) * 256, 256)
+
+    def part(s, colour, half):
+        return ubuf.at[:, s, :, lanes(colour, half)]
+
+    def own(colour, half):
+        return units_ref.at[:, :, lanes(colour, half)]
+
+    send, arrived = ring_units(y, z, x, core, own, Absolute(y, z), part, usend_sem, urecv_sem)
+    ring_start(send)
+    own_copy = pltpu.make_async_copy(units_ref, ubuf.at[:, me], own_sem)
+    own_copy.start()
+
+    copies = []
+    for n, (src, dst) in enumerate(((wd_ref, dbuf), (wo_ref, obuf_w))):
+        copies.append(pltpu.make_async_copy(src, dst.at[core], w_sem.at[3 * n]))
+        copies.append(pltpu.make_async_remote_copy(
+            src_ref=src, dst_ref=dst.at[core], send_sem=w_sem.at[3 * n + 1],
+            recv_sem=w_sem.at[3 * n + 2], device_id=(me, 2 * x + mate), device_id_type=MESH,
+        ))
+    for copy in copies:
+        copy.start()
+    ring_first(send, arrived)
+    for copy in copies:
+        copy.wait()
+
+    @pl.loop(0, 24)
+    def _(k):
+        h, at = k // 12, pl.ds(pl.multiple_of((k % 12) * 128, 128), 128)
+        dturn[h, :, at] = dbuf[h, at, :].T
+
+    @pl.loop(0, SIDE)
+    def _(i):
+        ring_second(send, arrived, gray(i))
+
+    own_copy.wait()
+    pltpu.make_async_copy(abuf, abuf, arecv_sem).wait()
+
+    @pl.loop(0, 8)
+    def _(q):
+        at = pl.ds(pl.multiple_of(q * NEW, NEW), NEW)
+        turned = jnp.zeros((384, NEW), jnp.float32)
+        for h in (0, 1):
+            turned += jnp.dot(
+                dturn[h], ubuf[h, :, :, at].reshape(PART, NEW), preferred_element_type=jnp.float32
+            )
+        attended = jnp.dot(
+            abuf[q], obuf_w[...].reshape(768, 384), preferred_element_type=jnp.float32
+        )
+        total[q] = turned.T + attended
+
+    def rcopy(step):
+        to = lax.rem(x + step, SIDE)
+        return pltpu.make_async_remote_copy(
+            src_ref=total.at[:, pl.ds(pl.multiple_of(32 * to, 32), 32)], dst_ref=rsum.at[step - 1],
+            send_sem=rsend_sem.at[step - 1], recv_sem=rrecv_sem.at[step - 1],
+            device_id=(me, 2 * to + core), device_id_type=MESH,
+        )
+
+    for step in (2, 1, 3):
+        rcopy(step).start()
+    for step in (1, 3, 2):
+        rcopy(step).wait_recv()
+    share[...] = (
+        total[:, pl.ds(pl.multiple_of(32 * x, 32), 32), :] + rsum[0] + rsum[1] + rsum[2]
+    )
+
+    @pl.loop(0, 8)
+    def _(q):
+        row = 8 * core + q
+
+        @pl.when(row != me)
+        def _():
+            pltpu.make_async_remote_copy(
+                src_ref=share.at[q], dst_ref=fbuf.at[spot],
+                send_sem=fsend_sem, recv_sem=frecv_sem,
+                device_id=(row, 2 * x + goal), device_id_type=MESH,
+            ).start()
+
+        @pl.when(row == me)
+        def _():
+            pltpu.make_async_copy(share.at[q], fbuf.at[spot], frecv_sem).start()
+
+    pltpu.make_async_copy(fbuf, fbuf, frecv_sem).wait()
+    rows = pl.ds(pl.multiple_of(32 * x, 32), 32)
+    for j in range(8):
+        at = pl.ds(pl.multiple_of(core * HALF + 384 * j, 384), 384)
+        fout[rows, at] = (base_ref[:, 384 * j:384 * (j + 1)] + fbuf[j]).astype(jnp.bfloat16)
+
+    def piece(owner, c):
+        return fout.at[
+            pl.ds(pl.multiple_of(32 * owner, 32), 32), pl.ds(pl.multiple_of(c * HALF, HALF), HALF)
+        ]
+
+    def gcopy(step):
+        to = lax.rem(x + step, SIDE)
+        return pltpu.make_async_remote_copy(
+            src_ref=piece(x, core), dst_ref=piece(x, core), send_sem=gsend_sem.at[0, step],
+            recv_sem=grecv_sem.at[0, step], device_id=(me, 2 * to + core), device_id_type=MESH,
+        )
+
+    def pass_on(step):
+        owner = lax.rem(x - step + SIDE, SIDE)
+        return pltpu.make_async_remote_copy(
+            src_ref=piece(owner, core), dst_ref=piece(owner, core), send_sem=gsend_sem.at[1, step],
+            recv_sem=grecv_sem.at[1, step], device_id=(me, 2 * x + mate), device_id_type=MESH,
+        )
+
+    def landed(kind, step):
+        owner = lax.rem(x - step + SIDE, SIDE)
+        ref = piece(owner, core if kind == 0 else mate)
+        pltpu.make_async_copy(ref, ref, grecv_sem.at[kind, step]).wait()
+
+    for step in (2, 1, 3):
+        gcopy(step).start()
+    pass_on(0).start()
+    for step in (1, 3, 2):
+        landed(0, step)
+        pass_on(step).start()
+    for step in (0, 1, 3, 2):
+        landed(1, step)
+    out_ref[...] = fout[...]
+
+    for step in (1, 2, 3):
+        gcopy(step).wait_send()
+        rcopy(step).wait_send()
+    for step in range(4):
+        pass_on(step).wait_send()
+
+    @pl.when(goal == core)
+    def _():
+        some = share.at[pl.ds(0, 7)]
+        pltpu.make_async_copy(some, some, fsend_sem).wait()
+
+    @pl.when(goal != core)
+    def _():
+        pltpu.make_async_copy(share, share, fsend_sem).wait()
+        mate_a().wait_send()
+
+    for half in (0, 1):
+        some = abuf.at[pl.ds(0, 7), :, pl.ds(384 * half, 384)]
+        if half == 0:
+            some = abuf.at[:, :, pl.ds(0, 384)]
+        else:
+            some = abuf.at[pl.ds(0, 7), :, pl.ds(384, 384)]
+        pltpu.make_async_copy(some, some, asend_sem).wait()
+    for colour in (0, 1):
+        some = ubuf.at[:, pl.ds(0, 15), :, pl.ds(512 * colour, 512)]
+        pltpu.make_async_copy(some, some, usend_sem.at[colour]).wait()
+
+
+def back(units, attended, hidden, out_weight, down_weight, bias_total):
+    head = lax.axis_index("head")
+    x, core = head // 2, head % 2
+    base = lax.dynamic_slice(hidden, (32 * x, core * HALF), (32, HALF)).astype(jnp.float32)
+    base = base + lax.dynamic_slice_in_dim(bias_total, core * HALF, HALF, 0)
+    vmem = pl.BlockSpec(memory_space=pltpu.VMEM)
+    hbm = pl.BlockSpec(memory_space=pl.ANY)
+    dma = pltpu.SemaphoreType.DMA
+    return pl.pallas_call(
+        back_kernel,
+        out_shape=jax.ShapeDtypeStruct((NEW, 2 * HALF), jnp.bfloat16),
+        in_specs=[hbm, hbm, hbm, hbm, vmem],
+        out_specs=vmem,
+        scratch_shapes=[
+            pltpu.VMEM((2, 16, 96, 1024), jnp.bfloat16),
+            pltpu.VMEM((8, NEW, 768), jnp.bfloat16),
+            pltpu.VMEM((2, PART, 384), jnp.bfloat16),
+            pltpu.VMEM((2, 384, 384), jnp.bfloat16),
+            pltpu.VMEM((2, 384, PART), jnp.bfloat16),
+            pltpu.VMEM((8, NEW, 384), jnp.float32),
+            pltpu.VMEM((3, 8, 32, 384), jnp.float32),
+            pltpu.VMEM((8, 32, 384), jnp.float32),
+            pltpu.VMEM((8, 32, 384), jnp.float32),
+            pltpu.VMEM((NEW, 2 * HALF), jnp.bfloat16),
+            dma((2,)), dma((2, 2, 16)), dma, dma, dma, dma, dma((6,)),
+            dma((3,)), dma((3,)), dma, dma, dma((2, 4)), dma((2, 4)),
+        ],
+        compiler_params=pltpu.CompilerParams(
+            collective_id=1, has_side_effects=True, vmem_limit_bytes=VMEM_LIMIT
+        ),
+        name="back",
+    )(units, attended, down_weight, out_weight, base)
+
+
 def body(
     hidden,
     attn_norm_gain,
@@ -157,39 +713,13 @@
     cache_values,
     cached_len,
 ):
-    qkv_cols = qkv_weight.shape[1]
-    attn_normed = normalize(hidden, attn_norm_gain, attn_norm_bias)
-    mlp_normed = normalize(hidden, mlp_norm_gain, mlp_norm_bias)
-    attn_blocks, mlp_blocks = (
-        lax.all_to_all(attn_normed, "req", split_axis=1, concat_axis=0, tiled=True),
-        lax.all_to_all(mlp_normed, "req", split_axis=1, concat_axis=0, tiled=True),
+    gains = (attn_norm_gain, attn_norm_bias, mlp_norm_gain, mlp_norm_bias)
+    qkv, units = front(hidden, gains, qkv_weight, up_weight, up_bias)
+    attended, key_rows, value_rows = attention(
+        qkv, qkv_bias, cached_len, cache_keys[0], cache_values[0]
     )
-    qkv_term = jnp.dot(attn_blocks, qkv_weight, preferred_element_type=jnp.float32)
-    up_term = jnp.dot(mlp_blocks, up_weight, preferred_element_type=jnp.float32)
-    summed = lax.psum_scatter(
-        jnp.concatenate([qkv_term, up_term], axis=1), "req", scatter_dimension=0, tiled=True
-    )
-    qkv_sum = summed[:, :qkv_cols]
-    up_sum = summed[:, qkv_cols:]
-    units = jax.nn.gelu(up_sum + up_bias, approximate=True).astype(jnp.bfloat16)
-    attended_rows, key_rows, value_rows = attention(
-        qkv_sum.T, qkv_bias, cached_len, cache_keys[0], cache_values[0]
-    )
-    new_keys, new_values = key_rows[None], value_rows[None]
-    joined = jnp.concatenate([attended_rows, units], axis=1)
-    head_width = attended_rows.shape[1]
-    shard_rows = lax.all_gather(joined, "req", axis=0, tiled=True)
-    attention_part = jnp.dot(
-        shard_rows[:, :head_width], out_weight, preferred_element_type=jnp.float32
-    )
-    partial_out = attention_part + jnp.dot(
-        shard_rows[:, head_width:], down_weight, preferred_element_type=jnp.float32
-    )
-    bias_total = out_bias + down_bias
-    spread_out = lax.all_to_all(partial_out, "req", split_axis=0, concat_axis=1, tiled=True)
-    summed_out = lax.psum(spread_out, "head")
-    result = (hidden.astype(jnp.float32) + summed_out + bias_total).astype(jnp.bfloat16)
-    return (result, new_keys, new_values)
+    result = back(units, attended, hidden, out_weight, down_weight, out_bias + down_bias)
+    return (result, key_rows[None], value_rows[None])
 
 
 def solution(mesh):

time: 459 us -> 297 us (0.65)
  waiting for transfers between devices: 303 us -> 0 us
  Pallas kernels: 4.99 us -> 277 us
  blocking collectives: 71.2 us -> 0 us
  other arithmetic: 24.6 us -> 7.45 us
  matrix products: 16.4 us -> 0 us
  between operations: 14.6 us -> 1.46 us
  local copies, waits for them, and re-layouts: 18.1 us -> 10.7 us
    pallas_call x0 -> x2, Pallas kernels: none -> 273 us  [the longest x1 151 us: front(): pl.pallas_call(front_kernel, out_shape=(jax.ShapeDtypeStruct((1152, NEW),...]
    reduce_scatter x1 -> x0, waiting for transfers between devices: 136 us -> none  [body(): lax.psum_scatter(jnp.concatenate([qkv_term, up_term], axis=1), 'req', sca...]
    all_gather x1 -> x0, waiting for transfers between devices: 80.9 us -> none  [body(): shard_rows = lax.all_gather(joined, 'req', axis=0, tiled=True)]
    all_to_all x2 -> x0, blocking collectives: 71.2 us -> none  [the longest x1 41.2 us: body(): lax.all_to_all(partial_out, 'req', split_axis=0, concat_axis=1, tiled=True)]
    psum x1 -> x0, waiting for transfers between devices: 68 us -> none  [body(): summed_out = lax.psum(spread_out, 'head')]
    all_to_all x1 -> x0, waiting for transfers between devices: 18.1 us -> none  [body(): lax.all_to_all(attn_normed, 'req', split_axis=1, concat_axis=0, tiled=True)]
    dot_general x4 -> x0, matrix products: 16.4 us -> none  [the longest x1 5.88 us: body(): jnp.dot(shard_rows[:, head_width:], down_weight, preferred_element_type=j...]
    concatenate x2 -> x0, other arithmetic: 11.9 us -> none  [the longest x1 11.1 us: body(): jnp.concatenate([qkv_term, up_term], axis=1)]
  transfers between devices with their start and end apart: 4 -> 0, of which waited for: 4 -> 0; matrix products, arithmetic and copies ran while one was open for 1% -> 0% of each run, Pallas kernels for 0% -> 0%
where the time goes in v2:
time: 297 us
  Pallas kernels  277 us (93%)
  local copies, waits for them, and re-layouts  10.7 us (4%)
  other arithmetic  7.45 us (3%)
    pallas_call x1, Pallas kernels, front(): pl.pallas_call(front_kernel, out_shape=(jax.ShapeDtypeStruct((1152, NEW),...  151 us
    pallas_call x1, Pallas kernels, back(): pl.pallas_call(back_kernel, out_shape=jax.ShapeDtypeStruct((NEW, 2 * HALF...  121 us

profile of v2, /device:TPU:1, one launch (start us, length us, event | category | flops | bytes accessed | tf_op | source)
XLA Modules:
  0.0 297.0 jit_solution(11620362439030703333)
XLA Ops:
  0.6 1.8 convert_reduce_fusion
  2.5 0.1 copy-done
  2.5 0.6 fusion.1
  3.1 0.1 copy.32
  3.3 0.1 constant_dynamic-slice_fusion
  3.3 0.1 fusion.6
  3.4 1.0 pad_maximum_fusion.1.xe_ref
  4.4 1.7 copy.34
  6.1 2.2 copy.33
  8.3 1.3 pad_bitcast_fusion
  9.6 0.0 copy-start.1
  9.6 0.0 copy-start.3
  9.7 1.7 pad_maximum_fusion.wt_ref
  11.3 0.8 fusion.9
  12.1 0.8 dynamic_slice.17
  12.9 0.7 broadcast_in_dim.8.ub_ref
  13.6 151.5 %front.1 = (f32[1152,128]{1,0:T(8,128)}, bf16[2,96,1024]{2,1,0:T(8,128)(2,1)}) custom-call(bf16[2,128,1664]{2,1,0:T(8,128)(2,1)} %pad_maximum_fusion.1.xe_ref, bf16[16,2,96,384]{3,2,1,0:T(8,128)(2,1)} %pad_maximum_fusion.wt_ref, f32[2,4,1536]{2,1,0:T(4,128)} %bitcast.42, f32[96,128]{1,0:T(8,128)} %broadcast_in_dim.8.ub_ref), custom_call_target="tpu_custom_call" | custom-call | tf_op jit(solution)/shard_map/front/pallas_call | solution.py:432
  165.7 1.0 broadcast_in_dim.24.bias_ref
  166.8 0.1 fusion.10
  166.9 0.6 pad_maximum_fusion.2
  167.5 4.8 %attention.1 = (bf16[128,384]{1,0:T(8,128)(2,1)}, bf16[128,384]{1,0:T(8,128)(2,1)}, bf16[128,384]{1,0:T(8,128)(2,1)}) custom-call(s32[1]{0:T(128)S(6)} %copy.37.len_ref, f32[1152,128]{1,0:T(8,128)} %get-tuple-element.9.qkv_ref, f32[1152,1]{1,0:T(8,128)} %broadcast_in_dim.24.bias_ref, f32[24,128]{1,0:T(8,128)} %get-tuple-element.29.cos_ref, ...), custom_call_target="tpu_custom_call" | custom-call | tf_op jit(solution)/shard_map/attention/pallas_call | solution.py:115
  172.4 0.8 convert_add_fusion.base_ref
  173.2 121.1 %back.1 = bf16[128,6144]{1,0:T(8,128)(2,1)} custom-call(bf16[2,96,1024]{2,1,0:T(8,128)(2,1)} %get-tuple-element.8.units_ref, bf16[128,384]{1,0:T(8,128)(2,1)} %get-tuple-element.10.att_ref, bf16[1536,384]{1,0:T(8,128)(2,1)} %wd_ref.1, bf16[384,384]{1,0:T(8,128)(2,1)} %wo_ref.1, f32[32,3072]{1,0:T(8,128)} %convert_add_fusion.base_ref), custom_call_target="tpu_custom_call" | custom-call | tf_op jit(solution)/shard_map/back/pallas_call | solution.py:672
  294.3 2.7 copy.38
  (19 shorter events, 0.1 us)
Async XLA Ops:
  0.6 1.9 copy-start
  9.6 1.7 copy-start.1
  9.6 1.7 copy-start.2
  9.6 1.7 copy-start.3
  9.6 1.7 copy-start.4
  13.6 152.1 %copy-start.5 = (f32[1152]{0:T(1024)S(1)}, f32[1152]{0:T(1024)}, u32[]{:S(2)}) copy-start(f32[1152]{0:T(1024)} %param.22) | copy-start | bytes 13828
  167.5 4.8 %copy-start.6 = (f32[6144]{0:T(1024)S(1)}, f32[6144]{0:T(1024)}, u32[]{:S(2)}) copy-start(f32[6144]{0:T(1024)} %param.28) | copy-start | bytes 73732
  167.5 4.8 %copy-start.7 = (f32[6144]{0:T(1024)S(1)}, f32[6144]{0:T(1024)}, u32[]{:S(2)}) copy-start(f32[6144]{0:T(1024)} %param.24) | copy-start | bytes 73732

commit v3 on v2

--- a/solution.py
+++ b/solution.py
@@ -189,18 +189,30 @@
                     send(colour, 0, 0, half, along, step).start()
 
 
+def ring_spread(send, dp):
+    for half in (0, 1):
+        for colour in (0, 1):
+            for step in (1, -1):
+                send(colour, dp, 0, half, 1, step).start()
+
+
 def ring_first(send, arrived):
     for dp, half in FIRST:
+        if (dp, half) == (2, 0):
+            ring_spread(send, 1)
         for colour in (0, 1):
             arrived(colour, dp, 0, half)
             if (dp, half) in ((1, 0), (3, 1)):
                 send(colour, dp, 0, half, 0, 1 if dp == 1 else -1).start()
-            for step in (1, -1):
-                send(colour, dp, 0, half, 1, step).start()
-
-
-def ring_second(send, arrived, dp):
+
+
+def ring_second(send, arrived, i):
+    dp = gray(i)
     for ds, half in FIRST:
+        if (ds, half) == (2, 0):
+            @pl.when(i < 2)
+            def _():
+                ring_spread(send, gray(i + 2))
         for colour in (0, 1):
             arrived(colour, dp, ds, half)
             if (ds, half) in ((1, 0), (3, 1)):
@@ -332,7 +344,7 @@
     @pl.loop(0, SIDE)
     def _(i):
         dp = gray(i)
-        ring_second(send, arrived, dp)
+        ring_second(send, arrived, i)
 
         @pl.when(i == 0)
         def _():
@@ -457,10 +469,10 @@
 
 
 def back_kernel(
-    units_ref, att_ref, wd_ref, wo_ref, base_ref, out_ref,
-    ubuf, abuf, dbuf, obuf_w, dturn, total, rsum, share, fbuf, fout,
-    usend_sem, urecv_sem, own_sem, asend_sem, aself_sem, arecv_sem, w_sem,
-    rsend_sem, rrecv_sem, fsend_sem, frecv_sem, gsend_sem, grecv_sem,
+    units_ref, att_ref, wd_ref, wo_ref, rest_ref, bias_ref, out_ref,
+    ubuf, aring, amate, dbuf, obuf, dturn, total, tsend, rsum, share, rest, fout,
+    usend_sem, urecv_sem, own_sem, asend_sem, arecv_sem, amate_sem, w_sem,
+    hsend_sem, hrecv_sem, rsend_sem, rrecv_sem, fsend_sem, frecv_sem, gsend_sem, grecv_sem,
 ):
     y, z, x, core = place()
     me = y * SIDE + z
@@ -480,34 +492,14 @@
     ])
     pl.semaphore_wait(barrier, 37)
 
-    spot = (y % 2) * SIDE + z
-    alane = pl.ds(pl.multiple_of(core * 384, 384), 384)
-
-    def acopy(r, sem):
-        return pltpu.make_async_remote_copy(
-            src_ref=att_ref, dst_ref=abuf.at[spot, :, alane],
-            send_sem=sem, recv_sem=arecv_sem,
-            device_id=(r, 2 * x + goal), device_id_type=MESH,
-        )
-
-    @pl.loop(1, 16)
-    def _(i):
-        acopy(lax.rem(y + i // SIDE, SIDE) * SIDE + lax.rem(z + i % SIDE, SIDE), asend_sem).start()
-
-    def mate_a():
-        return pltpu.make_async_remote_copy(
-            src_ref=att_ref, dst_ref=abuf.at[spot, :, alane],
-            send_sem=aself_sem, recv_sem=arecv_sem,
-            device_id=(me, 2 * x + mate), device_id_type=MESH,
-        )
-
-    @pl.when(goal != core)
-    def _():
-        mate_a().start()
-
-    @pl.when(goal == core)
-    def _():
-        pltpu.make_async_copy(att_ref, abuf.at[spot, :, alane], arecv_sem).start()
+    def apart(s, colour, half):
+        return aring.at[s, pl.ds(32 * (2 * colour + half), 32)]
+
+    def aown(colour, half):
+        return att_ref.at[pl.ds(32 * (2 * colour + half), 32)]
+
+    asend, aarrived = ring_units(y, z, x, core, aown, Absolute(y, z), apart, asend_sem, arecv_sem)
+    ring_start(asend)
 
     def lanes(colour, half):
         return pl.ds((2 * colour + half) * 256, 256)
@@ -520,11 +512,11 @@
 
     send, arrived = ring_units(y, z, x, core, own, Absolute(y, z), part, usend_sem, urecv_sem)
     ring_start(send)
-    own_copy = pltpu.make_async_copy(units_ref, ubuf.at[:, me], own_sem)
-    own_copy.start()
-
-    copies = []
-    for n, (src, dst) in enumerate(((wd_ref, dbuf), (wo_ref, obuf_w))):
+    copies = [
+        pltpu.make_async_copy(units_ref, ubuf.at[:, me], own_sem.at[0]),
+        pltpu.make_async_copy(att_ref, aring.at[me], own_sem.at[1]),
+    ]
+    for n, (src, dst) in enumerate(((wd_ref, dbuf), (wo_ref, obuf))):
         copies.append(pltpu.make_async_copy(src, dst.at[core], w_sem.at[3 * n]))
         copies.append(pltpu.make_async_remote_copy(
             src_ref=src, dst_ref=dst.at[core], send_sem=w_sem.at[3 * n + 1],
@@ -532,72 +524,103 @@
         ))
     for copy in copies:
         copy.start()
+    slot = me % 8
+
+    @pl.when(goal == core)
+    def _():
+        @pl.loop(1, 16)
+        def _(i):
+            row = lax.rem(y + i // SIDE, SIDE) * SIDE + lax.rem(z + i % SIDE, SIDE)
+            pltpu.make_async_remote_copy(
+                src_ref=rest_ref.at[row], dst_ref=rest.at[slot],
+                send_sem=hsend_sem, recv_sem=hrecv_sem,
+                device_id=(row, 2 * x + core), device_id_type=MESH,
+            ).start()
+        pltpu.make_async_copy(rest_ref.at[me], rest.at[slot], hrecv_sem).start()
+
+    ring_first(asend, aarrived)
     ring_first(send, arrived)
+
+    @pl.loop(0, SIDE)
+    def _(i):
+        ring_second(asend, aarrived, i)
+
     for copy in copies:
         copy.wait()
-
-    @pl.loop(0, 24)
-    def _(k):
-        h, at = k // 12, pl.ds(pl.multiple_of((k % 12) * 128, 128), 128)
-        dturn[h, :, at] = dbuf[h, at, :].T
+    pair = pltpu.make_async_remote_copy(
+        src_ref=aring.at[pl.ds(8 * mate, 8)], dst_ref=amate,
+        send_sem=amate_sem.at[0], recv_sem=amate_sem.at[1],
+        device_id=(me, 2 * x + mate), device_id_type=MESH,
+    )
+    pair.start()
 
     @pl.loop(0, SIDE)
     def _(i):
-        ring_second(send, arrived, gray(i))
-
-    own_copy.wait()
-    pltpu.make_async_copy(abuf, abuf, arecv_sem).wait()
-
-    @pl.loop(0, 8)
-    def _(q):
-        at = pl.ds(pl.multiple_of(q * NEW, NEW), NEW)
-        turned = jnp.zeros((384, NEW), jnp.float32)
-        for h in (0, 1):
-            turned += jnp.dot(
-                dturn[h], ubuf[h, :, :, at].reshape(PART, NEW), preferred_element_type=jnp.float32
-            )
-        attended = jnp.dot(
-            abuf[q], obuf_w[...].reshape(768, 384), preferred_element_type=jnp.float32
-        )
-        total[q] = turned.T + attended
-
-    def rcopy(step):
+        @pl.loop(0, 6)
+        def _(k):
+            n = 6 * i + k
+            h, at = n // 12, pl.ds(pl.multiple_of((n % 12) * 128, 128), 128)
+            dturn[h, :, at] = dbuf[h, at, :].T
+
+        ring_second(send, arrived, i)
+
+    pair.wait_recv()
+
+    def rcopy(q, step):
         to = lax.rem(x + step, SIDE)
         return pltpu.make_async_remote_copy(
-            src_ref=total.at[:, pl.ds(pl.multiple_of(32 * to, 32), 32)], dst_ref=rsum.at[step - 1],
+            src_ref=tsend.at[q, pl.ds(pl.multiple_of(32 * to, 32), 32)],
+            dst_ref=rsum.at[step - 1, q],
             send_sem=rsend_sem.at[step - 1], recv_sem=rrecv_sem.at[step - 1],
             device_id=(me, 2 * to + core), device_id_type=MESH,
         )
 
-    for step in (2, 1, 3):
-        rcopy(step).start()
+    @pl.loop(0, 4)
+    def _(p):
+        at = pl.ds(pl.multiple_of(2 * p * NEW, 2 * NEW), 2 * NEW)
+        turned = jnp.zeros((384, 2 * NEW), jnp.float32)
+        for h in (0, 1):
+            turned += jnp.dot(
+                dturn[h], ubuf[h, :, :, at].reshape(PART, 2 * NEW),
+                preferred_element_type=jnp.float32,
+            )
+        for n in (0, 1):
+            q = 2 * p + n
+            value = turned[:, n * NEW:(n + 1) * NEW].T
+            value += jnp.dot(
+                aring[8 * core + q], obuf[core], preferred_element_type=jnp.float32
+            ) + jnp.dot(amate[q], obuf[mate], preferred_element_type=jnp.float32)
+            total[q] = value
+            tsend[q] = value.astype(jnp.bfloat16)
+        for n in (0, 1):
+            for step in (2, 1, 3):
+                rcopy(2 * p + n, step).start()
+
+    pltpu.make_async_copy(rest, rest, hrecv_sem).wait()
     for step in (1, 3, 2):
-        rcopy(step).wait_recv()
-    share[...] = (
-        total[:, pl.ds(pl.multiple_of(32 * x, 32), 32), :] + rsum[0] + rsum[1] + rsum[2]
-    )
+        some = rsum.at[step - 1]
+        pltpu.make_async_copy(some, some, rrecv_sem.at[step - 1]).wait()
+    rows = pl.ds(pl.multiple_of(32 * x, 32), 32)
+    mine = pl.ds(pl.multiple_of(384 * me, 384), 384)
 
     @pl.loop(0, 8)
     def _(q):
+        value = total[q, rows, :] + rsum[0, q].astype(jnp.float32)
+        value += rsum[1, q].astype(jnp.float32) + rsum[2, q].astype(jnp.float32)
+        share[q] = (rest[q].astype(jnp.float32) + (value + bias_ref[...])).astype(jnp.bfloat16)
         row = 8 * core + q
 
         @pl.when(row != me)
         def _():
             pltpu.make_async_remote_copy(
-                src_ref=share.at[q], dst_ref=fbuf.at[spot],
+                src_ref=share.at[q], dst_ref=fout.at[rows, mine],
                 send_sem=fsend_sem, recv_sem=frecv_sem,
                 device_id=(row, 2 * x + goal), device_id_type=MESH,
             ).start()
 
         @pl.when(row == me)
         def _():
-            pltpu.make_async_copy(share.at[q], fbuf.at[spot], frecv_sem).start()
-
-    pltpu.make_async_copy(fbuf, fbuf, frecv_sem).wait()
-    rows = pl.ds(pl.multiple_of(32 * x, 32), 32)
-    for j in range(8):
-        at = pl.ds(pl.multiple_of(core * HALF + 384 * j, 384), 384)
-        fout[rows, at] = (base_ref[:, 384 * j:384 * (j + 1)] + fbuf[j]).astype(jnp.bfloat16)
+            pltpu.make_async_copy(share.at[q], fout.at[rows, mine], frecv_sem).start()
 
     def piece(owner, c):
         return fout.at[
@@ -623,6 +646,7 @@
         ref = piece(owner, core if kind == 0 else mate)
         pltpu.make_async_copy(ref, ref, grecv_sem.at[kind, step]).wait()
 
+    pltpu.make_async_copy(piece(x, core), piece(x, core), frecv_sem).wait()
     for step in (2, 1, 3):
         gcopy(step).start()
     pass_on(0).start()
@@ -635,64 +659,64 @@
 
     for step in (1, 2, 3):
         gcopy(step).wait_send()
-        rcopy(step).wait_send()
+        some = rsum.at[step - 1]
+        pltpu.make_async_copy(some, some, rsend_sem.at[step - 1]).wait()
     for step in range(4):
         pass_on(step).wait_send()
+    pair.wait_send()
 
     @pl.when(goal == core)
     def _():
         some = share.at[pl.ds(0, 7)]
         pltpu.make_async_copy(some, some, fsend_sem).wait()
+        some = rest_ref.at[pl.ds(0, 15)]
+        pltpu.make_async_copy(some, some, hsend_sem).wait()
 
     @pl.when(goal != core)
     def _():
         pltpu.make_async_copy(share, share, fsend_sem).wait()
-        mate_a().wait_send()
-
-    for half in (0, 1):
-        some = abuf.at[pl.ds(0, 7), :, pl.ds(384 * half, 384)]
-        if half == 0:
-            some = abuf.at[:, :, pl.ds(0, 384)]
-        else:
-            some = abuf.at[pl.ds(0, 7), :, pl.ds(384, 384)]
-        pltpu.make_async_copy(some, some, asend_sem).wait()
+
     for colour in (0, 1):
         some = ubuf.at[:, pl.ds(0, 15), :, pl.ds(512 * colour, 512)]
         pltpu.make_async_copy(some, some, usend_sem.at[colour]).wait()
+        some = aring.at[pl.ds(0, 15), pl.ds(64 * colour, 64)]
+        pltpu.make_async_copy(some, some, asend_sem.at[colour]).wait()
 
 
 def back(units, attended, hidden, out_weight, down_weight, bias_total):
-    head = lax.axis_index("head")
-    x, core = head // 2, head % 2
-    base = lax.dynamic_slice(hidden, (32 * x, core * HALF), (32, HALF)).astype(jnp.float32)
-    base = base + lax.dynamic_slice_in_dim(bias_total, core * HALF, HALF, 0)
+    req, x = lax.axis_index("req"), lax.axis_index("head") // 2
+    rest = lax.dynamic_slice_in_dim(hidden, 32 * x, 32, 0)
+    rest = rest.reshape(32, 16, 384).transpose(1, 0, 2)
+    bias = lax.dynamic_slice_in_dim(bias_total, req * 384, 384, 0)[None, :]
     vmem = pl.BlockSpec(memory_space=pltpu.VMEM)
     hbm = pl.BlockSpec(memory_space=pl.ANY)
     dma = pltpu.SemaphoreType.DMA
     return pl.pallas_call(
         back_kernel,
         out_shape=jax.ShapeDtypeStruct((NEW, 2 * HALF), jnp.bfloat16),
-        in_specs=[hbm, hbm, hbm, hbm, vmem],
+        in_specs=[hbm, hbm, hbm, hbm, hbm, vmem],
         out_specs=vmem,
         scratch_shapes=[
             pltpu.VMEM((2, 16, 96, 1024), jnp.bfloat16),
-            pltpu.VMEM((8, NEW, 768), jnp.bfloat16),
+            pltpu.VMEM((16, NEW, 384), jnp.bfloat16),
+            pltpu.VMEM((8, NEW, 384), jnp.bfloat16),
             pltpu.VMEM((2, PART, 384), jnp.bfloat16),
             pltpu.VMEM((2, 384, 384), jnp.bfloat16),
             pltpu.VMEM((2, 384, PART), jnp.bfloat16),
             pltpu.VMEM((8, NEW, 384), jnp.float32),
-            pltpu.VMEM((3, 8, 32, 384), jnp.float32),
-            pltpu.VMEM((8, 32, 384), jnp.float32),
-            pltpu.VMEM((8, 32, 384), jnp.float32),
+            pltpu.VMEM((8, NEW, 384), jnp.bfloat16),
+            pltpu.VMEM((3, 8, 32, 384), jnp.bfloat16),
+            pltpu.VMEM((8, 32, 384), jnp.bfloat16),
+            pltpu.VMEM((8, 32, 384), jnp.bfloat16),
             pltpu.VMEM((NEW, 2 * HALF), jnp.bfloat16),
-            dma((2,)), dma((2, 2, 16)), dma, dma, dma, dma, dma((6,)),
-            dma((3,)), dma((3,)), dma, dma, dma((2, 4)), dma((2, 4)),
+            dma((2,)), dma((2, 2, 16)), dma((2,)), dma((2,)), dma((2, 2, 16)), dma((2,)), dma((6,)),
+            dma, dma, dma((3,)), dma((3,)), dma, dma, dma((2, 4)), dma((2, 4)),
         ],
         compiler_params=pltpu.CompilerParams(
             collective_id=1, has_side_effects=True, vmem_limit_bytes=VMEM_LIMIT
         ),
         name="back",
-    )(units, attended, down_weight, out_weight, base)
+    )(units, attended, down_weight, out_weight, rest, bias)
 
 
 def body(

time: 297 us -> 268 us (0.902)
  Pallas kernels: 277 us -> 246 us
    pallas_call x1, Pallas kernels: 121 us -> 103 us  [back(): pl.pallas_call(back_kernel, out_shape=jax.ShapeDtypeStruct((NEW, 2 * HALF...]
    pallas_call x1, Pallas kernels: 151 us -> 139 us  [front(): pl.pallas_call(front_kernel, out_shape=(jax.ShapeDtypeStruct((1152, NEW),...]
where the time goes in v3:
time: 268 us; the launch traced here: 267 us
  Pallas kernels  246 us (92%)
  local copies, waits for them, and re-layouts  12.1 us (5%)
  other arithmetic  7.44 us (3%)
    pallas_call x1, Pallas kernels, front(): pl.pallas_call(front_kernel, out_shape=(jax.ShapeDtypeStruct((1152, NEW),...  139 us
    pallas_call x1, Pallas kernels, back(): pl.pallas_call(back_kernel, out_shape=jax.ShapeDtypeStruct((NEW, 2 * HALF...  103 us

profile of v3, /device:TPU:1, one launch (start us, length us, event | category | flops | bytes accessed | tf_op | source)
XLA Modules:
  0.0 267.5 jit_solution(8206979117236111375)
XLA Ops:
  0.6 1.8 convert_reduce_fusion
  2.5 0.1 copy-done
  2.5 0.6 fusion.1
  3.1 0.1 copy.33
  3.3 0.1 constant_dynamic-slice_fusion
  3.3 0.1 fusion.6
  3.4 1.0 pad_maximum_fusion.1.xe_ref
  4.4 1.7 copy.35
  6.1 2.2 copy.34
  8.3 1.3 pad_bitcast_fusion
  9.7 1.7 pad_maximum_fusion.wt_ref
  11.3 0.8 fusion.9
  12.1 0.8 dynamic_slice.17
  12.9 0.7 broadcast_in_dim.10.ub_ref
  13.6 139.1 %front.1 = (f32[1152,128]{1,0:T(8,128)}, bf16[2,96,1024]{2,1,0:T(8,128)(2,1)}) custom-call(bf16[2,128,1664]{2,1,0:T(8,128)(2,1)} %pad_maximum_fusion.1.xe_ref, bf16[16,2,96,384]{3,2,1,0:T(8,128)(2,1)} %pad_maximum_fusion.wt_ref, f32[2,4,1536]{2,1,0:T(4,128)} %bitcast.51, f32[96,128]{1,0:T(8,128)} %broadcast_in_dim.10.ub_ref), custom_call_target="tpu_custom_call" | custom-call | tf_op jit(solution)/shard_map/front/pallas_call | solution.py:444
  153.3 1.0 broadcast_in_dim.27.bias_ref
  154.4 0.1 fusion.10
  154.5 0.6 pad_maximum_fusion.2
  155.1 4.8 %attention.1 = (bf16[128,384]{1,0:T(8,128)(2,1)}, bf16[128,384]{1,0:T(8,128)(2,1)}, bf16[128,384]{1,0:T(8,128)(2,1)}) custom-call(s32[1]{0:T(128)S(6)} %copy.42.len_ref, f32[1152,128]{1,0:T(8,128)} %get-tuple-element.9.qkv_ref, f32[1152,1]{1,0:T(8,128)} %broadcast_in_dim.27.bias_ref, f32[24,128]{1,0:T(8,128)} %get-tuple-element.29.cos_ref, ...), custom_call_target="tpu_custom_call" | custom-call | tf_op jit(solution)/shard_map/attention/pallas_call | solution.py:115
  160.0 0.8 copy.40
  160.8 0.8 dynamic-slice_add_fusion
  161.6 0.6 broadcast_in_dim.24.bias_ref
  162.2 102.6 %back.1 = bf16[128,6144]{1,0:T(8,128)(2,1)} custom-call(bf16[2,96,1024]{2,1,0:T(8,128)(2,1)} %get-tuple-element.8.units_ref, bf16[128,384]{1,0:T(8,128)(2,1)} %get-tuple-element.10.att_ref, bf16[1536,384]{1,0:T(8,128)(2,1)} %wd_ref.1, bf16[384,384]{1,0:T(8,128)(2,1)} %wo_ref.1, bf16[16,32,384]{2,1,0:T(8,128)(2,1)} %bitcast.47, ...), custom_call_target="tpu_custom_call" | custom-call | tf_op jit(solution)/shard_map/back/pallas_call | solution.py:694
  264.8 2.7 %copy.43 = bf16[128,6144]{1,0:T(8,128)(2,1)} copy(bf16[128,6144]{1,0:T(8,128)(2,1)} %back.1) | data formatting | bytes 3145728
  (17 shorter events, 0.1 us)
Async XLA Ops:
  0.6 1.9 copy-start
  9.6 1.7 copy-start.1
  9.6 1.7 copy-start.2
  9.6 1.7 copy-start.3
  9.6 1.7 copy-start.4
  13.6 139.7 %copy-start.5 = (f32[1152]{0:T(1024)S(1)}, f32[1152]{0:T(1024)}, u32[]{:S(2)}) copy-start(f32[1152]{0:T(1024)} %param.22) | copy-start | bytes 13828

commit v4 on v3

--- a/solution.py
+++ b/solution.py
@@ -134,7 +134,7 @@
 SIDE = 4
 HALF = 3072
 PART = 1536
-EXT = PART + 128
+DIRECT = 512
 VMEM_LIMIT = 62 * 2**20
 
 
@@ -242,65 +242,68 @@
 
 
 def front_kernel(
-    xe_ref, wt_ref, gain_ref, ub_ref, qkv_ref, units_ref,
-    xbuf, wbuf, nbuf, pbuf, rbuf, bbuf, qsend, qrecv,
-    xsend_sem, xrecv_sem, own_sem, wsend_sem, wrecv_sem, wself_sem,
-    bias_sem, pair_sem, qsend_sem, qrecv_sem,
+    hid_ref, stat_ref, wt_ref, gain_ref, ub_ref, qkv_ref, units_ref,
+    xbuf, sbuf, stats, wbuf, nbuf, pbuf, rbuf, bbuf, qsend, qrecv,
+    xsend_sem, xrecv_sem, own_sem, side_send, side_recv, stat_send, stat_recv,
+    wsend_sem, wrecv_sem, wself_sem, bias_sem, pair_sem, qsend_sem, qrecv_sem,
 ):
     y, z, x, core = place()
     me = y * SIDE + z
     mate = 1 - core
+    own_copies = []
+    for colour in (0, 1):
+        base = core * HALF + colour * PART
+
+        def take(lane, width, dst, n):
+            at = pl.ds(pl.multiple_of(base + lane, 256), width)
+            own_copies.append(
+                pltpu.make_async_copy(hid_ref.at[:, at], dst, own_sem.at[colour, n]))
+
+        take(0, DIRECT, xbuf.at[colour, 0, :, pl.ds(0, DIRECT)], 0)
+        take(DIRECT + 256 * x, 256, xbuf.at[colour, 0, :, pl.ds(DIRECT, 256)], 1)
+        for dx in (1, 2, 3):
+            plane_at = lax.rem(x - dx + SIDE, SIDE)
+            take(DIRECT + 256 * plane_at, 256, sbuf.at[colour, dx - 1, 0], 1 + dx)
+    for copy in own_copies:
+        copy.start()
     barrier = pltpu.get_barrier_semaphore()
 
     def plane(i):
         return (i // 2, 2 * x + i % 2)
 
-    meet(barrier, [(32, plane, lambda i: i != 2 * me + core)])
-    pl.semaphore_wait(barrier, 31)
+    def line(i):
+        return (me, i)
+
+    meet(barrier, [
+        (32, plane, lambda i: i != 2 * me + core),
+        (8, line, lambda i: i // 2 != x),
+    ])
+    for copy in own_copies:
+        copy.wait()
+    pl.semaphore_wait(barrier, 37)
 
     goal = y // 2
     kat = pl.ds(pl.multiple_of(((y % 2) * SIDE + z) * 384, 384), 384)
 
-    def wcopy(r):
-        return pltpu.make_async_remote_copy(
-            src_ref=wt_ref.at[r], dst_ref=wbuf.at[:, core, :, kat],
-            send_sem=wsend_sem, recv_sem=wrecv_sem,
-            device_id=(r, 2 * x + goal), device_id_type=MESH,
-        )
+    def part(s, colour, half):
+        return xbuf.at[colour, s, pl.ds(64 * half, 64)]
+
+    def own(colour, half):
+        return part(0, colour, half)
+
+    send, arrived = ring_units(y, z, x, core, own, Relative(), part, xsend_sem, xrecv_sem)
+    ring_start(send)
+
+    def other(i):
+        return lax.rem(y + i // SIDE, SIDE) * SIDE + lax.rem(z + i % SIDE, SIDE)
 
     @pl.loop(1, 16)
     def _(i):
-        wcopy(lax.rem(y + i // SIDE, SIDE) * SIDE + lax.rem(z + i % SIDE, SIDE)).start()
-
-    def mate_w():
-        return pltpu.make_async_remote_copy(
-            src_ref=wt_ref.at[me], dst_ref=wbuf.at[:, core, :, kat],
-            send_sem=wself_sem, recv_sem=wrecv_sem,
-            device_id=(me, 2 * x + mate), device_id_type=MESH,
-        )
-
-    @pl.when(goal != core)
-    def _():
-        mate_w().start()
-
-    @pl.when(goal == core)
-    def _():
-        pltpu.make_async_copy(wt_ref.at[me], wbuf.at[:, core, :, kat], wrecv_sem).start()
-
-    def part(s, colour, half):
-        return xbuf.at[colour, s, pl.ds(64 * half, 64)]
-
-    def own(colour, half):
-        return xe_ref.at[colour, pl.ds(64 * half, 64)]
-
-    send, arrived = ring_units(y, z, x, core, own, Relative(), part, xsend_sem, xrecv_sem)
-    ring_start(send)
-    own_copies = [
-        pltpu.make_async_copy(xe_ref.at[colour], xbuf.at[colour, 0], own_sem.at[colour])
-        for colour in (0, 1)
-    ]
-    for copy in own_copies:
-        copy.start()
+        pltpu.make_async_remote_copy(
+            src_ref=stat_ref, dst_ref=stats.at[me], send_sem=stat_send, recv_sem=stat_recv,
+            device_id=(other(i), 2 * x + core), device_id_type=MESH,
+        ).start()
+    pltpu.make_async_copy(stat_ref, stats.at[me], stat_recv).start()
     bias_own = pltpu.make_async_copy(ub_ref, bbuf.at[core], bias_sem.at[0])
     bias_mate = pltpu.make_async_remote_copy(
         src_ref=ub_ref, dst_ref=bbuf.at[core], send_sem=bias_sem.at[1], recv_sem=bias_sem.at[2],
@@ -308,27 +311,104 @@
     )
     bias_own.start()
     bias_mate.start()
+
+    def mate_w():
+        return pltpu.make_async_remote_copy(
+            src_ref=wt_ref.at[me], dst_ref=wbuf.at[:, core, :, kat],
+            send_sem=wself_sem, recv_sem=wrecv_sem,
+            device_id=(me, 2 * x + mate), device_id_type=MESH,
+        )
+
+    @pl.when(goal != core)
+    def _():
+        mate_w().start()
+
+    @pl.when(goal == core)
+    def _():
+        pltpu.make_async_copy(wt_ref.at[me], wbuf.at[:, core, :, kat], wrecv_sem).start()
+
+    def weights_out(first, count):
+        @pl.loop(first, first + count)
+        def _(i):
+            pltpu.make_async_remote_copy(
+                src_ref=wt_ref.at[other(i)], dst_ref=wbuf.at[:, core, :, kat],
+                send_sem=wsend_sem, recv_sem=wrecv_sem,
+                device_id=(other(i), 2 * x + goal), device_id_type=MESH,
+            ).start()
+
+    def slots(kind, dp):
+        return pl.ds(dp * SIDE, 1) if kind == 0 else pl.ds(dp * SIDE + 1, 3)
+
+    def side_full(colour, kind, dp, step):
+        way = (1 - step) // 2
+        return pltpu.make_async_remote_copy(
+            src_ref=xbuf.at[colour, slots(kind, dp), :, pl.ds(DIRECT, 256)],
+            dst_ref=sbuf.at[colour, 2 * way, slots(kind, dp)],
+            send_sem=side_send.at[colour], recv_sem=side_recv.at[colour, kind, dp, way],
+            device_id=(me, 2 * lax.rem(x + step + SIDE, SIDE) + core), device_id_type=MESH,
+        )
+
+    def side_relay(colour, kind, dp, step):
+        way = (1 - step) // 2
+        rows = pl.ds(64 * way, 64)
+        return pltpu.make_async_remote_copy(
+            src_ref=sbuf.at[colour, 2 * way, slots(kind, dp), rows],
+            dst_ref=sbuf.at[colour, 1, slots(kind, dp), rows],
+            send_sem=side_send.at[colour], recv_sem=side_recv.at[colour, kind, dp, 2 + way],
+            device_id=(me, 2 * lax.rem(x + step + SIDE, SIDE) + core), device_id_type=MESH,
+        )
+
+    def side_wait(colour, kind, dp, n):
+        if n < 2:
+            ref = sbuf.at[colour, 2 * n, slots(kind, dp)]
+        else:
+            ref = sbuf.at[colour, 1, slots(kind, dp), pl.ds(64 * (n - 2), 64)]
+        pltpu.make_async_copy(ref, ref, side_recv.at[colour, kind, dp, n]).wait()
+
+    def side_out(kind, dp):
+        for colour in (0, 1):
+            for step in (1, -1):
+                side_full(colour, kind, dp, step).start()
+
+    def side_on(kind, dp):
+        for colour in (0, 1):
+            for way in (0, 1):
+                side_wait(colour, kind, dp, way)
+                side_relay(colour, kind, dp, 1 - 2 * way).start()
+
     pbuf[...] = jnp.zeros_like(pbuf)
-    for copy in own_copies:
-        copy.wait()
     ring_first(send, arrived)
+    for dp in (1, 3, 2):
+        side_out(0, dp)
+
+    def origin(colour, dp, ds):
+        dy = colour * dp + (1 - colour) * ds
+        dz = colour * ds + (1 - colour) * dp
+        return lax.rem(y - dy + SIDE, SIDE) * SIDE + lax.rem(z - dz + SIDE, SIDE)
 
     def compute(colour, dp):
         @pl.loop(0, SIDE)
         def _(ds):
             s = dp * SIDE + ds
-            stat = xbuf[colour, s, :, PART:EXT].astype(jnp.float32)
-            center = stat[:, 0:1] + stat[:, 1:2] + stat[:, 2:3]
-            spread = stat[:, 3:4] + stat[:, 4:5] + stat[:, 5:6]
+            turned = stats[origin(colour, dp, ds)].T
+            center, spread = turned[:, 0:1], turned[:, 1:2]
             rows = pl.ds(pl.multiple_of(ds * NEW, NEW), NEW)
-            for k in range(PART // 512):
-                at = slice(k * 512, (k + 1) * 512)
-                value = (xbuf[colour, s, :, at].astype(jnp.float32) - center) * spread
+            base = core * HALF + colour * PART
+
+            def norm(raw, lane, width):
+                value = (raw.astype(jnp.float32) - center) * spread
+                at = pl.ds(pl.multiple_of(base + lane, 256), width)
+                to = pl.ds(pl.multiple_of(lane, 256), width)
                 for kind in (0, 1):
-                    nbuf[kind, rows, at] = (
-                        value * gain_ref[colour, 2 * kind:2 * kind + 1, at]
-                        + gain_ref[colour, 2 * kind + 1:2 * kind + 2, at]
+                    nbuf[kind, rows, to] = (
+                        value * gain_ref[2 * kind:2 * kind + 1, at]
+                        + gain_ref[2 * kind + 1:2 * kind + 2, at]
                     ).astype(jnp.bfloat16)
+
+            norm(xbuf[colour, s, :, 0:DIRECT], 0, DIRECT)
+            norm(xbuf[colour, s, :, DIRECT:DIRECT + 256], DIRECT + 256 * x, 256)
+            for dx in (1, 2, 3):
+                norm(sbuf[colour, dx - 1, s], DIRECT + 256 * lax.rem(x - dx + SIDE, SIDE), 256)
 
         for kind in (0, 1):
             left = wbuf[kind, :, :, pl.ds(pl.multiple_of(colour * PART, PART), PART)]
@@ -336,19 +416,36 @@
                 left.reshape(192, PART), nbuf[kind], NT, preferred_element_type=jnp.float32
             )
             for ds in range(SIDE):
-                dy = colour * dp + (1 - colour) * ds
-                dz = colour * ds + (1 - colour) * dp
-                row = lax.rem(y - dy + SIDE, SIDE) * SIDE + lax.rem(z - dz + SIDE, SIDE)
+                row = origin(colour, dp, ds)
                 pbuf[row, 192 * kind:192 * (kind + 1), :] += product[:, ds * NEW:(ds + 1) * NEW]
+
+    @pl.loop(0, SIDE)
+    def _(i):
+        ring_second(send, arrived, i)
+        side_out(1, gray(i))
+
+    weights_out(1, 15)
+    for dp in (1, 3, 2):
+        side_on(0, dp)
+
+    @pl.loop(0, SIDE)
+    def _(i):
+        side_on(1, gray(i))
+
+    pltpu.make_async_copy(stats, stats, stat_recv).wait()
+    pltpu.make_async_copy(wbuf, wbuf, wrecv_sem).wait()
 
     @pl.loop(0, SIDE)
     def _(i):
         dp = gray(i)
-        ring_second(send, arrived, i)
-
-        @pl.when(i == 0)
-        def _():
-            pltpu.make_async_copy(wbuf, wbuf, wrecv_sem).wait()
+        for colour in (0, 1):
+            for n in (2, 3):
+                side_wait(colour, 1, dp, n)
+
+            @pl.when(i > 0)
+            def _():
+                for n in (2, 3):
+                    side_wait(colour, 0, dp, n)
 
         @pl.loop(0, 2)
         def _(colour):
@@ -410,32 +507,22 @@
     for colour in (0, 1):
         some = xbuf.at[colour, pl.ds(1, 15)]
         pltpu.make_async_copy(some, some, xsend_sem.at[colour]).wait()
-
-
-def pieces(value):
-    high = lax.reduce_precision(value, 8, 7)
-    rest = value - high
-    middle = lax.reduce_precision(rest, 8, 7)
-    return [high, middle, rest - middle]
+        some = sbuf.at[colour, :, pl.ds(1, 15)]
+        pltpu.make_async_copy(some, some, side_send.at[colour]).wait()
+    some = stats.at[pl.ds(0, 15)]
+    pltpu.make_async_copy(some, some, stat_send).wait()
 
 
 def front(hidden, gains, qkv_weight, up_weight, up_bias):
-    req, core = lax.axis_index("req"), lax.axis_index("head") % 2
+    req = lax.axis_index("req")
     widened = hidden.astype(jnp.float32)
-    center = jnp.mean(widened, axis=-1, keepdims=True)
-    spread = lax.rsqrt(jnp.mean(jnp.square(widened - center), axis=-1, keepdims=True) + 1e-05)
-    stat = jnp.concatenate(pieces(center) + pieces(spread), axis=1).astype(jnp.bfloat16)
-    stat = jnp.pad(stat, ((0, 0), (0, 122)))
-    mine = lax.dynamic_slice_in_dim(hidden, core * HALF, HALF, 1)
-    xe = jnp.stack([
-        jnp.concatenate([mine[:, :PART], stat], axis=1),
-        jnp.concatenate([mine[:, PART:], stat], axis=1),
-    ])
+    center = jnp.mean(widened, axis=-1)
+    spread = lax.rsqrt(jnp.mean(jnp.square(widened - center[:, None]), axis=-1) + 1e-05)
+    stat = jnp.pad(jnp.stack([center, spread]), ((0, 6), (0, 0)))
     depth = qkv_weight.shape[0]
     wq = jnp.pad(qkv_weight.T.reshape(16, 72, depth), ((0, 0), (0, 24), (0, 0)))
     wt = jnp.stack([wq, up_weight.T.reshape(16, 96, depth)], axis=1)
-    gain = lax.dynamic_slice_in_dim(jnp.stack(gains), core * HALF, HALF, 1)
-    gain = gain.reshape(4, 2, PART).transpose(1, 0, 2)
+    gain = jnp.stack(gains)
     bias = lax.dynamic_slice_in_dim(up_bias, req * 96, 96, 0)
     bias = jnp.broadcast_to(bias[:, None], (96, 128))
     vmem = pl.BlockSpec(memory_space=pltpu.VMEM)
@@ -447,10 +534,12 @@
             jax.ShapeDtypeStruct((1152, NEW), jnp.float32),
             jax.ShapeDtypeStruct((2, 96, 1024), jnp.bfloat16),
         ),
-        in_specs=[hbm, hbm, vmem, hbm],
+        in_specs=[hbm, hbm, hbm, vmem, hbm],
         out_specs=(vmem, vmem),
         scratch_shapes=[
-            pltpu.VMEM((2, 16, NEW, EXT), jnp.bfloat16),
+            pltpu.VMEM((2, 16, NEW, DIRECT + 256), jnp.bfloat16),
+            pltpu.VMEM((2, 3, 16, NEW, 256), jnp.bfloat16),
+            pltpu.VMEM((16, 8, NEW), jnp.float32),
             pltpu.VMEM((2, 2, 96, HALF), jnp.bfloat16),
             pltpu.VMEM((2, 512, PART), jnp.bfloat16),
             pltpu.VMEM((16, 384, NEW), jnp.float32),
@@ -458,14 +547,14 @@
             pltpu.VMEM((2, 96, NEW), jnp.float32),
             pltpu.VMEM((16, 72, NEW), jnp.float32),
             pltpu.VMEM((1152, NEW), jnp.float32),
-            dma((2,)), dma((2, 2, 16)), dma((2,)), dma, dma, dma,
-            dma((3,)), dma((2,)), dma, dma,
+            dma((2,)), dma((2, 2, 16)), dma((2, 5)), dma((2,)), dma((2, 2, 4, 4)), dma, dma,
+            dma, dma, dma, dma((3,)), dma((2,)), dma, dma,
         ],
         compiler_params=pltpu.CompilerParams(
             collective_id=0, has_side_effects=True, vmem_limit_bytes=VMEM_LIMIT
         ),
         name="front",
-    )(xe, wt, gain, bias)
+    )(hidden, stat, wt, gain, bias)
 
 
 def back_kernel(

time: 268 us -> 238 us (0.89)
  Pallas kernels: 246 us -> 219 us
  local copies, waits for them, and re-layouts: 12.1 us -> 9.36 us
    pallas_call x1, Pallas kernels: 139 us -> 113 us  [front(): pl.pallas_call(front_kernel, out_shape=(jax.ShapeDtypeStruct((1152, NEW),...]
    pallas_call x1, Pallas kernels: 103 us -> 94.2 us  [back(): pl.pallas_call(back_kernel, out_shape=jax.ShapeDtypeStruct((NEW, 2 * HALF...]
    pallas_call x1, Pallas kernels: 4.8 us -> 12.5 us  [attention(): pl.pallas_call(functools.partial(attention_kernel, heads), out_shape=(out...]
where the time goes in v4:
time: 238 us; the launch traced here: 237 us
  Pallas kernels  219 us (92%)
  local copies, waits for them, and re-layouts  9.36 us (4%)
  other arithmetic  6.97 us (3%)
    pallas_call x1, Pallas kernels, front(): pl.pallas_call(front_kernel, out_shape=(jax.ShapeDtypeStruct((1152, NEW),...  113 us
    pallas_call x1, Pallas kernels, back(): pl.pallas_call(back_kernel, out_shape=jax.ShapeDtypeStruct((NEW, 2 * HALF...  94.2 us
    pallas_call x1, Pallas kernels, attention(): pl.pallas_call(functools.partial(attention_kernel, heads), out_shape=(out...  12.5 us

profile of v4, /device:TPU:1, one launch (start us, length us, event | category | flops | bytes accessed | tf_op | source)
XLA Modules:
  0.0 237.3 jit_solution(1306960795307226998)
XLA Ops:
  0.6 0.0 copy-start
  0.7 1.8 convert_reduce_fusion
  2.5 0.0 copy-done
  2.5 0.6 fusion.1
  3.1 0.6 select_maximum_fusion.stat_ref
  3.7 0.7 copy.22
  4.5 0.9 copy.21
  5.3 0.1 pad_bitcast_fusion
  5.5 0.0 copy-start.3
  5.5 1.7 pad_maximum_fusion.wt_ref
  7.2 0.7 pad_maximum_fusion.1.gain_ref
  7.9 0.8 dynamic_slice.9
  8.7 0.7 broadcast_in_dim.10.ub_ref
  9.4 112.8 %front.1 = (f32[1152,128]{1,0:T(8,128)}, bf16[2,96,1024]{2,1,0:T(8,128)(2,1)}) custom-call(bf16[128,6144]{1,0:T(8,128)(2,1)} %hid_ref.1, f32[8,128]{1,0:T(8,128)} %select_maximum_fusion.stat_ref, bf16[16,2,96,384]{3,2,1,0:T(8,128)(2,1)} %pad_maximum_fusion.wt_ref, f32[4,6144]{1,0:T(4,128)} %pad_maximum_fusion.1.gain_ref, f32[96,128]{1,0:T(8,128)} %broadcast_in_dim.10.ub_ref), custom_call_target="tpu_custom_call" | custom-call | tf_op jit(solution)/shard_map/front/pallas_call | solution.py:531
  122.8 1.0 broadcast_in_dim.26.bias_ref
  123.9 0.1 fusion.2
  124.0 0.6 pad_maximum_fusion.2
  124.6 12.5 %attention.1 = (bf16[128,384]{1,0:T(8,128)(2,1)}, bf16[128,384]{1,0:T(8,128)(2,1)}, bf16[128,384]{1,0:T(8,128)(2,1)}) custom-call(s32[1]{0:T(128)S(6)} %copy.29.len_ref, f32[1152,128]{1,0:T(8,128)} %get-tuple-element.9.qkv_ref, f32[1152,1]{1,0:T(8,128)} %broadcast_in_dim.26.bias_ref, f32[24,128]{1,0:T(8,128)} %get-tuple-element.18.cos_ref, ...), custom_call_target="tpu_custom_call" | custom-call | tf_op jit(solution)/shard_map/attention/pallas_call | solution.py:115
  137.2 1.0 constant_dynamic-slice_fusion
  138.2 0.8 copy.27
  139.0 0.8 dynamic-slice_add_fusion
  139.8 0.6 broadcast_in_dim.23.bias_ref
  140.4 94.2 %back.1 = bf16[128,6144]{1,0:T(8,128)(2,1)} custom-call(bf16[2,96,1024]{2,1,0:T(8,128)(2,1)} %get-tuple-element.8.units_ref, bf16[128,384]{1,0:T(8,128)(2,1)} %get-tuple-element.10.att_ref, bf16[1536,384]{1,0:T(8,128)(2,1)} %wd_ref.1, bf16[384,384]{1,0:T(8,128)(2,1)} %wo_ref.1, bf16[16,32,384]{2,1,0:T(8,128)(2,1)} %bitcast.30, ...), custom_call_target="tpu_custom_call" | custom-call | tf_op jit(solution)/shard_map/back/pallas_call | solution.py:783
  234.6 2.7 %copy.30 = bf16[128,6144]{1,0:T(8,128)(2,1)} copy(bf16[128,6144]{1,0:T(8,128)(2,1)} %back.1) | data formatting | bytes 3145728
  (17 shorter events, 0.1 us)
Async XLA Ops:
  0.6 1.9 copy-start
  0.6 3.1 %copy-start.1 = (bf16[384,1536]{1,0:T(8,128)(2,1)S(1)}, bf16[384,1536]{1,0:T(8,128)(2,1)}, u32[]{:S(2)}) copy-start(bf16[384,1536]{1,0:T(8,128)(2,1)} %param.25) | copy-start | bytes 3538948
  3.1 1.4 copy-start.2
  5.5 1.7 copy-start.3
  5.5 1.7 copy-start.4
  5.5 1.7 copy-start.5
  5.5 1.7 copy-start.6
  9.4 113.4 %copy-start.7 = (f32[1152]{0:T(1024)S(1)}, f32[1152]{0:T(1024)}, u32[]{:S(2)}) copy-start(f32[1152]{0:T(1024)} %param.22) | copy-start | bytes 13828

commit v5 on v4

--- a/solution.py
+++ b/solution.py
@@ -26,25 +26,15 @@
     return jnp.concatenate([cosine, cosine], 0), jnp.concatenate([-sine, sine], 0)
 
 
-def attention_kernel(
-    heads, len_ref, qkv_ref, bias_ref, cos_ref, sin_ref, k_hbm, v_hbm,
-    att_ref, nk_ref, nv_ref, kbuf, vbuf, sbuf, qexp, ksem, vsem,
-):
+def fetch(n, hbm, buf, sem):
+    rows = pl.ds(pl.multiple_of(n * KB, KB), KB)
+    return pltpu.make_async_copy(hbm.at[rows], buf.at[rows], sem.at[n])
+
+
+def attention_scores(heads, length, qkv_ref, bias_ref, cos_ref, sin_ref, nk_ref, nv_ref, keep, key_block):
     scale = 1.0 / math.sqrt(DH)
-    length = len_ref[0]
     width = heads * DH
-    blocks = CACHE // KB
-    used = (length + KB - 1) // KB
-
-    def fetch(i, hbm, buf, sem):
-        rows = pl.ds(pl.multiple_of(i * KB, KB), KB)
-        return pltpu.make_async_copy(hbm.at[rows], buf.at[rows], sem.at[i])
-
-    for hbm, buf, sem in ((k_hbm, kbuf, ksem), (v_hbm, vbuf, vsem)):
-        @pl.loop(0, used)
-        def _(i):
-            fetch(i, hbm, buf, sem).start()
-
+    vkeep, qexp, sbuf = keep
     cosine, sine = cos_ref[...], sin_ref[...]
 
     def turned(rows):
@@ -61,6 +51,7 @@
     values = jnp.concatenate([block(j, 2) for j in range(heads)], 0).T.astype(jnp.bfloat16)
     nk_ref[...] = keys
     nv_ref[...] = values
+    vkeep[...] = values
     lane_head = lax.broadcasted_iota(jnp.int32, (NEW, width), 1) // DH
     for j in range(heads):
         qexp[pl.ds(j * NEW, NEW), :] = jnp.where(lane_head == j, queries, jnp.zeros_like(queries))
@@ -69,35 +60,43 @@
     row_at = lax.broadcasted_iota(jnp.int32, (rows, NEW), 0) % NEW
     col_at = lax.broadcasted_iota(jnp.int32, (rows, NEW), 1)
     fresh = jnp.where(col_at <= row_at, fresh, -1e30)
-
-    def score(i, top):
-        fetch(i, k_hbm, kbuf, ksem).wait()
-        at = pl.ds(pl.multiple_of(i * KB, KB), KB)
-        part = lax.dot_general(qexp[...], kbuf[at, :], NT, preferred_element_type=jnp.float32) * scale
-        col = lax.broadcasted_iota(jnp.int32, (rows, KB), 1) + i * KB
+    sbuf[:, CACHE:] = fresh
+
+    def score(n, top):
+        at = pl.ds(pl.multiple_of(n * KB, KB), KB)
+        part = lax.dot_general(
+            qexp[...], key_block(n, at), NT, preferred_element_type=jnp.float32) * scale
+        col = lax.broadcasted_iota(jnp.int32, (rows, KB), 1) + n * KB
         part = jnp.where(col < length, part, -1e30)
         sbuf[:, at] = part
         for t in range(KB // NEW):
             top = jnp.maximum(top, part[:, t * NEW:(t + 1) * NEW])
         return top
 
-    top = lax.fori_loop(0, used, score, fresh)
+    return lax.fori_loop(0, CACHE // KB, score, fresh)
+
+
+def attention_mix(heads, top, keep, att_ref, value_block):
+    width = heads * DH
+    vkeep, _, sbuf = keep
     highest = jnp.max(top, axis=1, keepdims=True)
-    fresh_weights = jnp.exp(fresh - highest)
-    mixed = jnp.dot(fresh_weights.astype(jnp.bfloat16), values, preferred_element_type=jnp.float32)
-
-    def weigh(i, carry):
+    fresh_weights = jnp.exp(sbuf[:, CACHE:] - highest)
+    mixed = jnp.dot(
+        fresh_weights.astype(jnp.bfloat16), vkeep[...], preferred_element_type=jnp.float32)
+
+    def weigh(n, carry):
         mixed, total = carry
-        fetch(i, v_hbm, vbuf, vsem).wait()
-        at = pl.ds(pl.multiple_of(i * KB, KB), KB)
+        at = pl.ds(pl.multiple_of(n * KB, KB), KB)
         weights = jnp.exp(sbuf[:, at] - highest)
         for t in range(KB // NEW):
             total = total + weights[:, t * NEW:(t + 1) * NEW]
-        mixed = mixed + jnp.dot(weights.astype(jnp.bfloat16), vbuf[at, :], preferred_element_type=jnp.float32)
+        mixed = mixed + jnp.dot(
+            weights.astype(jnp.bfloat16), value_block(n, at), preferred_element_type=jnp.float32)
         return mixed, total
 
-    mixed, total = lax.fori_loop(0, used, weigh, (mixed, fresh_weights))
+    mixed, total = lax.fori_loop(0, CACHE // KB, weigh, (mixed, fresh_weights))
     total = jnp.sum(total, axis=1, keepdims=True)
+    lane_head = lax.broadcasted_iota(jnp.int32, (NEW, width), 1) // DH
     out = jnp.zeros((NEW, width), jnp.float32)
     for j in range(heads):
         at = slice(j * NEW, (j + 1) * NEW)
@@ -105,36 +104,12 @@
     att_ref[...] = out.astype(jnp.bfloat16)
 
 
-def attention(qkv_t, bias, length, keys_old, values_old):
-    heads = qkv_t.shape[0] // (3 * DH)
-    width = heads * DH
-    cosine, sine = rotation_tables(length[0])
-    vmem = pl.BlockSpec(memory_space=pltpu.VMEM)
-    hbm = pl.BlockSpec(memory_space=pl.ANY)
-    out = jax.ShapeDtypeStruct((NEW, width), jnp.bfloat16)
-    return pl.pallas_call(
-        functools.partial(attention_kernel, heads),
-        out_shape=(out, out, out),
-        in_specs=[pl.BlockSpec(memory_space=pltpu.SMEM), vmem, vmem, vmem, vmem, hbm, hbm],
-        out_specs=(vmem, vmem, vmem),
-        scratch_shapes=[
-            pltpu.VMEM((CACHE, width), jnp.bfloat16),
-            pltpu.VMEM((CACHE, width), jnp.bfloat16),
-            pltpu.VMEM((heads * NEW, CACHE), jnp.float32),
-            pltpu.VMEM((heads * NEW, width), jnp.bfloat16),
-            pltpu.SemaphoreType.DMA((CACHE // KB,)),
-            pltpu.SemaphoreType.DMA((CACHE // KB,)),
-        ],
-        compiler_params=pltpu.CompilerParams(vmem_limit_bytes=60 * 2**20),
-        name="attention",
-    )(length, qkv_t, bias[:, None], cosine, sine, keys_old, values_old)
-
-
 MESH = pl.DeviceIdType.MESH
 SIDE = 4
 HALF = 3072
 PART = 1536
 DIRECT = 512
+HEADS_HERE = 4
 VMEM_LIMIT = 62 * 2**20
 
 
@@ -210,8 +185,7 @@
     dp = gray(i)
     for ds, half in FIRST:
         if (ds, half) == (2, 0):
-            @pl.when(i < 2)
-            def _():
+            if i < 2:
                 ring_spread(send, gray(i + 2))
         for colour in (0, 1):
             arrived(colour, dp, ds, half)
@@ -419,8 +393,7 @@
                 row = origin(colour, dp, ds)
                 pbuf[row, 192 * kind:192 * (kind + 1), :] += product[:, ds * NEW:(ds + 1) * NEW]
 
-    @pl.loop(0, SIDE)
-    def _(i):
+    for i in range(SIDE):
         ring_second(send, arrived, i)
         side_out(1, gray(i))
 
@@ -558,11 +531,16 @@
 
 
 def back_kernel(
-    units_ref, att_ref, wd_ref, wo_ref, rest_ref, bias_ref, out_ref,
+    len_ref, units_ref, qkv_ref, qbias_ref, cos_ref, sin_ref, k_hbm, v_hbm,
+    wd_ref, wo_ref, rest_ref, bias_ref, out_ref, nk_ref, nv_ref,
     ubuf, aring, amate, dbuf, obuf, dturn, total, tsend, rsum, share, rest, fout,
+    kbuf, vbuf, sbuf, qexp, vkeep, att_ref, ksem, vsem,
     usend_sem, urecv_sem, own_sem, asend_sem, arecv_sem, amate_sem, w_sem,
     hsend_sem, hrecv_sem, rsend_sem, rrecv_sem, fsend_sem, frecv_sem, gsend_sem, grecv_sem,
 ):
+    for hbm, buf, sem in ((k_hbm, kbuf, ksem), (v_hbm, vbuf, vsem)):
+        for n in range(CACHE // KB):
+            fetch(n, hbm, buf, sem).start()
     y, z, x, core = place()
     me = y * SIDE + z
     mate = 1 - core
@@ -588,7 +566,6 @@
         return att_ref.at[pl.ds(32 * (2 * colour + half), 32)]
 
     asend, aarrived = ring_units(y, z, x, core, aown, Absolute(y, z), apart, asend_sem, arecv_sem)
-    ring_start(asend)
 
     def lanes(colour, half):
         return pl.ds((2 * colour + half) * 256, 256)
@@ -601,10 +578,7 @@
 
     send, arrived = ring_units(y, z, x, core, own, Absolute(y, z), part, usend_sem, urecv_sem)
     ring_start(send)
-    copies = [
-        pltpu.make_async_copy(units_ref, ubuf.at[:, me], own_sem.at[0]),
-        pltpu.make_async_copy(att_ref, aring.at[me], own_sem.at[1]),
-    ]
+    copies = [pltpu.make_async_copy(units_ref, ubuf.at[:, me], own_sem.at[0])]
     for n, (src, dst) in enumerate(((wd_ref, dbuf), (wo_ref, obuf))):
         copies.append(pltpu.make_async_copy(src, dst.at[core], w_sem.at[3 * n]))
         copies.append(pltpu.make_async_remote_copy(
@@ -627,32 +601,51 @@
             ).start()
         pltpu.make_async_copy(rest_ref.at[me], rest.at[slot], hrecv_sem).start()
 
-    ring_first(asend, aarrived)
+    heads = HEADS_HERE
+    keep = (vkeep, qexp, sbuf)
+
+    def key_block(n, at):
+        fetch(n, k_hbm, kbuf, ksem).wait()
+        return kbuf[at, :]
+
+    def value_block(n, at):
+        fetch(n, v_hbm, vbuf, vsem).wait()
+        return vbuf[at, :]
+
+    top = attention_scores(
+        heads, len_ref[0], qkv_ref, qbias_ref, cos_ref, sin_ref, nk_ref, nv_ref, keep, key_block)
     ring_first(send, arrived)
-
-    @pl.loop(0, SIDE)
-    def _(i):
-        ring_second(asend, aarrived, i)
-
+    attention_mix(heads, top, keep, att_ref, value_block)
+    att_own = pltpu.make_async_copy(att_ref, aring.at[me], own_sem.at[1])
+    att_own.start()
+    ring_start(asend)
     for copy in copies:
         copy.wait()
+
+    def turn(first, count):
+        @pl.loop(first, first + count)
+        def _(n):
+            h, at = n // 12, pl.ds(pl.multiple_of((n % 12) * 128, 128), 128)
+            dturn[h, :, at] = dbuf[h, at, :].T
+
+    ring_second(send, arrived, 0)
+    turn(0, 12)
+    ring_first(asend, aarrived)
+    ring_second(send, arrived, 1)
+    turn(12, 12)
+    ring_second(asend, aarrived, 0)
+    ring_second(asend, aarrived, 1)
+    ring_second(send, arrived, 2)
+    ring_second(asend, aarrived, 2)
+    ring_second(asend, aarrived, 3)
+    att_own.wait()
     pair = pltpu.make_async_remote_copy(
         src_ref=aring.at[pl.ds(8 * mate, 8)], dst_ref=amate,
         send_sem=amate_sem.at[0], recv_sem=amate_sem.at[1],
         device_id=(me, 2 * x + mate), device_id_type=MESH,
     )
     pair.start()
-
-    @pl.loop(0, SIDE)
-    def _(i):
-        @pl.loop(0, 6)
-        def _(k):
-            n = 6 * i + k
-            h, at = n // 12, pl.ds(pl.multiple_of((n % 12) * 128, 128), 128)
-            dturn[h, :, at] = dbuf[h, at, :].T
-
-        ring_second(send, arrived, i)
-
+    ring_second(send, arrived, 3)
     pair.wait_recv()
 
     def rcopy(q, step):
@@ -717,10 +710,26 @@
         ]
 
     def gcopy(step):
-        to = lax.rem(x + step, SIDE)
+        to = lax.rem(x + step + SIDE, SIDE)
+        way = (1 - step) // 2
         return pltpu.make_async_remote_copy(
-            src_ref=piece(x, core), dst_ref=piece(x, core), send_sem=gsend_sem.at[0, step],
-            recv_sem=grecv_sem.at[0, step], device_id=(me, 2 * to + core), device_id_type=MESH,
+            src_ref=piece(x, core), dst_ref=piece(x, core), send_sem=gsend_sem.at[0, way],
+            recv_sem=grecv_sem.at[0, way], device_id=(me, 2 * to + core), device_id_type=MESH,
+        )
+
+    def strip(owner, way):
+        return fout.at[
+            pl.ds(pl.multiple_of(32 * owner + 16 * way, 16), 16),
+            pl.ds(pl.multiple_of(core * HALF, HALF), HALF),
+        ]
+
+    def grelay(step):
+        to = lax.rem(x + step + SIDE, SIDE)
+        owner = lax.rem(x - step + SIDE, SIDE)
+        way = (1 - step) // 2
+        return pltpu.make_async_remote_copy(
+            src_ref=strip(owner, way), dst_ref=strip(owner, way), send_sem=gsend_sem.at[0, 2 + way],
+            recv_sem=grecv_sem.at[0, 2 + way], device_id=(me, 2 * to + core), device_id_type=MESH,
         )
 
     def pass_on(step):
@@ -730,24 +739,31 @@
             recv_sem=grecv_sem.at[1, step], device_id=(me, 2 * x + mate), device_id_type=MESH,
         )
 
-    def landed(kind, step):
-        owner = lax.rem(x - step + SIDE, SIDE)
-        ref = piece(owner, core if kind == 0 else mate)
-        pltpu.make_async_copy(ref, ref, grecv_sem.at[kind, step]).wait()
+    def landed(kind, n, ref):
+        pltpu.make_async_copy(ref, ref, grecv_sem.at[kind, n]).wait()
+
+    def owner_at(step):
+        return lax.rem(x - step + SIDE, SIDE)
 
     pltpu.make_async_copy(piece(x, core), piece(x, core), frecv_sem).wait()
-    for step in (2, 1, 3):
+    for step in (1, -1):
         gcopy(step).start()
     pass_on(0).start()
-    for step in (1, 3, 2):
-        landed(0, step)
-        pass_on(step).start()
+    for step in (1, -1):
+        landed(0, (1 - step) // 2, piece(owner_at(step), core))
+        grelay(step).start()
+        pass_on(step % SIDE).start()
+    for way in (0, 1):
+        landed(0, 2 + way, strip(owner_at(2), way))
+    pass_on(2).start()
     for step in (0, 1, 3, 2):
-        landed(1, step)
+        landed(1, step, piece(owner_at(step), mate))
     out_ref[...] = fout[...]
 
+    for step in (1, -1):
+        gcopy(step).wait_send()
+        grelay(step).wait_send()
     for step in (1, 2, 3):
-        gcopy(step).wait_send()
         some = rsum.at[step - 1]
         pltpu.make_async_copy(some, some, rsend_sem.at[step - 1]).wait()
     for step in range(4):
@@ -772,7 +788,8 @@
         pltpu.make_async_copy(some, some, asend_sem.at[colour]).wait()
 
 
-def back(units, attended, hidden, out_weight, down_weight, bias_total):
+def back(units, qkv, qkv_bias, length, keys_old, values_old, hidden, out_weight, down_weight, bias_total):
+    cosine, sine = rotation_tables(length[0])
     req, x = lax.axis_index("req"), lax.axis_index("head") // 2
     rest = lax.dynamic_slice_in_dim(hidden, 32 * x, 32, 0)
     rest = rest.reshape(32, 16, 384).transpose(1, 0, 2)
@@ -782,9 +799,16 @@
     dma = pltpu.SemaphoreType.DMA
     return pl.pallas_call(
         back_kernel,
-        out_shape=jax.ShapeDtypeStruct((NEW, 2 * HALF), jnp.bfloat16),
-        in_specs=[hbm, hbm, hbm, hbm, hbm, vmem],
-        out_specs=vmem,
+        out_shape=(
+            jax.ShapeDtypeStruct((NEW, 2 * HALF), jnp.bfloat16),
+            jax.ShapeDtypeStruct((NEW, 384), jnp.bfloat16),
+            jax.ShapeDtypeStruct((NEW, 384), jnp.bfloat16),
+        ),
+        in_specs=[
+            pl.BlockSpec(memory_space=pltpu.SMEM), hbm, vmem, vmem, vmem, vmem, hbm, hbm,
+            hbm, hbm, hbm, vmem,
+        ],
+        out_specs=(vmem, vmem, vmem),
         scratch_shapes=[
             pltpu.VMEM((2, 16, 96, 1024), jnp.bfloat16),
             pltpu.VMEM((16, NEW, 384), jnp.bfloat16),
@@ -798,6 +822,13 @@
             pltpu.VMEM((8, 32, 384), jnp.bfloat16),
             pltpu.VMEM((8, 32, 384), jnp.bfloat16),
             pltpu.VMEM((NEW, 2 * HALF), jnp.bfloat16),
+            pltpu.VMEM((CACHE, 384), jnp.bfloat16),
+            pltpu.VMEM((CACHE, 384), jnp.bfloat16),
+            pltpu.VMEM((HEADS_HERE * NEW, CACHE + NEW), jnp.float32),
+            pltpu.VMEM((HEADS_HERE * NEW, 384), jnp.bfloat16),
+            pltpu.VMEM((NEW, 384), jnp.bfloat16),
+            pltpu.VMEM((NEW, 384), jnp.bfloat16),
+            dma((CACHE // KB,)), dma((CACHE // KB,)),
             dma((2,)), dma((2, 2, 16)), dma((2,)), dma((2,)), dma((2, 2, 16)), dma((2,)), dma((6,)),
             dma, dma, dma((3,)), dma((3,)), dma, dma, dma((2, 4)), dma((2, 4)),
         ],
@@ -805,7 +836,8 @@
             collective_id=1, has_side_effects=True, vmem_limit_bytes=VMEM_LIMIT
         ),
         name="back",
-    )(units, attended, down_weight, out_weight, rest, bias)
+    )(length, units, qkv, qkv_bias[:, None], cosine, sine, keys_old, values_old,
+      down_weight, out_weight, rest, bias)
 
 
 def body(
@@ -828,10 +860,10 @@
 ):
     gains = (attn_norm_gain, attn_norm_bias, mlp_norm_gain, mlp_norm_bias)
     qkv, units = front(hidden, gains, qkv_weight, up_weight, up_bias)
-    attended, key_rows, value_rows = attention(
-        qkv, qkv_bias, cached_len, cache_keys[0], cache_values[0]
+    result, key_rows, value_rows = back(
+        units, qkv, qkv_bias, cached_len, cache_keys[0], cache_values[0],
+        hidden, out_weight, down_weight, out_bias + down_bias,
     )
-    result = back(units, attended, hidden, out_weight, down_weight, out_bias + down_bias)
     return (result, key_rows[None], value_rows[None])
 
 

time: 238 us -> 235 us (0.987)
  Pallas kernels: 219 us -> 216 us
    pallas_call x2 -> x1, Pallas kernels: 107 us -> 103 us  [back(): pl.pallas_call(back_kernel, out_shape=(jax.ShapeDtypeStruct((NEW, 2 * HAL...]
where the time goes in v5:
time: 235 us
  Pallas kernels  216 us (92%)
  local copies, waits for them, and re-layouts  10.7 us (5%)
  other arithmetic  6.92 us (3%)
    pallas_call x1, Pallas kernels, front(): pl.pallas_call(front_kernel, out_shape=(jax.ShapeDtypeStruct((1152, NEW),...  113 us
    pallas_call x1, Pallas kernels, back(): pl.pallas_call(back_kernel, out_shape=(jax.ShapeDtypeStruct((NEW, 2 * HAL...  103 us

profile of v5, /device:TPU:1, one launch (start us, length us, event | category | flops | bytes accessed | tf_op | source)
XLA Modules:
  0.0 235.0 jit_solution(14697680760830979397)
XLA Ops:
  1.4 1.8 convert_reduce_fusion
  3.2 0.6 fusion.1
  3.8 0.6 select_maximum_fusion.stat_ref
  4.4 0.7 copy.22
  5.2 0.9 copy.21
  6.0 0.1 pad_bitcast_fusion
  6.2 0.0 copy-start.5
  6.2 0.0 copy-start.6
  6.2 1.7 pad_maximum_fusion.wt_ref
  7.9 0.7 pad_maximum_fusion.1.gain_ref
  8.6 0.8 dynamic_slice.9
  9.4 0.7 broadcast_in_dim.10.ub_ref
  10.1 112.8 %front.1 = (f32[1152,128]{1,0:T(8,128)}, bf16[2,96,1024]{2,1,0:T(8,128)(2,1)}) custom-call(bf16[128,6144]{1,0:T(8,128)(2,1)} %hid_ref.1, f32[8,128]{1,0:T(8,128)} %select_maximum_fusion.stat_ref, bf16[16,2,96,384]{3,2,1,0:T(8,128)(2,1)} %pad_maximum_fusion.wt_ref, f32[4,6144]{1,0:T(4,128)} %pad_maximum_fusion.1.gain_ref, f32[96,128]{1,0:T(8,128)} %broadcast_in_dim.10.ub_ref), custom_call_target="tpu_custom_call" | custom-call | tf_op jit(solution)/shard_map/front/pallas_call | solution.py:504
  122.9 1.0 broadcast_in_dim.26.qbias_ref
  124.0 0.1 fusion.2
  124.1 0.6 pad_maximum_fusion.2
  124.7 1.0 constant_dynamic-slice_fusion
  125.7 0.8 copy.27
  126.5 0.8 dynamic-slice_add_fusion
  127.3 0.6 broadcast_in_dim.23.bias_ref
  127.9 103.1 %back.1 = (bf16[128,6144]{1,0:T(8,128)(2,1)}, bf16[128,384]{1,0:T(8,128)(2,1)}, bf16[128,384]{1,0:T(8,128)(2,1)}) custom-call(s32[1]{0:T(128)S(6)} %copy.31.len_ref, bf16[2,96,1024]{2,1,0:T(8,128)(2,1)} %get-tuple-element.8.units_ref, f32[1152,128]{1,0:T(8,128)} %get-tuple-element.9.qkv_ref, f32[1152,1]{1,0:T(8,128)} %broadcast_in_dim.26.qbias_ref, ...), custom_call_target="tpu_custom_call" | custom-call | tf_op jit(solution)/shard_map/back/pallas_call | solution.py:800
  231.0 2.7 %copy.32 = bf16[128,6144]{1,0:T(8,128)(2,1)} copy(bf16[128,6144]{1,0:T(8,128)(2,1)} %get-tuple-element.23) | data formatting | bytes 3145728
  233.7 0.6 copy.33
  234.4 0.6 copy.34
  (22 shorter events, 0.1 us)
Async XLA Ops:
  0.6 2.6 %copy-start = (bf16[128,6144]{1,0:T(8,128)(2,1)S(1)}, bf16[128,6144]{1,0:T(8,128)(2,1)}, u32[]{:S(2)}) copy-start(bf16[128,6144]{1,0:T(8,128)(2,1)} %hid_ref.1) | copy-start | bytes 4718596
  1.4 3.0 %copy-start.1 = (bf16[384,1536]{1,0:T(8,128)(2,1)S(1)}, bf16[384,1536]{1,0:T(8,128)(2,1)}, u32[]{:S(2)}) copy-start(bf16[384,1536]{1,0:T(8,128)(2,1)} %param.25) | copy-start | bytes 3538948
  3.8 1.4 copy-start.2
  6.2 1.7 copy-start.5
  6.2 1.7 copy-start.6
  6.2 1.7 copy-start.7
  6.2 1.7 copy-start.8
  10.1 112.8 %copy-start.9 = (f32[1152]{0:T(1024)S(1)}, f32[1152]{0:T(1024)}, u32[]{:S(2)}) copy-start(f32[1152]{0:T(1024)} %param.22) | copy-start | bytes 13828
  231.0 2.8 %copy-start.4 = (bf16[128,384]{1,0:T(8,128)(2,1)S(1)}, bf16[128,384]{1,0:T(8,128)(2,1)}, u32[]{:S(2)}) copy-start(bf16[128,384]{1,0:T(8,128)(2,1)} %get-tuple-element.11) | copy-start | bytes 294916
  231.0 3.4 %copy-start.3 = (bf16[128,384]{1,0:T(8,128)(2,1)S(1)}, bf16[128,384]{1,0:T(8,128)(2,1)}, u32[]{:S(2)}) copy-start(bf16[128,384]{1,0:T(8,128)(2,1)} %get-tuple-element.12) | copy-start | bytes 294916

commit v6 on v5

--- a/solution.py
+++ b/solution.py
@@ -42,9 +42,11 @@
         swapped = jnp.concatenate([low[ROT // 2:], low[: ROT // 2]], axis=0)
         return jnp.concatenate([low * cosine + swapped * sine, rows[ROT:]], axis=0)
 
+    bias = jnp.broadcast_to(bias_ref[...], (8, 3 * width)).T
+
     def block(j, part):
-        at = pl.ds((3 * j + part) * DH, DH)
-        return qkv_ref[at, :] + bias_ref[at, :]
+        first = (3 * j + part) * DH
+        return qkv_ref[pl.ds(first, DH), :] + bias[first:first + DH, 0:1]
 
     queries = jnp.concatenate([turned(block(j, 0)) for j in range(heads)], 0).T.astype(jnp.bfloat16)
     keys = jnp.concatenate([turned(block(j, 1)) for j in range(heads)], 0).T.astype(jnp.bfloat16)
@@ -171,20 +173,23 @@
                 send(colour, dp, 0, half, 1, step).start()
 
 
-def ring_first(send, arrived):
+def ring_first(send, arrived, eager=False):
     for dp, half in FIRST:
-        if (dp, half) == (2, 0):
+        if (dp, half) == (2, 0) and not eager:
             ring_spread(send, 1)
         for colour in (0, 1):
             arrived(colour, dp, 0, half)
             if (dp, half) in ((1, 0), (3, 1)):
                 send(colour, dp, 0, half, 0, 1 if dp == 1 else -1).start()
-
-
-def ring_second(send, arrived, i):
+            if eager:
+                for step in (1, -1):
+                    send(colour, dp, 0, half, 1, step).start()
+
+
+def ring_second(send, arrived, i, eager=False):
     dp = gray(i)
     for ds, half in FIRST:
-        if (ds, half) == (2, 0):
+        if (ds, half) == (2, 0) and not eager:
             if i < 2:
                 ring_spread(send, gray(i + 2))
         for colour in (0, 1):
@@ -360,34 +365,43 @@
         dz = colour * ds + (1 - colour) * dp
         return lax.rem(y - dy + SIDE, SIDE) * SIDE + lax.rem(z - dz + SIDE, SIDE)
 
-    def compute(colour, dp):
+    def norm(colour, dp, pieces):
+        base = core * HALF + colour * PART
+
         @pl.loop(0, SIDE)
         def _(ds):
-            s = dp * SIDE + ds
             turned = stats[origin(colour, dp, ds)].T
             center, spread = turned[:, 0:1], turned[:, 1:2]
             rows = pl.ds(pl.multiple_of(ds * NEW, NEW), NEW)
-            base = core * HALF + colour * PART
-
-            def norm(raw, lane, width):
+            for raw, lane, width in pieces(colour, dp * SIDE + ds):
                 value = (raw.astype(jnp.float32) - center) * spread
                 at = pl.ds(pl.multiple_of(base + lane, 256), width)
                 to = pl.ds(pl.multiple_of(lane, 256), width)
                 for kind in (0, 1):
-                    nbuf[kind, rows, to] = (
+                    nbuf[colour, dp, kind, rows, to] = (
                         value * gain_ref[2 * kind:2 * kind + 1, at]
                         + gain_ref[2 * kind + 1:2 * kind + 2, at]
                     ).astype(jnp.bfloat16)
 
-            norm(xbuf[colour, s, :, 0:DIRECT], 0, DIRECT)
-            norm(xbuf[colour, s, :, DIRECT:DIRECT + 256], DIRECT + 256 * x, 256)
-            for dx in (1, 2, 3):
-                norm(sbuf[colour, dx - 1, s], DIRECT + 256 * lax.rem(x - dx + SIDE, SIDE), 256)
-
+    def side_lane(dx):
+        return DIRECT + 256 * lax.rem(x - dx + SIDE, SIDE)
+
+    def early(colour, s):
+        yield xbuf[colour, s, :, 0:DIRECT], 0, DIRECT
+        yield xbuf[colour, s, :, DIRECT:DIRECT + 256], DIRECT + 256 * x, 256
+        for dx in (1, 3):
+            yield sbuf[colour, dx - 1, s], side_lane(dx), 256
+
+    def late(colour, s):
+        yield sbuf[colour, 1, s], side_lane(2), 256
+
+    def compute(colour, dp):
+        norm(colour, dp, late)
         for kind in (0, 1):
             left = wbuf[kind, :, :, pl.ds(pl.multiple_of(colour * PART, PART), PART)]
             product = lax.dot_general(
-                left.reshape(192, PART), nbuf[kind], NT, preferred_element_type=jnp.float32
+                left.reshape(192, PART), nbuf[colour, dp, kind], NT,
+                preferred_element_type=jnp.float32,
             )
             for ds in range(SIDE):
                 row = origin(colour, dp, ds)
@@ -398,6 +412,7 @@
         side_out(1, gray(i))
 
     weights_out(1, 15)
+    pltpu.make_async_copy(stats, stats, stat_recv).wait()
     for dp in (1, 3, 2):
         side_on(0, dp)
 
@@ -405,7 +420,10 @@
     def _(i):
         side_on(1, gray(i))
 
-    pltpu.make_async_copy(stats, stats, stat_recv).wait()
+        @pl.loop(0, 2)
+        def _(colour):
+            norm(colour, gray(i), early)
+
     pltpu.make_async_copy(wbuf, wbuf, wrecv_sem).wait()
 
     @pl.loop(0, SIDE)
@@ -514,7 +532,7 @@
             pltpu.VMEM((2, 3, 16, NEW, 256), jnp.bfloat16),
             pltpu.VMEM((16, 8, NEW), jnp.float32),
             pltpu.VMEM((2, 2, 96, HALF), jnp.bfloat16),
-            pltpu.VMEM((2, 512, PART), jnp.bfloat16),
+            pltpu.VMEM((2, SIDE, 2, 512, PART), jnp.bfloat16),
             pltpu.VMEM((16, 384, NEW), jnp.float32),
             pltpu.VMEM((8, 384, NEW), jnp.float32),
             pltpu.VMEM((2, 96, NEW), jnp.float32),
@@ -589,17 +607,22 @@
         copy.start()
     slot = me % 8
 
+    def tile(row):
+        return rest_ref.at[
+            pl.ds(pl.multiple_of(32 * x, 32), 32), pl.ds(pl.multiple_of(384 * row, 384), 384)
+        ]
+
     @pl.when(goal == core)
     def _():
         @pl.loop(1, 16)
         def _(i):
             row = lax.rem(y + i // SIDE, SIDE) * SIDE + lax.rem(z + i % SIDE, SIDE)
             pltpu.make_async_remote_copy(
-                src_ref=rest_ref.at[row], dst_ref=rest.at[slot],
+                src_ref=tile(row), dst_ref=rest.at[slot],
                 send_sem=hsend_sem, recv_sem=hrecv_sem,
                 device_id=(row, 2 * x + core), device_id_type=MESH,
             ).start()
-        pltpu.make_async_copy(rest_ref.at[me], rest.at[slot], hrecv_sem).start()
+        pltpu.make_async_copy(tile(me), rest.at[slot], hrecv_sem).start()
 
     heads = HEADS_HERE
     keep = (vkeep, qexp, sbuf)
@@ -614,7 +637,7 @@
 
     top = attention_scores(
         heads, len_ref[0], qkv_ref, qbias_ref, cos_ref, sin_ref, nk_ref, nv_ref, keep, key_block)
-    ring_first(send, arrived)
+    ring_first(send, arrived, True)
     attention_mix(heads, top, keep, att_ref, value_block)
     att_own = pltpu.make_async_copy(att_ref, aring.at[me], own_sem.at[1])
     att_own.start()
@@ -628,16 +651,17 @@
             h, at = n // 12, pl.ds(pl.multiple_of((n % 12) * 128, 128), 128)
             dturn[h, :, at] = dbuf[h, at, :].T
 
-    ring_second(send, arrived, 0)
+    ring_second(send, arrived, 0, True)
     turn(0, 12)
-    ring_first(asend, aarrived)
-    ring_second(send, arrived, 1)
+    ring_second(send, arrived, 1, True)
     turn(12, 12)
-    ring_second(asend, aarrived, 0)
-    ring_second(asend, aarrived, 1)
-    ring_second(send, arrived, 2)
-    ring_second(asend, aarrived, 2)
-    ring_second(asend, aarrived, 3)
+    ring_first(asend, aarrived, True)
+    ring_second(send, arrived, 2, True)
+    ring_second(asend, aarrived, 0, True)
+    ring_second(asend, aarrived, 1, True)
+    ring_second(send, arrived, 3, True)
+    ring_second(asend, aarrived, 2, True)
+    ring_second(asend, aarrived, 3, True)
     att_own.wait()
     pair = pltpu.make_async_remote_copy(
         src_ref=aring.at[pl.ds(8 * mate, 8)], dst_ref=amate,
@@ -645,7 +669,6 @@
         device_id=(me, 2 * x + mate), device_id_type=MESH,
     )
     pair.start()
-    ring_second(send, arrived, 3)
     pair.wait_recv()
 
     def rcopy(q, step):
@@ -774,7 +797,7 @@
     def _():
         some = share.at[pl.ds(0, 7)]
         pltpu.make_async_copy(some, some, fsend_sem).wait()
-        some = rest_ref.at[pl.ds(0, 15)]
+        some = rest_ref.at[pl.ds(0, 32), pl.ds(0, 15 * 384)]
         pltpu.make_async_copy(some, some, hsend_sem).wait()
 
     @pl.when(goal != core)
@@ -790,9 +813,7 @@
 
 def back(units, qkv, qkv_bias, length, keys_old, values_old, hidden, out_weight, down_weight, bias_total):
     cosine, sine = rotation_tables(length[0])
-    req, x = lax.axis_index("req"), lax.axis_index("head") // 2
-    rest = lax.dynamic_slice_in_dim(hidden, 32 * x, 32, 0)
-    rest = rest.reshape(32, 16, 384).transpose(1, 0, 2)
+    req = lax.axis_index("req")
     bias = lax.dynamic_slice_in_dim(bias_total, req * 384, 384, 0)[None, :]
     vmem = pl.BlockSpec(memory_space=pltpu.VMEM)
     hbm = pl.BlockSpec(memory_space=pl.ANY)
@@ -836,8 +857,8 @@
             collective_id=1, has_side_effects=True, vmem_limit_bytes=VMEM_LIMIT
         ),
         name="back",
-    )(length, units, qkv, qkv_bias[:, None], cosine, sine, keys_old, values_old,
-      down_weight, out_weight, rest, bias)
+    )(length, units, qkv, qkv_bias[None, :], cosine, sine, keys_old, values_old,
+      down_weight, out_weight, hidden, bias)
 
 
 def body(

time: 235 us -> 232 us (0.987)
    pallas_call x1, Pallas kernels: 113 us -> 108 us  [front(): pl.pallas_call(front_kernel, out_shape=(jax.ShapeDtypeStruct((1152, NEW),...]
    pallas_call x1, Pallas kernels: 103 us -> 107 us  [back(): pl.pallas_call(back_kernel, out_shape=(jax.ShapeDtypeStruct((NEW, 2 * HAL...]
where the time goes in v6:
time: 232 us
  Pallas kernels  215 us (93%)
  local copies, waits for them, and re-layouts  8.42 us (4%)
  other arithmetic  6.92 us (3%)
    pallas_call x1, Pallas kernels, front(): pl.pallas_call(front_kernel, out_shape=(jax.ShapeDtypeStruct((1152, NEW),...  108 us
    pallas_call x1, Pallas kernels, back(): pl.pallas_call(back_kernel, out_shape=(jax.ShapeDtypeStruct((NEW, 2 * HAL...  107 us

profile of v6, /device:TPU:1, one launch (start us, length us, event | category | flops | bytes accessed | tf_op | source)
XLA Modules:
  0.0 231.7 jit_solution(4069046342873324371)
XLA Ops:
  0.6 0.0 copy-start
  1.4 1.8 convert_reduce_fusion
  3.2 0.6 fusion.1
  3.8 0.6 select_maximum_fusion.stat_ref
  4.4 0.7 copy.20
  5.2 0.9 copy.19
  6.0 0.1 pad_bitcast_fusion
  6.2 0.0 copy-start.5
  6.2 0.0 copy-start.6
  6.2 0.0 copy-start.7
  6.2 1.7 pad_maximum_fusion.wt_ref
  7.9 0.7 pad_maximum_fusion.1.gain_ref
  8.6 0.8 dynamic_slice.6
  9.4 0.7 broadcast_in_dim.10.ub_ref
  10.1 107.6 %front.1 = (f32[1152,128]{1,0:T(8,128)}, bf16[2,96,1024]{2,1,0:T(8,128)(2,1)}) custom-call(bf16[128,6144]{1,0:T(8,128)(2,1)} %rest_ref.1, f32[8,128]{1,0:T(8,128)} %select_maximum_fusion.stat_ref, bf16[16,2,96,384]{3,2,1,0:T(8,128)(2,1)} %pad_maximum_fusion.wt_ref, f32[4,6144]{1,0:T(4,128)} %pad_maximum_fusion.1.gain_ref, f32[96,128]{1,0:T(8,128)} %broadcast_in_dim.10.ub_ref), custom_call_target="tpu_custom_call" | custom-call | tf_op jit(solution)/shard_map/front/pallas_call | solution.py:522
  117.7 0.6 broadcast_in_dim.22.qbias_ref
  118.4 0.1 fusion.2
  118.5 0.6 pad_maximum_fusion.2
  119.1 0.8 dynamic-slice_add_fusion
  119.9 0.6 broadcast_in_dim.23.bias_ref
  120.5 107.2 %back.1 = (bf16[128,6144]{1,0:T(8,128)(2,1)}, bf16[128,384]{1,0:T(8,128)(2,1)}, bf16[128,384]{1,0:T(8,128)(2,1)}) custom-call(s32[1]{0:T(128)S(6)} %copy.24.len_ref, bf16[2,96,1024]{2,1,0:T(8,128)(2,1)} %get-tuple-element.8.units_ref, f32[1152,128]{1,0:T(8,128)} %get-tuple-element.9.qkv_ref, f32[1,1152]{1,0:T(1,128)} %broadcast_in_dim.22.qbias_ref, ...), custom_call_target="tpu_custom_call" | custom-call | tf_op jit(solution)/shard_map/back/pallas_call | solution.py:821
  227.7 2.7 %copy.25 = bf16[128,6144]{1,0:T(8,128)(2,1)} copy(bf16[128,6144]{1,0:T(8,128)(2,1)} %get-tuple-element.23) | data formatting | bytes 3145728
  230.4 0.6 copy.26
  231.0 0.6 copy.27
  (20 shorter events, 0.1 us)
Async XLA Ops:
  0.6 2.6 %copy-start = (bf16[128,6144]{1,0:T(8,128)(2,1)S(1)}, bf16[128,6144]{1,0:T(8,128)(2,1)}, u32[]{:S(2)}) copy-start(bf16[128,6144]{1,0:T(8,128)(2,1)} %rest_ref.1) | copy-start | bytes 4718596
  1.4 3.0 %copy-start.1 = (bf16[384,1536]{1,0:T(8,128)(2,1)S(1)}, bf16[384,1536]{1,0:T(8,128)(2,1)}, u32[]{:S(2)}) copy-start(bf16[384,1536]{1,0:T(8,128)(2,1)} %param.25) | copy-start | bytes 3538948
  3.8 1.4 copy-start.2
  6.2 1.7 copy-start.5
  6.2 1.7 copy-start.6
  6.2 1.7 copy-start.7
  6.2 1.7 copy-start.8
  10.1 107.6 %copy-start.9 = (f32[1152]{0:T(1024)S(1)}, f32[1152]{0:T(1024)}, u32[]{:S(2)}) copy-start(f32[1152]{0:T(1024)} %param.22) | copy-start | bytes 13828
  227.6 2.8 %copy-start.4 = (bf16[128,384]{1,0:T(8,128)(2,1)S(1)}, bf16[128,384]{1,0:T(8,128)(2,1)}, u32[]{:S(2)}) copy-start(bf16[128,384]{1,0:T(8,128)(2,1)} %get-tuple-element.11) | copy-start | bytes 294916
  227.6 3.4 %copy-start.3 = (bf16[128,384]{1,0:T(8,128)(2,1)S(1)}, bf16[128,384]{1,0:T(8,128)(2,1)}, u32[]{:S(2)}) copy-start(bf16[128,384]{1,0:T(8,128)(2,1)} %get-tuple-element.12) | copy-start | bytes 294916

commit v7 on v6

--- a/solution.py
+++ b/solution.py
@@ -173,31 +173,50 @@
                 send(colour, dp, 0, half, 1, step).start()
 
 
-def ring_first(send, arrived, eager=False):
+def ring_first(send, arrived):
     for dp, half in FIRST:
-        if (dp, half) == (2, 0) and not eager:
+        if (dp, half) == (2, 0):
             ring_spread(send, 1)
         for colour in (0, 1):
             arrived(colour, dp, 0, half)
             if (dp, half) in ((1, 0), (3, 1)):
                 send(colour, dp, 0, half, 0, 1 if dp == 1 else -1).start()
-            if eager:
-                for step in (1, -1):
-                    send(colour, dp, 0, half, 1, step).start()
-
-
-def ring_second(send, arrived, i, eager=False):
+
+
+def ring_second(send, arrived, i):
     dp = gray(i)
     for ds, half in FIRST:
-        if (ds, half) == (2, 0) and not eager:
-            if i < 2:
-                ring_spread(send, gray(i + 2))
+        if (ds, half) == (2, 0) and i < 2:
+            ring_spread(send, gray(i + 2))
         for colour in (0, 1):
             arrived(colour, dp, ds, half)
             if (ds, half) in ((1, 0), (3, 1)):
                 send(colour, dp, ds, half, 1, 1 if ds == 1 else -1).start()
 
 
+def two_start(send):
+    for along in (0, 1):
+        for half in (0, 1):
+            for colour in (0, 1):
+                for step in (1, -1, 2):
+                    send(colour, 0, 0, half, along, step).start()
+
+
+def two_first(send, arrived):
+    for dp, half in FIRST:
+        for colour in (0, 1):
+            arrived(colour, dp, 0, half)
+            for step in (1, -1, 2):
+                send(colour, dp, 0, half, 1, step).start()
+
+
+def two_second(arrived):
+    for dp in (0, 1, 3, 2):
+        for ds, half in FIRST:
+            for colour in (0, 1):
+                arrived(colour, dp, ds, half)
+
+
 def gray(i):
     return i + (i // 2) * (1 - 2 * (i % 2))
 
@@ -221,8 +240,8 @@
 
 
 def front_kernel(
-    hid_ref, stat_ref, wt_ref, gain_ref, ub_ref, qkv_ref, units_ref,
-    xbuf, sbuf, stats, wbuf, nbuf, pbuf, rbuf, bbuf, qsend, qrecv,
+    hid_ref, wq_ref, wu_ref, gain0, gain1, gain2, gain3, ub_in, qkv_ref, units_ref,
+    wturn, wt_ref, stat_ref, bturn, ub_ref, xbuf, sbuf, stats, wbuf, nbuf, pbuf, rbuf, bbuf, qsend, qrecv,
     xsend_sem, xrecv_sem, own_sem, side_send, side_recv, stat_send, stat_recv,
     wsend_sem, wrecv_sem, wself_sem, bias_sem, pair_sem, qsend_sem, qrecv_sem,
 ):
@@ -275,6 +294,103 @@
 
     def other(i):
         return lax.rem(y + i // SIDE, SIDE) * SIDE + lax.rem(z + i % SIDE, SIDE)
+
+    def mate_w():
+        return pltpu.make_async_remote_copy(
+            src_ref=wt_ref.at[me], dst_ref=wbuf.at[:, core, :, kat],
+            send_sem=wself_sem, recv_sem=wrecv_sem,
+            device_id=(me, 2 * x + mate), device_id_type=MESH,
+        )
+
+    def weights_out(first, count):
+        @pl.loop(first, first + count)
+        def _(i):
+            pltpu.make_async_remote_copy(
+                src_ref=wt_ref.at[other(i)], dst_ref=wbuf.at[:, core, :, kat],
+                send_sem=wsend_sem, recv_sem=wrecv_sem,
+                device_id=(other(i), 2 * x + goal), device_id_type=MESH,
+            ).start()
+
+    def slots(kind, dp):
+        return pl.ds(dp * SIDE, 1) if kind == 0 else pl.ds(dp * SIDE + 1, 3)
+
+    def side_full(colour, kind, dp, step):
+        way = (1 - step) // 2
+        return pltpu.make_async_remote_copy(
+            src_ref=xbuf.at[colour, slots(kind, dp), :, pl.ds(DIRECT, 256)],
+            dst_ref=sbuf.at[colour, 2 * way, slots(kind, dp)],
+            send_sem=side_send.at[colour], recv_sem=side_recv.at[colour, kind, dp, way],
+            device_id=(me, 2 * lax.rem(x + step + SIDE, SIDE) + core), device_id_type=MESH,
+        )
+
+    def side_relay(colour, kind, dp, step):
+        way = (1 - step) // 2
+        rows = pl.ds(64 * way, 64)
+        return pltpu.make_async_remote_copy(
+            src_ref=sbuf.at[colour, 2 * way, slots(kind, dp), rows],
+            dst_ref=sbuf.at[colour, 1, slots(kind, dp), rows],
+            send_sem=side_send.at[colour], recv_sem=side_recv.at[colour, kind, dp, 2 + way],
+            device_id=(me, 2 * lax.rem(x + step + SIDE, SIDE) + core), device_id_type=MESH,
+        )
+
+    def side_wait(colour, kind, dp, n):
+        if n < 2:
+            ref = sbuf.at[colour, 2 * n, slots(kind, dp)]
+        else:
+            ref = sbuf.at[colour, 1, slots(kind, dp), pl.ds(64 * (n - 2), 64)]
+        pltpu.make_async_copy(ref, ref, side_recv.at[colour, kind, dp, n]).wait()
+
+    def side_out(kind, dp):
+        for colour in (0, 1):
+            for step in (1, -1):
+                side_full(colour, kind, dp, step).start()
+
+    def side_on(kind, dp):
+        for colour in (0, 1):
+            for way in (0, 1):
+                side_wait(colour, kind, dp, way)
+                side_relay(colour, kind, dp, 1 - 2 * way).start()
+
+    pbuf[...] = jnp.zeros_like(pbuf)
+    ring_first(send, arrived)
+    for dp in (1, 3, 2):
+        side_out(0, dp)
+
+    def lane_sum(tile):
+        total = jnp.zeros((NEW, NEW), jnp.float32)
+        for k in range(2 * HALF // 512):
+            value = tile(hid_ref[:, 512 * k:512 * (k + 1)].astype(jnp.float32))
+            for n in range(4):
+                total += value[:, NEW * n:NEW * (n + 1)]
+        return jnp.sum(total, axis=1, keepdims=True) * (1.0 / (2 * HALF))
+
+    mean = lane_sum(lambda value: value)
+    scatter = lax.rsqrt(lane_sum(lambda value: jnp.square(value - mean)) + 1e-05)
+    lane = lax.broadcasted_iota(jnp.int32, (NEW, NEW), 1)
+    stat_ref[...] = jnp.where(lane == 0, mean, jnp.where(lane == 1, scatter, 0.0)).T[0:8]
+    bturn[...] = jnp.broadcast_to(ub_in[...], (8, PART)).T
+    ub_ref[...] = jnp.broadcast_to(
+        bturn[pl.ds(pl.multiple_of(96 * me, 8), 96), 0:1], (96, NEW))
+
+    def turn(src, count):
+        @pl.loop(0, count)
+        def _(k):
+            at = pl.ds(pl.multiple_of(k * NEW, NEW), NEW)
+            wturn[at, :] = src[:, at].astype(jnp.float32).T
+
+    turn(wq_ref, 9)
+
+    @pl.loop(0, 16)
+    def _(r):
+        block = wturn[pl.ds(pl.multiple_of(72 * r, 8), 72), :]
+        wt_ref[r, 0] = jnp.concatenate(
+            [block, jnp.zeros((24, 384), jnp.float32)], axis=0).astype(jnp.bfloat16)
+
+    turn(wu_ref, 12)
+
+    @pl.loop(0, 16)
+    def _(r):
+        wt_ref[r, 1] = wturn[pl.ds(pl.multiple_of(96 * r, 8), 96), :].astype(jnp.bfloat16)
 
     @pl.loop(1, 16)
     def _(i):
@@ -291,13 +407,6 @@
     bias_own.start()
     bias_mate.start()
 
-    def mate_w():
-        return pltpu.make_async_remote_copy(
-            src_ref=wt_ref.at[me], dst_ref=wbuf.at[:, core, :, kat],
-            send_sem=wself_sem, recv_sem=wrecv_sem,
-            device_id=(me, 2 * x + mate), device_id_type=MESH,
-        )
-
     @pl.when(goal != core)
     def _():
         mate_w().start()
@@ -306,59 +415,6 @@
     def _():
         pltpu.make_async_copy(wt_ref.at[me], wbuf.at[:, core, :, kat], wrecv_sem).start()
 
-    def weights_out(first, count):
-        @pl.loop(first, first + count)
-        def _(i):
-            pltpu.make_async_remote_copy(
-                src_ref=wt_ref.at[other(i)], dst_ref=wbuf.at[:, core, :, kat],
-                send_sem=wsend_sem, recv_sem=wrecv_sem,
-                device_id=(other(i), 2 * x + goal), device_id_type=MESH,
-            ).start()
-
-    def slots(kind, dp):
-        return pl.ds(dp * SIDE, 1) if kind == 0 else pl.ds(dp * SIDE + 1, 3)
-
-    def side_full(colour, kind, dp, step):
-        way = (1 - step) // 2
-        return pltpu.make_async_remote_copy(
-            src_ref=xbuf.at[colour, slots(kind, dp), :, pl.ds(DIRECT, 256)],
-            dst_ref=sbuf.at[colour, 2 * way, slots(kind, dp)],
-            send_sem=side_send.at[colour], recv_sem=side_recv.at[colour, kind, dp, way],
-            device_id=(me, 2 * lax.rem(x + step + SIDE, SIDE) + core), device_id_type=MESH,
-        )
-
-    def side_relay(colour, kind, dp, step):
-        way = (1 - step) // 2
-        rows = pl.ds(64 * way, 64)
-        return pltpu.make_async_remote_copy(
-            src_ref=sbuf.at[colour, 2 * way, slots(kind, dp), rows],
-            dst_ref=sbuf.at[colour, 1, slots(kind, dp), rows],
-            send_sem=side_send.at[colour], recv_sem=side_recv.at[colour, kind, dp, 2 + way],
-            device_id=(me, 2 * lax.rem(x + step + SIDE, SIDE) + core), device_id_type=MESH,
-        )
-
-    def side_wait(colour, kind, dp, n):
-        if n < 2:
-            ref = sbuf.at[colour, 2 * n, slots(kind, dp)]
-        else:
-            ref = sbuf.at[colour, 1, slots(kind, dp), pl.ds(64 * (n - 2), 64)]
-        pltpu.make_async_copy(ref, ref, side_recv.at[colour, kind, dp, n]).wait()
-
-    def side_out(kind, dp):
-        for colour in (0, 1):
-            for step in (1, -1):
-                side_full(colour, kind, dp, step).start()
-
-    def side_on(kind, dp):
-        for colour in (0, 1):
-            for way in (0, 1):
-                side_wait(colour, kind, dp, way)
-                side_relay(colour, kind, dp, 1 - 2 * way).start()
-
-    pbuf[...] = jnp.zeros_like(pbuf)
-    ring_first(send, arrived)
-    for dp in (1, 3, 2):
-        side_out(0, dp)
 
     def origin(colour, dp, ds):
         dy = colour * dp + (1 - colour) * ds
@@ -377,10 +433,9 @@
                 value = (raw.astype(jnp.float32) - center) * spread
                 at = pl.ds(pl.multiple_of(base + lane, 256), width)
                 to = pl.ds(pl.multiple_of(lane, 256), width)
-                for kind in (0, 1):
+                for kind, (gain, shift) in enumerate(((gain0, gain1), (gain2, gain3))):
                     nbuf[colour, dp, kind, rows, to] = (
-                        value * gain_ref[2 * kind:2 * kind + 1, at]
-                        + gain_ref[2 * kind + 1:2 * kind + 2, at]
+                        value * gain[:, at] + shift[:, at]
                     ).astype(jnp.bfloat16)
 
     def side_lane(dx):
@@ -505,17 +560,6 @@
 
 
 def front(hidden, gains, qkv_weight, up_weight, up_bias):
-    req = lax.axis_index("req")
-    widened = hidden.astype(jnp.float32)
-    center = jnp.mean(widened, axis=-1)
-    spread = lax.rsqrt(jnp.mean(jnp.square(widened - center[:, None]), axis=-1) + 1e-05)
-    stat = jnp.pad(jnp.stack([center, spread]), ((0, 6), (0, 0)))
-    depth = qkv_weight.shape[0]
-    wq = jnp.pad(qkv_weight.T.reshape(16, 72, depth), ((0, 0), (0, 24), (0, 0)))
-    wt = jnp.stack([wq, up_weight.T.reshape(16, 96, depth)], axis=1)
-    gain = jnp.stack(gains)
-    bias = lax.dynamic_slice_in_dim(up_bias, req * 96, 96, 0)
-    bias = jnp.broadcast_to(bias[:, None], (96, 128))
     vmem = pl.BlockSpec(memory_space=pltpu.VMEM)
     hbm = pl.BlockSpec(memory_space=pl.ANY)
     dma = pltpu.SemaphoreType.DMA
@@ -525,9 +569,14 @@
             jax.ShapeDtypeStruct((1152, NEW), jnp.float32),
             jax.ShapeDtypeStruct((2, 96, 1024), jnp.bfloat16),
         ),
-        in_specs=[hbm, hbm, hbm, vmem, hbm],
+        in_specs=[vmem] * 8,
         out_specs=(vmem, vmem),
         scratch_shapes=[
+            pltpu.VMEM((PART, 384), jnp.float32),
+            pltpu.VMEM((16, 2, 96, 384), jnp.bfloat16),
+            pltpu.VMEM((8, NEW), jnp.float32),
+            pltpu.VMEM((PART, 8), jnp.float32),
+            pltpu.VMEM((96, NEW), jnp.float32),
             pltpu.VMEM((2, 16, NEW, DIRECT + 256), jnp.bfloat16),
             pltpu.VMEM((2, 3, 16, NEW, 256), jnp.bfloat16),
             pltpu.VMEM((16, 8, NEW), jnp.float32),
@@ -545,7 +594,7 @@
             collective_id=0, has_side_effects=True, vmem_limit_bytes=VMEM_LIMIT
         ),
         name="front",
-    )(hidden, stat, wt, gain, bias)
+    )(hidden, qkv_weight, up_weight, *(gain[None, :] for gain in gains), up_bias[None, :])
 
 
 def back_kernel(
@@ -637,11 +686,11 @@
 
     top = attention_scores(
         heads, len_ref[0], qkv_ref, qbias_ref, cos_ref, sin_ref, nk_ref, nv_ref, keep, key_block)
-    ring_first(send, arrived, True)
+    ring_first(send, arrived)
     attention_mix(heads, top, keep, att_ref, value_block)
     att_own = pltpu.make_async_copy(att_ref, aring.at[me], own_sem.at[1])
     att_own.start()
-    ring_start(asend)
+    two_start(asend)
     for copy in copies:
         copy.wait()
 
@@ -651,17 +700,12 @@
             h, at = n // 12, pl.ds(pl.multiple_of((n % 12) * 128, 128), 128)
             dturn[h, :, at] = dbuf[h, at, :].T
 
-    ring_second(send, arrived, 0, True)
+    ring_second(send, arrived, 0)
     turn(0, 12)
-    ring_second(send, arrived, 1, True)
+    two_first(asend, aarrived)
+    ring_second(send, arrived, 1)
     turn(12, 12)
-    ring_first(asend, aarrived, True)
-    ring_second(send, arrived, 2, True)
-    ring_second(asend, aarrived, 0, True)
-    ring_second(asend, aarrived, 1, True)
-    ring_second(send, arrived, 3, True)
-    ring_second(asend, aarrived, 2, True)
-    ring_second(asend, aarrived, 3, True)
+    two_second(aarrived)
     att_own.wait()
     pair = pltpu.make_async_remote_copy(
         src_ref=aring.at[pl.ds(8 * mate, 8)], dst_ref=amate,
@@ -669,6 +713,8 @@
         device_id=(me, 2 * x + mate), device_id_type=MESH,
     )
     pair.start()
+    ring_second(send, arrived, 2)
+    ring_second(send, arrived, 3)
     pair.wait_recv()
 
     def rcopy(q, step):

time: 232 us -> 213 us (0.918)
  Pallas kernels: 215 us -> 203 us
  other arithmetic: 6.92 us -> 1.54 us
    pallas_call x1, Pallas kernels: 107 us -> 93.6 us  [back(): pl.pallas_call(back_kernel, out_shape=(jax.ShapeDtypeStruct((NEW, 2 * HAL...]
    another operation x3 -> x0, other arithmetic: 3.02 us -> none  [the longest x1 1.68 us: front(): wt = jnp.stack([wq, up_weight.T.reshape(16, 96, depth)], axis=1)]
    reduce_sum x2 -> x0, other arithmetic: 2.36 us -> none  [the longest x1 1.79 us: front(): center = jnp.mean(widened, axis=-1)]
where the time goes in v7:
time: 213 us
  Pallas kernels  203 us (95%)
  local copies, waits for them, and re-layouts  7.2 us (3%)
    pallas_call x1, Pallas kernels, front(): pl.pallas_call(front_kernel, out_shape=(jax.ShapeDtypeStruct((1152, NEW),...  109 us
    pallas_call x1, Pallas kernels, back(): pl.pallas_call(back_kernel, out_shape=(jax.ShapeDtypeStruct((NEW, 2 * HAL...  93.6 us

profile of v7, /device:TPU:1, one launch (start us, length us, event | category | flops | bytes accessed | tf_op | source)
XLA Modules:
  0.0 212.6 jit_solution(7309734108305627502)
XLA Ops:
  1.3 0.8 dynamic-slice_add_fusion
  2.1 0.6 broadcast_in_dim.35.bias_ref
  2.7 1.3 broadcast_in_dim.34.qbias_ref
  4.0 1.3 broadcast_in_dim.33.ub_in
  5.3 0.1 fusion
  5.4 0.6 pad_maximum_fusion
  6.0 109.0 %front.1 = (f32[1152,128]{1,0:T(8,128)}, bf16[2,96,1024]{2,1,0:T(8,128)(2,1)}) custom-call(bf16[128,6144]{1,0:T(8,128)(2,1)} %rest_ref.1, bf16[384,1152]{1,0:T(8,128)(2,1)} %wq_ref.1, bf16[384,1536]{1,0:T(8,128)(2,1)} %wu_ref.1, f32[1,6144]{1,0:T(1,128)} %bitcast.13, f32[1,6144]{1,0:T(1,128)} %bitcast.14, f32[1,6144]{1,0:T(1,128)} %bitcast.15, ...), custom_call_target="tpu_custom_call" | custom-call | tf_op jit(solution)/shard_map/front/pallas_call | solution.py:566
  115.0 93.6 %back.1 = (bf16[128,6144]{1,0:T(8,128)(2,1)}, bf16[128,384]{1,0:T(8,128)(2,1)}, bf16[128,384]{1,0:T(8,128)(2,1)}) custom-call(s32[1]{0:T(128)S(6)} %copy.22.len_ref, bf16[2,96,1024]{2,1,0:T(8,128)(2,1)} %get-tuple-element.8.units_ref, f32[1152,128]{1,0:T(8,128)} %get-tuple-element.9.qkv_ref, f32[1,1152]{1,0:T(1,128)} %broadcast_in_dim.34.qbias_ref, ...), custom_call_target="tpu_custom_call" | custom-call | tf_op jit(solution)/shard_map/back/pallas_call | solution.py:867
  208.6 0.0 copy-start.1
  208.6 0.0 copy-start
  208.6 2.7 %copy.23 = bf16[128,6144]{1,0:T(8,128)(2,1)} copy(bf16[128,6144]{1,0:T(8,128)(2,1)} %get-tuple-element.21) | data formatting | bytes 3145728
  211.3 0.0 copy-done.1
  211.3 0.6 copy.24
  211.9 0.0 copy-done
  212.0 0.6 copy.25
  (2 shorter events, 0.0 us)
Async XLA Ops:
  208.6 2.8 %copy-start.1 = (bf16[128,384]{1,0:T(8,128)(2,1)S(1)}, bf16[128,384]{1,0:T(8,128)(2,1)}, u32[]{:S(2)}) copy-start(bf16[128,384]{1,0:T(8,128)(2,1)} %get-tuple-element.11) | copy-start | bytes 294916
  208.6 3.4 %copy-start = (bf16[128,384]{1,0:T(8,128)(2,1)S(1)}, bf16[128,384]{1,0:T(8,128)(2,1)}, u32[]{:S(2)}) copy-start(bf16[128,384]{1,0:T(8,128)(2,1)} %get-tuple-element.12) | copy-start | bytes 294916

commit v8 on v7

--- a/solution.py
+++ b/solution.py
@@ -42,7 +42,7 @@
         swapped = jnp.concatenate([low[ROT // 2:], low[: ROT // 2]], axis=0)
         return jnp.concatenate([low * cosine + swapped * sine, rows[ROT:]], axis=0)
 
-    bias = jnp.broadcast_to(bias_ref[...], (8, 3 * width)).T
+    bias = jnp.broadcast_to(bias_ref[...][None, :], (8, 3 * width)).T
 
     def block(j, part):
         first = (3 * j + part) * DH
@@ -243,7 +243,7 @@
     hid_ref, wq_ref, wu_ref, gain0, gain1, gain2, gain3, ub_in, qkv_ref, units_ref,
     wturn, wt_ref, stat_ref, bturn, ub_ref, xbuf, sbuf, stats, wbuf, nbuf, pbuf, rbuf, bbuf, qsend, qrecv,
     xsend_sem, xrecv_sem, own_sem, side_send, side_recv, stat_send, stat_recv,
-    wsend_sem, wrecv_sem, wself_sem, bias_sem, pair_sem, qsend_sem, qrecv_sem,
+    wsend_sem, wrecv_sem, wself_sem, bias_sem, pair_sem, qsend_sem, qrecv_sem, extra_send, extra_recv,
 ):
     y, z, x, core = place()
     me = y * SIDE + z
@@ -290,7 +290,29 @@
         return part(0, colour, half)
 
     send, arrived = ring_units(y, z, x, core, own, Relative(), part, xsend_sem, xrecv_sem)
+
+    def extra(colour, dp, half):
+        return sbuf.at[colour, :, dp * SIDE, pl.ds(64 * half, 64)]
+
+    def extra_out(colour, dp, half, step):
+        to = (dp + step) % SIDE
+        dev_y = y if colour == 0 else lax.rem(y + step + SIDE, SIDE)
+        dev_z = lax.rem(z + step + SIDE, SIDE) if colour == 0 else z
+        pltpu.make_async_remote_copy(
+            src_ref=extra(colour, dp, half), dst_ref=extra(colour, to, half),
+            send_sem=extra_send.at[colour], recv_sem=extra_recv.at[colour, half, to],
+            device_id=(dev_y * SIDE + dev_z, 2 * x + core), device_id_type=MESH,
+        ).start()
+
+    def extra_wait(colour, dp, half):
+        ref = extra(colour, dp, half)
+        pltpu.make_async_copy(ref, ref, extra_recv.at[colour, half, dp]).wait()
+
     ring_start(send)
+    for half in (0, 1):
+        for colour in (0, 1):
+            for step in (1, -1):
+                extra_out(colour, 0, half, step)
 
     def other(i):
         return lax.rem(y + i // SIDE, SIDE) * SIDE + lax.rem(z + i % SIDE, SIDE)
@@ -312,7 +334,7 @@
             ).start()
 
     def slots(kind, dp):
-        return pl.ds(dp * SIDE, 1) if kind == 0 else pl.ds(dp * SIDE + 1, 3)
+        return pl.ds(dp * SIDE + 1, 3)
 
     def side_full(colour, kind, dp, step):
         way = (1 - step) // 2
@@ -353,8 +375,10 @@
 
     pbuf[...] = jnp.zeros_like(pbuf)
     ring_first(send, arrived)
-    for dp in (1, 3, 2):
-        side_out(0, dp)
+    for dp, half in ((1, 0), (3, 1)):
+        for colour in (0, 1):
+            extra_wait(colour, dp, half)
+            extra_out(colour, dp, half, 1 if dp == 1 else -1)
 
     def lane_sum(tile):
         total = jnp.zeros((NEW, NEW), jnp.float32)
@@ -368,7 +392,7 @@
     scatter = lax.rsqrt(lane_sum(lambda value: jnp.square(value - mean)) + 1e-05)
     lane = lax.broadcasted_iota(jnp.int32, (NEW, NEW), 1)
     stat_ref[...] = jnp.where(lane == 0, mean, jnp.where(lane == 1, scatter, 0.0)).T[0:8]
-    bturn[...] = jnp.broadcast_to(ub_in[...], (8, PART)).T
+    bturn[...] = jnp.broadcast_to(ub_in[...][None, :], (8, PART)).T
     ub_ref[...] = jnp.broadcast_to(
         bturn[pl.ds(pl.multiple_of(96 * me, 8), 96), 0:1], (96, NEW))
 
@@ -468,8 +492,9 @@
 
     weights_out(1, 15)
     pltpu.make_async_copy(stats, stats, stat_recv).wait()
-    for dp in (1, 3, 2):
-        side_on(0, dp)
+    for dp, half in FIRST[2:]:
+        for colour in (0, 1):
+            extra_wait(colour, dp, half)
 
     @pl.loop(0, SIDE)
     def _(i):
@@ -480,6 +505,22 @@
             norm(colour, gray(i), early)
 
     pltpu.make_async_copy(wbuf, wbuf, wrecv_sem).wait()
+
+    def pair_out(last):
+        @pl.loop(0, 16)
+        def _(j):
+            dy, dz = j // SIDE, j % SIDE
+            row = origin(0, dz, dy)
+            final = jnp.logical_or(dy == 2, dz == 2)
+
+            @pl.when(jnp.logical_and(row // 8 != core, final == last))
+            def _():
+                pltpu.make_async_remote_copy(
+                    src_ref=pbuf.at[row], dst_ref=rbuf.at[lax.rem(row, 8)],
+                    send_sem=pair_sem.at[0], recv_sem=pair_sem.at[1],
+                    device_id=(me, 2 * x + mate), device_id_type=MESH,
+                ).start()
+
 
     @pl.loop(0, SIDE)
     def _(i):
@@ -488,24 +529,17 @@
             for n in (2, 3):
                 side_wait(colour, 1, dp, n)
 
-            @pl.when(i > 0)
-            def _():
-                for n in (2, 3):
-                    side_wait(colour, 0, dp, n)
-
         @pl.loop(0, 2)
         def _(colour):
             compute(colour, dp)
 
-    pair = pltpu.make_async_remote_copy(
-        src_ref=pbuf.at[pl.ds(8 * mate, 8)], dst_ref=rbuf,
-        send_sem=pair_sem.at[0], recv_sem=pair_sem.at[1],
-        device_id=(me, 2 * x + mate), device_id_type=MESH,
-    )
-    pair.start()
+        @pl.when(i >= 2)
+        def _():
+            pair_out(i == 3)
+
     bias_own.wait()
     bias_mate.wait()
-    pair.wait_recv()
+    pltpu.make_async_copy(rbuf, rbuf, pair_sem.at[1]).wait()
     mine = pl.ds(pl.multiple_of(me * 72, 8), 72)
 
     @pl.loop(0, 8)
@@ -536,7 +570,8 @@
 
     pltpu.make_async_copy(qrecv, qrecv, qrecv_sem).wait()
     qkv_ref[...] = qrecv[...]
-    pair.wait_send()
+    some = pbuf.at[pl.ds(0, 8)]
+    pltpu.make_async_copy(some, some, pair_sem.at[0]).wait()
 
     @pl.when(goal == core)
     def _():
@@ -553,8 +588,10 @@
     for colour in (0, 1):
         some = xbuf.at[colour, pl.ds(1, 15)]
         pltpu.make_async_copy(some, some, xsend_sem.at[colour]).wait()
-        some = sbuf.at[colour, :, pl.ds(1, 15)]
+        some = sbuf.at[colour, :, pl.ds(4, 12)]
         pltpu.make_async_copy(some, some, side_send.at[colour]).wait()
+        some = sbuf.at[colour, :, pl.ds(1, 3)]
+        pltpu.make_async_copy(some, some, extra_send.at[colour]).wait()
     some = stats.at[pl.ds(0, 15)]
     pltpu.make_async_copy(some, some, stat_send).wait()
 
@@ -588,13 +625,13 @@
             pltpu.VMEM((16, 72, NEW), jnp.float32),
             pltpu.VMEM((1152, NEW), jnp.float32),
             dma((2,)), dma((2, 2, 16)), dma((2, 5)), dma((2,)), dma((2, 2, 4, 4)), dma, dma,
-            dma, dma, dma, dma((3,)), dma((2,)), dma, dma,
+            dma, dma, dma, dma((3,)), dma((2,)), dma, dma, dma((2,)), dma((2, 2, 4)),
         ],
         compiler_params=pltpu.CompilerParams(
             collective_id=0, has_side_effects=True, vmem_limit_bytes=VMEM_LIMIT
         ),
         name="front",
-    )(hidden, qkv_weight, up_weight, *(gain[None, :] for gain in gains), up_bias[None, :])
+    )(hidden, qkv_weight, up_weight, *(gain[None, :] for gain in gains), up_bias)
 
 
 def back_kernel(
@@ -603,7 +640,7 @@
     ubuf, aring, amate, dbuf, obuf, dturn, total, tsend, rsum, share, rest, fout,
     kbuf, vbuf, sbuf, qexp, vkeep, att_ref, ksem, vsem,
     usend_sem, urecv_sem, own_sem, asend_sem, arecv_sem, amate_sem, w_sem,
-    hsend_sem, hrecv_sem, rsend_sem, rrecv_sem, fsend_sem, frecv_sem, gsend_sem, grecv_sem,
+    hsend_sem, hrecv_sem, rsend_sem, rrecv_sem, fsend_sem, frecv_sem, gsend_sem, grecv_sem, out_sem,
 ):
     for hbm, buf, sem in ((k_hbm, kbuf, ksem), (v_hbm, vbuf, vsem)):
         for n in range(CACHE // KB):
@@ -814,20 +851,42 @@
     def owner_at(step):
         return lax.rem(x - step + SIDE, SIDE)
 
+    store = []
+
+    def out_copy(c, step):
+        owner = owner_at(step)
+        whose = core if c == 0 else mate
+        dst = out_ref.at[
+            pl.ds(pl.multiple_of(32 * owner, 32), 32),
+            pl.ds(pl.multiple_of(whose * HALF, HALF), HALF),
+        ]
+        return pltpu.make_async_copy(piece(owner, whose), dst, out_sem.at[c, step])
+
+    def put(c, step):
+        out_copy(c, step).start()
+        store.append((c, step))
+
     pltpu.make_async_copy(piece(x, core), piece(x, core), frecv_sem).wait()
     for step in (1, -1):
         gcopy(step).start()
     pass_on(0).start()
+    put(0, 0)
     for step in (1, -1):
         landed(0, (1 - step) // 2, piece(owner_at(step), core))
         grelay(step).start()
         pass_on(step % SIDE).start()
+        put(0, step % SIDE)
+    landed(1, 0, piece(owner_at(0), mate))
+    put(1, 0)
     for way in (0, 1):
         landed(0, 2 + way, strip(owner_at(2), way))
     pass_on(2).start()
-    for step in (0, 1, 3, 2):
+    put(0, 2)
+    for step in (1, 3, 2):
         landed(1, step, piece(owner_at(step), mate))
-    out_ref[...] = fout[...]
+        put(1, step)
+    for c, step in store:
+        out_copy(c, step).wait()
 
     for step in (1, -1):
         gcopy(step).wait_send()
@@ -875,7 +934,7 @@
             pl.BlockSpec(memory_space=pltpu.SMEM), hbm, vmem, vmem, vmem, vmem, hbm, hbm,
             hbm, hbm, hbm, vmem,
         ],
-        out_specs=(vmem, vmem, vmem),
+        out_specs=(hbm, vmem, vmem),
         scratch_shapes=[
             pltpu.VMEM((2, 16, 96, 1024), jnp.bfloat16),
             pltpu.VMEM((16, NEW, 384), jnp.bfloat16),
@@ -897,13 +956,13 @@
             pltpu.VMEM((NEW, 384), jnp.bfloat16),
             dma((CACHE // KB,)), dma((CACHE // KB,)),
             dma((2,)), dma((2, 2, 16)), dma((2,)), dma((2,)), dma((2, 2, 16)), dma((2,)), dma((6,)),
-            dma, dma, dma((3,)), dma((3,)), dma, dma, dma((2, 4)), dma((2, 4)),
+            dma, dma, dma((3,)), dma((3,)), dma, dma, dma((2, 4)), dma((2, 4)), dma((2, 4)),
         ],
         compiler_params=pltpu.CompilerParams(
             collective_id=1, has_side_effects=True, vmem_limit_bytes=VMEM_LIMIT
         ),
         name="back",
-    )(length, units, qkv, qkv_bias[None, :], cosine, sine, keys_old, values_old,
+    )(length, units, qkv, qkv_bias, cosine, sine, keys_old, values_old,
       down_weight, out_weight, hidden, bias)
 
 

time: 213 us -> 217 us (1.019)
  Pallas kernels: 203 us -> 209 us
  local copies, waits for them, and re-layouts: 7.2 us -> 4.59 us
    pallas_call x1, Pallas kernels: 109 us -> 115 us  [front(): pl.pallas_call(front_kernel, out_shape=(jax.ShapeDtypeStruct((1152, NEW),...]
    broadcast_in_dim x2 -> x0, local copies, waits for them, and re-layouts: 2.58 us -> none  [the longest x1 1.29 us: front(): up_bias[None, :]]
where the time goes in v8:
time: 217 us
  Pallas kernels  209 us (96%)
  local copies, waits for them, and re-layouts  4.59 us (2%)
    pallas_call x1, Pallas kernels, front(): pl.pallas_call(front_kernel, out_shape=(jax.ShapeDtypeStruct((1152, NEW),...  115 us
    pallas_call x1, Pallas kernels, back(): pl.pallas_call(back_kernel, out_shape=(jax.ShapeDtypeStruct((NEW, 2 * HAL...  94.6 us

profile of v8, /device:TPU:1, one launch (start us, length us, event | category | flops | bytes accessed | tf_op | source)
XLA Modules:
  0.0 216.8 jit_solution(14304607246656165207)
XLA Ops:
  1.3 0.8 dynamic-slice_add_fusion
  2.1 0.6 broadcast_in_dim.27.bias_ref
  2.7 0.1 fusion
  2.8 0.6 pad_maximum_fusion
  3.4 114.8 %front.1 = (f32[1152,128]{1,0:T(8,128)}, bf16[2,96,1024]{2,1,0:T(8,128)(2,1)}) custom-call(bf16[128,6144]{1,0:T(8,128)(2,1)} %rest_ref.1, bf16[384,1152]{1,0:T(8,128)(2,1)} %wq_ref.1, bf16[384,1536]{1,0:T(8,128)(2,1)} %wu_ref.1, f32[1,6144]{1,0:T(1,128)} %bitcast.13, f32[1,6144]{1,0:T(1,128)} %bitcast.14, f32[1,6144]{1,0:T(1,128)} %bitcast.15, ...), custom_call_target="tpu_custom_call" | custom-call | tf_op jit(solution)/shard_map/front/pallas_call | solution.py:603
  118.2 94.6 %back.1 = (bf16[128,6144]{1,0:T(8,128)(2,1)}, bf16[128,384]{1,0:T(8,128)(2,1)}, bf16[128,384]{1,0:T(8,128)(2,1)}) custom-call(s32[1]{0:T(128)S(6)} %copy.22.len_ref, bf16[2,96,1024]{2,1,0:T(8,128)(2,1)} %get-tuple-element.8.units_ref, f32[1152,128]{1,0:T(8,128)} %get-tuple-element.9.qkv_ref, f32[1152]{0:T(1024)} %qbias_ref.1, ...), custom_call_target="tpu_custom_call" | custom-call | tf_op jit(solution)/shard_map/back/pallas_call | solution.py:926
  212.8 0.0 copy-start.1
  212.8 0.0 copy-start
  212.8 2.7 %copy.23 = bf16[128,6144]{1,0:T(8,128)(2,1)} copy(bf16[128,6144]{1,0:T(8,128)(2,1)} %get-tuple-element.21) | data formatting | bytes 3145728
  215.5 0.0 copy-done.1
  215.5 0.6 copy.24
  216.2 0.0 copy-done
  216.2 0.6 copy.25
  (2 shorter events, 0.0 us)
Async XLA Ops:
  212.8 2.8 %copy-start.1 = (bf16[128,384]{1,0:T(8,128)(2,1)S(1)}, bf16[128,384]{1,0:T(8,128)(2,1)}, u32[]{:S(2)}) copy-start(bf16[128,384]{1,0:T(8,128)(2,1)} %get-tuple-element.11) | copy-start | bytes 294916
  212.8 3.4 %copy-start = (bf16[128,384]{1,0:T(8,128)(2,1)S(1)}, bf16[128,384]{1,0:T(8,128)(2,1)}, u32[]{:S(2)}) copy-start(bf16[128,384]{1,0:T(8,128)(2,1)} %get-tuple-element.12) | copy-start | bytes 294916

commit v9 on v7

--- a/solution.py
+++ b/solution.py
@@ -42,7 +42,7 @@
         swapped = jnp.concatenate([low[ROT // 2:], low[: ROT // 2]], axis=0)
         return jnp.concatenate([low * cosine + swapped * sine, rows[ROT:]], axis=0)
 
-    bias = jnp.broadcast_to(bias_ref[...], (8, 3 * width)).T
+    bias = jnp.broadcast_to(bias_ref[...][None, :], (8, 3 * width)).T
 
     def block(j, part):
         first = (3 * j + part) * DH
@@ -368,7 +368,7 @@
     scatter = lax.rsqrt(lane_sum(lambda value: jnp.square(value - mean)) + 1e-05)
     lane = lax.broadcasted_iota(jnp.int32, (NEW, NEW), 1)
     stat_ref[...] = jnp.where(lane == 0, mean, jnp.where(lane == 1, scatter, 0.0)).T[0:8]
-    bturn[...] = jnp.broadcast_to(ub_in[...], (8, PART)).T
+    bturn[...] = jnp.broadcast_to(ub_in[...][None, :], (8, PART)).T
     ub_ref[...] = jnp.broadcast_to(
         bturn[pl.ds(pl.multiple_of(96 * me, 8), 96), 0:1], (96, NEW))
 
@@ -481,6 +481,22 @@
 
     pltpu.make_async_copy(wbuf, wbuf, wrecv_sem).wait()
 
+    def pair_out(last):
+        @pl.loop(0, 16)
+        def _(j):
+            dy, dz = j // SIDE, j % SIDE
+            row = origin(0, dz, dy)
+            final = jnp.logical_or(dy == 2, dz == 2)
+
+            @pl.when(jnp.logical_and(row // 8 != core, final == last))
+            def _():
+                pltpu.make_async_remote_copy(
+                    src_ref=pbuf.at[row], dst_ref=rbuf.at[lax.rem(row, 8)],
+                    send_sem=pair_sem.at[0], recv_sem=pair_sem.at[1],
+                    device_id=(me, 2 * x + mate), device_id_type=MESH,
+                ).start()
+
+
     @pl.loop(0, SIDE)
     def _(i):
         dp = gray(i)
@@ -497,15 +513,13 @@
         def _(colour):
             compute(colour, dp)
 
-    pair = pltpu.make_async_remote_copy(
-        src_ref=pbuf.at[pl.ds(8 * mate, 8)], dst_ref=rbuf,
-        send_sem=pair_sem.at[0], recv_sem=pair_sem.at[1],
-        device_id=(me, 2 * x + mate), device_id_type=MESH,
-    )
-    pair.start()
+        @pl.when(i >= 2)
+        def _():
+            pair_out(i == 3)
+
     bias_own.wait()
     bias_mate.wait()
-    pair.wait_recv()
+    pltpu.make_async_copy(rbuf, rbuf, pair_sem.at[1]).wait()
     mine = pl.ds(pl.multiple_of(me * 72, 8), 72)
 
     @pl.loop(0, 8)
@@ -536,7 +550,8 @@
 
     pltpu.make_async_copy(qrecv, qrecv, qrecv_sem).wait()
     qkv_ref[...] = qrecv[...]
-    pair.wait_send()
+    some = pbuf.at[pl.ds(0, 8)]
+    pltpu.make_async_copy(some, some, pair_sem.at[0]).wait()
 
     @pl.when(goal == core)
     def _():
@@ -594,7 +609,7 @@
             collective_id=0, has_side_effects=True, vmem_limit_bytes=VMEM_LIMIT
         ),
         name="front",
-    )(hidden, qkv_weight, up_weight, *(gain[None, :] for gain in gains), up_bias[None, :])
+    )(hidden, qkv_weight, up_weight, *(gain[None, :] for gain in gains), up_bias)
 
 
 def back_kernel(
@@ -903,7 +918,7 @@
             collective_id=1, has_side_effects=True, vmem_limit_bytes=VMEM_LIMIT
         ),
         name="back",
-    )(length, units, qkv, qkv_bias[None, :], cosine, sine, keys_old, values_old,
+    )(length, units, qkv, qkv_bias, cosine, sine, keys_old, values_old,
       down_weight, out_weight, hidden, bias)
 
 

time: 213 us -> 211 us (level)
  local copies, waits for them, and re-layouts: 7.2 us -> 4.59 us
    broadcast_in_dim x2 -> x0, local copies, waits for them, and re-layouts: 2.58 us -> none  [the longest x1 1.29 us: front(): up_bias[None, :]]
where the time goes in v9:
time: 211 us; the launch traced here: 210 us
  Pallas kernels  203 us (96%)
  local copies, waits for them, and re-layouts  4.59 us (2%)
    pallas_call x1, Pallas kernels, front(): pl.pallas_call(front_kernel, out_shape=(jax.ShapeDtypeStruct((1152, NEW),...  109 us
    pallas_call x1, Pallas kernels, back(): pl.pallas_call(back_kernel, out_shape=(jax.ShapeDtypeStruct((NEW, 2 * HAL...  94 us

profile of v9, /device:TPU:1, one launch (start us, length us, event | category | flops | bytes accessed | tf_op | source)
XLA Modules:
  0.0 210.3 jit_solution(18180550585885846350)
XLA Ops:
  1.3 0.8 dynamic-slice_add_fusion
  2.1 0.6 broadcast_in_dim.27.bias_ref
  2.7 0.1 fusion
  2.8 0.6 pad_maximum_fusion
  3.4 108.8 %front.1 = (f32[1152,128]{1,0:T(8,128)}, bf16[2,96,1024]{2,1,0:T(8,128)(2,1)}) custom-call(bf16[128,6144]{1,0:T(8,128)(2,1)} %rest_ref.1, bf16[384,1152]{1,0:T(8,128)(2,1)} %wq_ref.1, bf16[384,1536]{1,0:T(8,128)(2,1)} %wu_ref.1, f32[1,6144]{1,0:T(1,128)} %bitcast.13, f32[1,6144]{1,0:T(1,128)} %bitcast.14, f32[1,6144]{1,0:T(1,128)} %bitcast.15, ...), custom_call_target="tpu_custom_call" | custom-call | tf_op jit(solution)/shard_map/front/pallas_call | solution.py:581
  112.2 94.0 %back.1 = (bf16[128,6144]{1,0:T(8,128)(2,1)}, bf16[128,384]{1,0:T(8,128)(2,1)}, bf16[128,384]{1,0:T(8,128)(2,1)}) custom-call(s32[1]{0:T(128)S(6)} %copy.22.len_ref, bf16[2,96,1024]{2,1,0:T(8,128)(2,1)} %get-tuple-element.8.units_ref, f32[1152,128]{1,0:T(8,128)} %get-tuple-element.9.qkv_ref, f32[1152]{0:T(1024)} %qbias_ref.1, ...), custom_call_target="tpu_custom_call" | custom-call | tf_op jit(solution)/shard_map/back/pallas_call | solution.py:882
  206.3 0.0 copy-start.1
  206.3 0.0 copy-start
  206.3 2.7 %copy.23 = bf16[128,6144]{1,0:T(8,128)(2,1)} copy(bf16[128,6144]{1,0:T(8,128)(2,1)} %get-tuple-element.21) | data formatting | bytes 3145728
  209.0 0.0 copy-done.1
  209.0 0.6 copy.24
  209.7 0.0 copy-done
  209.7 0.6 copy.25
  (2 shorter events, 0.0 us)
Async XLA Ops:
  206.3 2.8 %copy-start.1 = (bf16[128,384]{1,0:T(8,128)(2,1)S(1)}, bf16[128,384]{1,0:T(8,128)(2,1)}, u32[]{:S(2)}) copy-start(bf16[128,384]{1,0:T(8,128)(2,1)} %get-tuple-element.11) | copy-start | bytes 294916
  206.3 3.4 %copy-start = (bf16[128,384]{1,0:T(8,128)(2,1)S(1)}, bf16[128,384]{1,0:T(8,128)(2,1)}, u32[]{:S(2)}) copy-start(bf16[128,384]{1,0:T(8,128)(2,1)} %get-tuple-element.12) | copy-start | bytes 294916

commit v10 on v9

--- a/solution.py
+++ b/solution.py
@@ -614,7 +614,7 @@
 
 def back_kernel(
     len_ref, units_ref, qkv_ref, qbias_ref, cos_ref, sin_ref, k_hbm, v_hbm,
-    wd_ref, wo_ref, rest_ref, bias_ref, out_ref, nk_ref, nv_ref,
+    wd_ref, wo_ref, rest_ref, bias_a, bias_b, out_ref, nk_ref, nv_ref,
     ubuf, aring, amate, dbuf, obuf, dturn, total, tsend, rsum, share, rest, fout,
     kbuf, vbuf, sbuf, qexp, vkeep, att_ref, ksem, vsem,
     usend_sem, urecv_sem, own_sem, asend_sem, arecv_sem, amate_sem, w_sem,
@@ -768,12 +768,13 @@
         pltpu.make_async_copy(some, some, rrecv_sem.at[step - 1]).wait()
     rows = pl.ds(pl.multiple_of(32 * x, 32), 32)
     mine = pl.ds(pl.multiple_of(384 * me, 384), 384)
+    bias_here = bias_a[:, mine] + bias_b[:, mine]
 
     @pl.loop(0, 8)
     def _(q):
         value = total[q, rows, :] + rsum[0, q].astype(jnp.float32)
         value += rsum[1, q].astype(jnp.float32) + rsum[2, q].astype(jnp.float32)
-        share[q] = (rest[q].astype(jnp.float32) + (value + bias_ref[...])).astype(jnp.bfloat16)
+        share[q] = (rest[q].astype(jnp.float32) + (value + bias_here)).astype(jnp.bfloat16)
         row = 8 * core + q
 
         @pl.when(row != me)
@@ -872,10 +873,8 @@
         pltpu.make_async_copy(some, some, asend_sem.at[colour]).wait()
 
 
-def back(units, qkv, qkv_bias, length, keys_old, values_old, hidden, out_weight, down_weight, bias_total):
+def back(units, qkv, qkv_bias, length, keys_old, values_old, hidden, out_weight, down_weight, biases):
     cosine, sine = rotation_tables(length[0])
-    req = lax.axis_index("req")
-    bias = lax.dynamic_slice_in_dim(bias_total, req * 384, 384, 0)[None, :]
     vmem = pl.BlockSpec(memory_space=pltpu.VMEM)
     hbm = pl.BlockSpec(memory_space=pl.ANY)
     dma = pltpu.SemaphoreType.DMA
@@ -888,7 +887,7 @@
         ),
         in_specs=[
             pl.BlockSpec(memory_space=pltpu.SMEM), hbm, vmem, vmem, vmem, vmem, hbm, hbm,
-            hbm, hbm, hbm, vmem,
+            hbm, hbm, hbm, vmem, vmem,
         ],
         out_specs=(vmem, vmem, vmem),
         scratch_shapes=[
@@ -919,7 +918,7 @@
         ),
         name="back",
     )(length, units, qkv, qkv_bias, cosine, sine, keys_old, values_old,
-      down_weight, out_weight, hidden, bias)
+      down_weight, out_weight, hidden, biases[0][None, :], biases[1][None, :])
 
 
 def body(
@@ -944,7 +943,7 @@
     qkv, units = front(hidden, gains, qkv_weight, up_weight, up_bias)
     result, key_rows, value_rows = back(
         units, qkv, qkv_bias, cached_len, cache_keys[0], cache_values[0],
-        hidden, out_weight, down_weight, out_bias + down_bias,
+        hidden, out_weight, down_weight, (out_bias, down_bias),
     )
     return (result, key_rows[None], value_rows[None])
 

time: 211 us -> 209 us (level)
  no operation moved by 1% of the time
where the time goes in v10:
time: 209 us
  Pallas kernels  203 us (97%)
  local copies, waits for them, and re-layouts  4.02 us (2%)
    pallas_call x1, Pallas kernels, front(): pl.pallas_call(front_kernel, out_shape=(jax.ShapeDtypeStruct((1152, NEW),...  109 us
    pallas_call x1, Pallas kernels, back(): pl.pallas_call(back_kernel, out_shape=(jax.ShapeDtypeStruct((NEW, 2 * HAL...  94.1 us

profile of v10, /device:TPU:1, one launch (start us, length us, event | category | flops | bytes accessed | tf_op | source)
XLA Modules:
  0.0 209.0 jit_solution(7625812221177077748)
XLA Ops:
  1.3 0.1 fusion
  1.4 0.6 pad_maximum_fusion
  2.0 108.8 %front.1 = (f32[1152,128]{1,0:T(8,128)}, bf16[2,96,1024]{2,1,0:T(8,128)(2,1)}) custom-call(bf16[128,6144]{1,0:T(8,128)(2,1)} %rest_ref.1, bf16[384,1152]{1,0:T(8,128)(2,1)} %wq_ref.1, bf16[384,1536]{1,0:T(8,128)(2,1)} %wu_ref.1, f32[1,6144]{1,0:T(1,128)} %bitcast.15, f32[1,6144]{1,0:T(1,128)} %bitcast.16, f32[1,6144]{1,0:T(1,128)} %bitcast.17, ...), custom_call_target="tpu_custom_call" | custom-call | tf_op jit(solution)/shard_map/front/pallas_call | solution.py:581
  110.8 94.1 %back.1 = (bf16[128,6144]{1,0:T(8,128)(2,1)}, bf16[128,384]{1,0:T(8,128)(2,1)}, bf16[128,384]{1,0:T(8,128)(2,1)}) custom-call(s32[1]{0:T(128)S(6)} %copy.22.len_ref, bf16[2,96,1024]{2,1,0:T(8,128)(2,1)} %get-tuple-element.8.units_ref, f32[1152,128]{1,0:T(8,128)} %get-tuple-element.9.qkv_ref, f32[1152]{0:T(1024)} %qbias_ref.1, ...), custom_call_target="tpu_custom_call" | custom-call | tf_op jit(solution)/shard_map/back/pallas_call | solution.py:881
  204.9 0.0 copy-start.1
  204.9 0.0 copy-start
  205.0 2.7 %copy.23 = bf16[128,6144]{1,0:T(8,128)(2,1)} copy(bf16[128,6144]{1,0:T(8,128)(2,1)} %get-tuple-element.21) | data formatting | bytes 3145728
  207.7 0.0 copy-done.1
  207.7 0.6 copy.24
  208.3 0.0 copy-done
  208.3 0.6 copy.25
  (2 shorter events, 0.0 us)
Async XLA Ops:
  204.9 2.8 %copy-start.1 = (bf16[128,384]{1,0:T(8,128)(2,1)S(1)}, bf16[128,384]{1,0:T(8,128)(2,1)}, u32[]{:S(2)}) copy-start(bf16[128,384]{1,0:T(8,128)(2,1)} %get-tuple-element.11) | copy-start | bytes 294916
  204.9 3.4 %copy-start = (bf16[128,384]{1,0:T(8,128)(2,1)S(1)}, bf16[128,384]{1,0:T(8,128)(2,1)}, u32[]{:S(2)}) copy-start(bf16[128,384]{1,0:T(8,128)(2,1)} %get-tuple-element.12) | copy-start | bytes 294916
